TPU v7x, 512 devices: a whole 4x8x8 slice. The times are simulated.
512 devices in a mesh: dom: 64 (over z_lo, y, core), col: 8 (over x, z_hi).
Axes of the slice: x: 4, y: 8, z: 8 (z_hi: 2, z_lo: 4; z = z_hi * 4 + z_lo), core: 2. Of those that a mesh axis runs over, the one named last changes fastest.
Arguments:
- features: bfloat16 [128, 16384], P('col', 'dom'), may hold values from -6 to 6
- cached_embed: bfloat16 [128, 16384], P('col'), may hold values from -6 to 6
- staleness: int32 [64], replicated, may hold values from 0 to 15, as said below
- node_counts: int32 [64], replicated, may hold values from 64 to 256, as said below
- neighbours: int32 [16, 16384], P(None, 'dom'), may hold values from 0 to 16383, as said below
- degrees: int32 [16384], P('dom'), may hold values from 1 to 16
- w_self: bfloat16 [128, 256], P('col'), may hold values from -0.5 to 0.5
- w_nbr: bfloat16 [128, 256], P('col'), may hold values from -0.5 to 0.5
- sage_bias: float32 [256], P('col'), may hold values from -3 to 3
- cotangent: bfloat16 [256, 16384], P('col', 'dom'), may hold values from -6 to 6
Outputs:
- activation: bfloat16 [256, 16384], P('col', 'dom')
- grad_feat: bfloat16 [128, 16384], P('col', 'dom')
- grad_self: float32 [128, 256], P('col')
- grad_nbr: float32 [128, 256], P('col')
- grad_bias: float32 [256], P('col')
Inputs may be any that keep to these rules, and one draw needn't show every extreme that they name: Exactly 16 partitions have staleness of 8 or more. `node_counts`: some partition has all 256 node slots live. `neighbours`: every neighbour slot names a live node slot; about half lie in the node's own partition.
All inputs are finite; a program needn't handle non-finite values.
Results may differ from a plain program's by a relative error of at most 0.015.
Values may be sent and summed in bfloat16 or wider, within the bound.
A program may use at most 64 MiB of HBM per device.

v0:
```python
import jax
import jax.numpy as jnp
from jax import lax
from jax.sharding import PartitionSpec as P

LIMIT = 8


def left_product(weight, data):
    return lax.dot_general(
        weight, data, (((0,), (0,)), ((), ())), preferred_element_type=jnp.float32
    )


def right_product(data, grads):
    return lax.dot_general(
        data, grads, (((1,), (1,)), ((), ())), preferred_element_type=jnp.float32
    )


def per_device(
    features,
    cached_embed,
    staleness,
    node_counts,
    neighbours,
    degrees,
    w_self,
    w_nbr,
    sage_bias,
    cotangent,
):
    col_width = features.shape[0]
    part_rows = features.shape[1]
    slot_count = neighbours.shape[0]
    my_index = lax.axis_index("dom")
    fresh_flag = (staleness >= LIMIT).astype(jnp.int32)
    my_fresh = fresh_flag[my_index]
    own_cache = lax.dynamic_slice_in_dim(cached_embed, my_index * part_rows, part_rows, 1)
    own_source = jnp.where(my_fresh == 1, features, own_cache)
    sources = lax.all_gather(own_source, "dom", axis=1, tiled=True)
    local_slot = jnp.arange(part_rows, dtype=jnp.int32)
    live_rows = (local_slot < node_counts[my_index]).astype(jnp.float32)
    slot_index = jnp.arange(slot_count, dtype=jnp.int32)
    used = (slot_index[:, None] < degrees[None, :]).astype(jnp.float32)
    weights = used * (live_rows / degrees.astype(jnp.float32))[None, :]
    gathered = sources[:, neighbours].astype(jnp.float32)
    aggregated = jnp.sum(weights[None, :, :] * gathered, axis=1).astype(jnp.bfloat16)
    partial_pre = left_product(w_self, features) + left_product(w_nbr, aggregated)
    pre_act = (
        lax.psum_scatter(
            partial_pre.astype(jnp.bfloat16), "col", scatter_dimension=0, tiled=True
        ).astype(jnp.float32)
        + sage_bias[:, None]
    )
    sigmoid = 1.0 / (1.0 + jnp.exp(-pre_act))
    activation = (live_rows[None, :] * pre_act * sigmoid).astype(jnp.bfloat16)
    grad_pre = (
        live_rows[None, :]
        * cotangent.astype(jnp.float32)
        * sigmoid
        * (1.0 + pre_act * (1.0 - sigmoid))
    ).astype(jnp.bfloat16)
    grad_full = lax.all_gather(grad_pre, "col", axis=0, tiled=True)
    self_part = right_product(features, grad_full)
    nbr_part = right_product(aggregated, grad_full)
    bias_part = jnp.sum(grad_pre.astype(jnp.float32), axis=1)
    grad_self, grad_nbr, grad_bias = lax.psum((self_part, nbr_part, bias_part), "dom")
    grad_agg = jnp.dot(w_nbr, grad_full, preferred_element_type=jnp.float32).astype(jnp.bfloat16)
    own_term = jnp.dot(w_self, grad_full, preferred_element_type=jnp.float32)
    spread = weights[None, :, :] * grad_agg.astype(jnp.float32)[:, None, :]
    total_rows = cached_embed.shape[1]
    contrib = (
        jnp.zeros((col_width, total_rows), jnp.float32)
        .at[:, neighbours.reshape(-1)]
        .add(spread.reshape(col_width, -1))
    )
    back = lax.psum_scatter(contrib, "dom", scatter_dimension=1, tiled=True)
    grad_feat = (own_term + my_fresh.astype(jnp.float32) * back).astype(jnp.bfloat16)
    return (activation, grad_feat, grad_self, grad_nbr, grad_bias)


def solution(mesh):
    placed = (
        P("col", "dom"),
        P("col", None),
        P(),
        P(),
        P(None, "dom"),
        P("dom"),
        P("col", None),
        P("col", None),
        P("col"),
        P("col", "dom"),
    )
    return jax.shard_map(
        per_device,
        mesh=mesh,
        in_specs=placed,
        out_specs=(P("col", "dom"), P("col", "dom"), P("col", None), P("col", None), P("col")),
        check_vma=False,
    )
```

profile of v0, /device:TPU:1, one launch (start us, length us, event | category | flops | bytes accessed | tf_op | source)
XLA Modules:
  0.0 573.6 jit_solution(13687929819668123944)
XLA Ops:
  7.2 0.0 copy-start
  7.2 0.0 reduce-scatter.3.cloned.1.call-start
  7.2 0.7 compare_convert_fusion
  7.9 1.2 dynamic_slice.9
  9.2 0.6 dynamic_slice.10
  9.8 0.7 fusion.12
  10.5 1.3 convert_divide_fusion
  11.8 0.7 fusion.14
  12.5 0.1 copy.21
  12.7 0.8 copy.16
  14.1 100.4 %all_gather.6 = bf16[16,16384]{0,1:T(8,128)(2,1)} all-gather(bf16[16,256]{0,1:T(8,128)(2,1)S(1)} %broadcast_select_fusion), channel_id=1, replica_groups=mesh['dom'=64,'col'=8] {'dom'}, dimensions={1}, use_global_device_ids=true | all-gather | bytes 532480 | tf_op jit(solution)/shard_map/all_gather | solution.py:41
  114.5 13.8 %gather_fusion = bf16[4096,16]{1,0:T(8,128)(2,1)S(1)} fusion(bf16[16,16384]{0,1:T(8,128)(2,1)} %all_gather.6, s32[4096]{0:T(1024)S(1)} %broadcast_clamp_fusion), kind=kCustom, calls=%fused_computation | custom fusion | bytes 278528 | tf_op jit(solution)/shard_map/gather | solution.py:47
  128.4 0.7 fusion.2
  129.1 0.2 convolution_bitcast_fusion
  129.4 0.9 fusion.4
  130.2 0.0 reduce-scatter.3.cloned.1.call-update
  130.2 0.0 reduce-scatter.5.cloned.1.call-start
  130.4 0.7 compare_convert_fusion.1
  131.0 81.8 %reduce-scatter.3.cloned.1.call-done = bf16[32,256]{1,0:T(8,128)(2,1)} async-done(((bf16[256,256]{1,0:T(8,128)(2,1)}), bf16[32,256]{1,0:T(8,128)(2,1)}) %reduce-scatter.3.cloned.1.call-update) | async-done | bytes 16400 | tf_op jit(solution)/shard_map/reduce_scatter | solution.py:51
  212.9 1.5 convert_reduce_fusion
  214.4 37.6 %all_gather.7 = bf16[256,256]{1,0:T(8,128)(2,1)S(1)} all-gather(bf16[32,256]{1,0:T(8,128)(2,1)S(1)} %get-tuple-element.9), channel_id=1, replica_groups=mesh['dom'=64,'col'=8] {'col'}, dimensions={0}, use_global_device_ids=true | all-gather | bytes 147456 | tf_op jit(solution)/shard_map/all_gather | solution.py:64
  252.0 0.1 fusion.8
  252.2 0.1 copy.18
  252.3 0.6 bitcast_multiply_fusion
  252.9 26.1 %scatter_custom_fusion = f32[16,16384]{0,1:T(8,128)} fusion(s32[4096]{0:T(1024)S(1)} %bitcast.50, f32[]{:T(128)} %constant.14.clone.1, f32[16,4096]{0,1:T(8,128)S(1)} %bitcast_multiply_fusion), kind=kCustom, calls=%fused_computation.2 | custom fusion | flops 65536 | bytes 3145732 | tf_op jit(solution)/shard_map/scatter-add | solution.py:76
  279.0 6.0 %copy.19 = f32[16,16384]{1,0:T(8,128)} copy(f32[16,16384]{0,1:T(8,128)} %scatter_custom_fusion) | data formatting | bytes 2097152 | tf_op jit(solution)/shard_map/scatter-add | solution.py:76
  285.0 0.0 reduce-scatter.5.cloned.1.call-update
  285.7 0.1 convolution_bitcast_fusion.2
  285.8 0.2 fusion.15
  286.0 267.8 %all-reduce = (f32[16,256]{1,0:T(8,128)}, f32[16,256]{1,0:T(8,128)}, f32[32]{0:T(128)}) all-reduce(f32[16,256]{1,0:T(8,128)S(1)} %convolution_bitcast_fusion.2, f32[16,256]{1,0:T(8,128)S(1)} %fusion.15, f32[32]{0:T(128)S(1)} %get-tuple-element.8), channel_id=1, replica_groups=mesh['dom'=64,'col'=8] {'dom'}, use_global_device_ids=true, to_apply=%region_4.5 | all-reduce | flops 8224 | bytes 65792 | tf_op jit(solution)/shard_map/psum | solution.py:68
  553.8 11.5 %reduce-scatter.5.cloned.1.call-done = f32[16,256]{1,0:T(8,128)} async-done(((f32[16,16384]{1,0:T(8,128)}), f32[16,256]{1,0:T(8,128)}) %reduce-scatter.5.cloned.1.call-update) | async-done | bytes 16400 | tf_op jit(solution)/shard_map/reduce_scatter | solution.py:78
  565.3 1.5 fusion.6
  (20 shorter events, 0.1 us)
Async XLA Ops:
  7.2 5.4 copy-start
  7.2 205.7 %reduce-scatter.3.cloned.1.call-start = ((), (), s32[]{:S(2)}) async-start(), calls=%async_computation.2 | async-start | bytes 147456 | tf_op jit(solution)/shard_map/reduce_scatter | solution.py:51
  114.5 14.6 %copy-start.4 = (bf16[16,256]{1,0:T(8,128)(2,1)S(1)}, bf16[16,256]{1,0:T(8,128)(2,1)}, u32[]{:S(2)}) copy-start(bf16[16,256]{1,0:T(8,128)(2,1)} %param.17) | copy-start | bytes 24580
  114.5 14.8 %copy-start.1 = (bf16[16,256]{1,0:T(8,128)(2,1)S(1)}, bf16[16,256]{1,0:T(8,128)(2,1)}, u32[]{:S(2)}) copy-start(bf16[16,256]{1,0:T(8,128)(2,1)} %param.10) | copy-start | bytes 24580
  114.5 14.8 %copy-start.3 = (bf16[16,256]{1,0:T(8,128)(2,1)S(1)}, bf16[16,256]{1,0:T(8,128)(2,1)}, u32[]{:S(2)}) copy-start(bf16[16,256]{1,0:T(8,128)(2,1)} %param.16) | copy-start | bytes 24580
  114.5 15.8 %copy-start.2 = (s32[16,256]{1,0:T(8,128)S(1)}, s32[16,256]{1,0:T(8,128)}, u32[]{:S(2)}) copy-start(s32[16,256]{1,0:T(8,128)} %param.14) | copy-start | bytes 49156
  114.5 98.4 %copy-start.5 = (bf16[32,256]{1,0:T(8,128)(2,1)S(1)}, bf16[32,256]{1,0:T(8,128)(2,1)}, u32[]{:S(2)}) copy-start(bf16[32,256]{1,0:T(8,128)(2,1)} %param.19) | copy-start | bytes 49156
  114.5 98.4 %copy-start.6 = (f32[32]{0:T(128)S(1)}, f32[32]{0:T(128)}, u32[]{:S(2)}) copy-start(f32[32]{0:T(128)} %param.18) | copy-start | bytes 388
  130.2 435.1 %reduce-scatter.5.cloned.1.call-start = ((), (), s32[]{:S(2)}) async-start(), calls=%async_computation.3 | async-start | bytes 1064960 | tf_op jit(solution)/shard_map/reduce_scatter | solution.py:78
Sparse Core Ops, SparseCore 0:
  130.4 82.4 reduce-scatter.2
  285.1 280.1 reduce-scatter.4
where the time goes:
time: 578 us; the launch traced here: 574 us
  blocking collectives  406 us (70%)
  waiting for transfers between devices  93.4 us (16%)
  other arithmetic  33.1 us (6%)
  local copies, waits for them, and re-layouts  22.8 us (4%)
  between operations  15.5 us (3%)
    psum x1, blocking collectives, per_device(): lax.psum((self_part, nbr_part, bias_part), 'dom')  268 us
    all_gather x1, blocking collectives, per_device(): sources = lax.all_gather(own_source, 'dom', axis=1, tiled=True)  100 us
    reduce_scatter x1, waiting for transfers between devices, per_device(): lax.psum_scatter(partial_pre.astype(jnp.bfloat16), 'col', scatter_dimensi...  81.8 us
    all_gather x1, blocking collectives, per_device(): grad_full = lax.all_gather(grad_pre, 'col', axis=0, tiled=True)  37.6 us
    scatter-add x1, other arithmetic, per_device(): contrib = jnp.zeros((col_width, total_rows), jnp.float32).at[:, neighbour...  26.1 us
    gather x1, local copies, waits for them, and re-layouts, per_device(): gathered = sources[:, neighbours].astype(jnp.float32)  13.8 us
  transfers between devices with their start and end apart: 2, of which 2 were waited for; matrix products, arithmetic and copies ran while one was open for 0% of the time, Pallas kernels for 0%

commit v1 on v0

--- a/solution.py
+++ b/solution.py
@@ -1,9 +1,14 @@
+import functools
+
 import jax
 import jax.numpy as jnp
 from jax import lax
+from jax.experimental import pallas as pl
+from jax.experimental.pallas import tpu as pltpu
 from jax.sharding import PartitionSpec as P
 
 LIMIT = 8
+MESH = pl.DeviceIdType.MESH
 
 
 def left_product(weight, data):
@@ -18,6 +23,76 @@
     )
 
 
+def exchange_kernel(axis, size, stride, bcast, reduce, x_ref, y_ref, buf, send_sem, recv_sem):
+    me = lax.axis_index(axis)
+    pos = lax.rem(me // stride, size)
+
+    def member(j):
+        return me + (j - pos) * stride
+
+    barrier = pltpu.get_barrier_semaphore()
+
+    def greet(k, carry):
+        j = lax.rem(pos + k, size)
+        pl.semaphore_signal(barrier, 1, device_id={axis: member(j)}, device_id_type=MESH)
+        return carry
+
+    lax.fori_loop(1, size, greet, 0)
+    pl.semaphore_wait(barrier, size - 1)
+
+    def desc(j, slot):
+        src = x_ref if bcast else x_ref.at[j]
+        return pltpu.make_async_remote_copy(
+            src_ref=src,
+            dst_ref=buf.at[slot],
+            send_sem=send_sem.at[j],
+            recv_sem=recv_sem.at[slot],
+            device_id={axis: member(j)},
+            device_id_type=MESH,
+        )
+
+    def send(k, carry):
+        j = lax.rem(pos + k, size)
+        desc(j, pos).start()
+        return carry
+
+    lax.fori_loop(1, size, send, 0)
+    if bcast:
+        buf[pos] = x_ref[...]
+    else:
+        buf[pos] = x_ref[pos]
+
+    def finish(k, carry):
+        j = lax.rem(pos + k, size)
+        desc(j, pos).wait_send()
+        desc(j, j).wait_recv()
+        return carry
+
+    lax.fori_loop(1, size, finish, 0)
+    if reduce:
+        y_ref[...] = jnp.sum(buf[...].astype(jnp.float32), axis=0)
+    else:
+        y_ref[...] = buf[...]
+
+
+def exchange(x, ident, axis, size, stride=1, bcast=False, reduce=False):
+    block = x.shape if bcast else x.shape[1:]
+    out_shape = block if reduce else (size,) + block
+    out_dtype = jnp.float32 if reduce else x.dtype
+    return pl.pallas_call(
+        functools.partial(exchange_kernel, axis, size, stride, bcast, reduce),
+        out_shape=jax.ShapeDtypeStruct(out_shape, out_dtype),
+        in_specs=[pl.BlockSpec(memory_space=pltpu.VMEM)],
+        out_specs=pl.BlockSpec(memory_space=pltpu.VMEM),
+        scratch_shapes=[
+            pltpu.VMEM((size,) + block, x.dtype),
+            pltpu.SemaphoreType.DMA((size,)),
+            pltpu.SemaphoreType.DMA((size,)),
+        ],
+        compiler_params=pltpu.CompilerParams(collective_id=ident, has_side_effects=True),
+    )(x)
+
+
 def per_device(
     features,
     cached_embed,
@@ -30,15 +105,19 @@
     sage_bias,
     cotangent,
 ):
+    n_dom = lax.axis_size("dom")
+    n_col = lax.axis_size("col")
     col_width = features.shape[0]
     part_rows = features.shape[1]
     slot_count = neighbours.shape[0]
+    hidden = w_self.shape[1]
     my_index = lax.axis_index("dom")
     fresh_flag = (staleness >= LIMIT).astype(jnp.int32)
     my_fresh = fresh_flag[my_index]
     own_cache = lax.dynamic_slice_in_dim(cached_embed, my_index * part_rows, part_rows, 1)
     own_source = jnp.where(my_fresh == 1, features, own_cache)
-    sources = lax.all_gather(own_source, "dom", axis=1, tiled=True)
+    blocks = exchange(own_source, 0, "dom", n_dom, bcast=True)
+    sources = blocks.transpose(1, 0, 2).reshape(col_width, n_dom * part_rows)
     local_slot = jnp.arange(part_rows, dtype=jnp.int32)
     live_rows = (local_slot < node_counts[my_index]).astype(jnp.float32)
     slot_index = jnp.arange(slot_count, dtype=jnp.int32)
@@ -48,9 +127,7 @@
     aggregated = jnp.sum(weights[None, :, :] * gathered, axis=1).astype(jnp.bfloat16)
     partial_pre = left_product(w_self, features) + left_product(w_nbr, aggregated)
     pre_act = (
-        lax.psum_scatter(
-            partial_pre.astype(jnp.bfloat16), "col", scatter_dimension=0, tiled=True
-        ).astype(jnp.float32)
+        exchange(partial_pre.reshape(n_col, hidden // n_col, part_rows), 1, "col", n_col, reduce=True)
         + sage_bias[:, None]
     )
     sigmoid = 1.0 / (1.0 + jnp.exp(-pre_act))
@@ -61,11 +138,19 @@
         * sigmoid
         * (1.0 + pre_act * (1.0 - sigmoid))
     ).astype(jnp.bfloat16)
-    grad_full = lax.all_gather(grad_pre, "col", axis=0, tiled=True)
+    grad_full = exchange(grad_pre, 2, "col", n_col, bcast=True).reshape(hidden, part_rows)
     self_part = right_product(features, grad_full)
     nbr_part = right_product(aggregated, grad_full)
     bias_part = jnp.sum(grad_pre.astype(jnp.float32), axis=1)
-    grad_self, grad_nbr, grad_bias = lax.psum((self_part, nbr_part, bias_part), "dom")
+    bias_rows = jnp.zeros((8, hidden), jnp.float32).at[0, : bias_part.shape[0]].set(bias_part)
+    packed = jnp.concatenate([self_part, nbr_part, bias_rows], axis=0)
+    group = 8 if n_dom % 8 == 0 else n_dom
+    summed = exchange(packed, 3, "dom", group, bcast=True, reduce=True)
+    if group < n_dom:
+        summed = exchange(summed, 4, "dom", n_dom // group, stride=group, bcast=True, reduce=True)
+    grad_self = summed[:col_width]
+    grad_nbr = summed[col_width : 2 * col_width]
+    grad_bias = summed[2 * col_width, : bias_part.shape[0]]
     grad_agg = jnp.dot(w_nbr, grad_full, preferred_element_type=jnp.float32).astype(jnp.bfloat16)
     own_term = jnp.dot(w_self, grad_full, preferred_element_type=jnp.float32)
     spread = weights[None, :, :] * grad_agg.astype(jnp.float32)[:, None, :]
@@ -75,7 +160,8 @@
         .at[:, neighbours.reshape(-1)]
         .add(spread.reshape(col_width, -1))
     )
-    back = lax.psum_scatter(contrib, "dom", scatter_dimension=1, tiled=True)
+    contrib_blocks = contrib.reshape(col_width, n_dom, part_rows).transpose(1, 0, 2)
+    back = exchange(contrib_blocks, 5, "dom", n_dom, reduce=True)
     grad_feat = (own_term + my_fresh.astype(jnp.float32) * back).astype(jnp.bfloat16)
     return (activation, grad_feat, grad_self, grad_nbr, grad_bias)
 

time: 578 us -> 202 us (0.35)
  blocking collectives: 406 us -> 0 us
  Pallas kernels: 0 us -> 128 us
  waiting for transfers between devices: 93.4 us -> 0 us
  between operations: 15.5 us -> 2.12 us
  local copies, waits for them, and re-layouts: 22.8 us -> 29.6 us
    psum x1 -> x0, blocking collectives: 268 us -> none  [per_device(): lax.psum((self_part, nbr_part, bias_part), 'dom')]
    all_gather x2 -> x0, blocking collectives: 138 us -> none  [the longest x1 100 us: per_device(): sources = lax.all_gather(own_source, 'dom', axis=1, tiled=True)]
    pallas_call x0 -> x6, Pallas kernels: none -> 128 us  [exchange(): pl.pallas_call(functools.partial(exchange_kernel, axis, size, stride, bca...]
    reduce_scatter x2 -> x0, waiting for transfers between devices: 93.4 us -> none  [the longest x1 81.8 us: per_device(): lax.psum_scatter(partial_pre.astype(jnp.bfloat16), 'col', scatter_dimensi...]
    reshape x0 -> x2, local copies, waits for them, and re-layouts: none -> 10.5 us  [the longest x1 6.04 us: per_device(): contrib.reshape(col_width, n_dom, part_rows).transpose(1, 0, 2)]
    scatter-add x1 -> x0, local copies, waits for them, and re-layouts: 5.99 us -> none  [per_device(): contrib = jnp.zeros((col_width, total_rows), jnp.float32).at[:, neighbour...]
  transfers between devices with their start and end apart: 2 -> 0, of which waited for: 2 -> 0; matrix products, arithmetic and copies ran while one was open for 0% -> 0% of each run, Pallas kernels for 0% -> 0%
where the time goes in v1:
time: 202 us; the launch traced here: 201 us
  Pallas kernels  128 us (63%)
  other arithmetic  35 us (17%)
  local copies, waits for them, and re-layouts  29.6 us (15%)
  matrix products  5.8 us (3%)
  between operations  2.12 us (1%)
    pallas_call x6, Pallas kernels, exchange(): pl.pallas_call(functools.partial(exchange_kernel, axis, size, stride, bca...  128 us
    scatter-add x1, other arithmetic, per_device(): contrib = jnp.zeros((col_width, total_rows), jnp.float32).at[:, neighbour...  26.1 us
    gather x1, local copies, waits for them, and re-layouts, per_device(): gathered = sources[:, neighbours].astype(jnp.float32)  13.8 us
    reshape x1, local copies, waits for them, and re-layouts, per_device(): contrib.reshape(col_width, n_dom, part_rows).transpose(1, 0, 2)  6.04 us
    reshape x1, local copies, waits for them, and re-layouts, per_device(): sources = blocks.transpose(1, 0, 2).reshape(col_width, n_dom * part_rows)  4.48 us

profile of v1, /device:TPU:1, one launch (start us, length us, event | category | flops | bytes accessed | tf_op | source)
XLA Modules:
  0.0 200.9 jit_solution(5705402990911210353)
XLA Ops:
  0.7 1.2 dynamic_slice.9
  1.9 0.7 compare_convert_fusion
  2.6 0.6 dynamic_slice.10
  4.4 1.3 convert_divide_fusion
  5.8 0.7 compare_convert_fusion.1
  6.4 1.3 dynamic-slice_select_fusion.x_ref
  7.7 0.7 copy.26
  8.5 0.7 fusion.11
  9.3 0.7 fusion.13
  10.0 29.3 %shard_map.137 = bf16[64,16,256]{2,1,0:T(8,128)(2,1)} custom-call(bf16[16,256]{1,0:T(8,128)(2,1)} %dynamic-slice_select_fusion.x_ref), custom_call_target="tpu_custom_call" | custom-call | tf_op jit(solution)/shard_map/pallas_call | solution.py:82
  39.2 4.5 %copy.21 = bf16[16,64,256]{0,2,1:T(8,128)(2,1)} copy(bf16[16,64,256]{2,0,1:T(8,128)(2,1)} %bitcast.61) | data formatting | bytes 1048576 | tf_op jit(solution)/shard_map/reshape | solution.py:120
  43.7 13.8 %gather_fusion = bf16[4096,16]{1,0:T(8,128)(2,1)S(1)} fusion(bf16[16,16384]{0,1:T(8,128)(2,1)} %bitcast.55, s32[4096]{0:T(1024)S(1)} %broadcast_clamp_fusion), kind=kCustom, calls=%fused_computation | custom fusion | bytes 278528 | tf_op jit(solution)/shard_map/gather | solution.py:126
  57.5 0.7 fusion.2
  58.3 0.2 convolution_bitcast_fusion
  58.5 0.9 convolution_add_fusion
  59.4 15.8 %shard_map.138 = f32[32,256]{1,0:T(8,128)} custom-call(f32[8,32,256]{2,1,0:T(8,128)} %bitcast.63), custom_call_target="tpu_custom_call" | custom-call | tf_op jit(solution)/shard_map/pallas_call | solution.py:82
  75.3 1.6 convert_reduce_fusion
  76.8 11.3 %shard_map.139 = bf16[8,32,256]{2,1,0:T(8,128)(2,1)} custom-call(bf16[32,256]{1,0:T(8,128)(2,1)} %get-tuple-element.18.x_ref), custom_call_target="tpu_custom_call" | custom-call | tf_op jit(solution)/shard_map/pallas_call | solution.py:82
  88.2 1.1 fusion.15
  89.2 1.1 convolution_bitcast_fusion.2
  90.3 0.7 select_maximum_fusion.x_ref
  91.0 13.4 %shard_map.141.x_ref = f32[40,256]{1,0:T(8,128)} custom-call(f32[40,256]{1,0:T(8,128)} %select_maximum_fusion.x_ref), custom_call_target="tpu_custom_call" | custom-call | tf_op jit(solution)/shard_map/pallas_call | solution.py:82
  104.4 17.4 %shard_map.142 = f32[40,256]{1,0:T(8,128)} custom-call(f32[40,256]{1,0:T(8,128)} %shard_map.141.x_ref), custom_call_target="tpu_custom_call" | custom-call | tf_op jit(solution)/shard_map/pallas_call | solution.py:82
  121.8 1.2 slice_bitcast_fusion
  123.0 1.3 fusion.14
  124.4 1.0 fusion.7
  125.4 0.1 copy.18
  125.5 0.6 bitcast_multiply_fusion
  126.1 26.1 %scatter_custom_fusion = f32[16,16384]{0,1:T(8,128)} fusion(s32[4096]{0:T(1024)S(1)} %bitcast.68, f32[]{:T(128)} %constant.49.clone.1, f32[16,4096]{0,1:T(8,128)S(1)} %bitcast_multiply_fusion), kind=kCustom, calls=%fused_computation.2 | custom fusion | flops 65536 | bytes 3145732 | tf_op jit(solution)/shard_map/scatter-add | solution.py:161
  152.2 6.0 %copy.20 = f32[16,64,256]{2,0,1:T(8,128)} copy(f32[16,64,256]{0,2,1:T(8,128)} %bitcast.54) | data formatting | bytes 2097152 | tf_op jit(solution)/shard_map/reshape | solution.py:163
  158.3 41.1 %shard_map.140 = f32[16,256]{1,0:T(8,128)} custom-call(f32[64,16,256]{2,1,0:T(8,128)} %bitcast.56), custom_call_target="tpu_custom_call" | custom-call | tf_op jit(solution)/shard_map/pallas_call | solution.py:82
  199.4 1.5 fusion.5
  (16 shorter events, 0.1 us)
Async XLA Ops:
  0.6 57.6 %copy-start = (bf16[16,256]{1,0:T(8,128)(2,1)S(1)}, bf16[16,256]{1,0:T(8,128)(2,1)}, u32[]{:S(2)}) copy-start(bf16[16,256]{1,0:T(8,128)(2,1)} %param.19) | copy-start | bytes 24580
  43.7 14.8 %copy-start.2 = (bf16[16,256]{1,0:T(8,128)(2,1)S(1)}, bf16[16,256]{1,0:T(8,128)(2,1)}, u32[]{:S(2)}) copy-start(bf16[16,256]{1,0:T(8,128)(2,1)} %param.12) | copy-start | bytes 24580
  43.7 14.8 %copy-start.3 = (bf16[16,256]{1,0:T(8,128)(2,1)S(1)}, bf16[16,256]{1,0:T(8,128)(2,1)}, u32[]{:S(2)}) copy-start(bf16[16,256]{1,0:T(8,128)(2,1)} %param.18) | copy-start | bytes 24580
  43.7 31.6 %copy-start.4 = (bf16[32,256]{1,0:T(8,128)(2,1)S(1)}, bf16[32,256]{1,0:T(8,128)(2,1)}, u32[]{:S(2)}) copy-start(bf16[32,256]{1,0:T(8,128)(2,1)} %param.21) | copy-start | bytes 49156
  43.7 31.6 %copy-start.5 = (f32[32]{0:T(128)S(1)}, f32[32]{0:T(128)}, u32[]{:S(2)}) copy-start(f32[32]{0:T(128)} %param.20) | copy-start | bytes 388
  152.2 47.2 %copy-start.1 = (bf16[8,32,256]{2,1,0:T(8,128)(2,1)S(1)}, bf16[8,32,256]{2,1,0:T(8,128)(2,1)}, u32[]{:S(2)}) copy-start(bf16[8,32,256]{2,1,0:T(8,128)(2,1)} %shard_map.139) | copy-start | bytes 393220

commit v2 on v1

--- a/solution.py
+++ b/solution.py
@@ -23,7 +23,7 @@
     )
 
 
-def exchange_kernel(axis, size, stride, bcast, reduce, x_ref, y_ref, buf, send_sem, recv_sem):
+def exchange_kernel(axis, size, stride, bcast, reduce, lanes, x_ref, y_ref, buf, send_sem, recv_sem):
     me = lax.axis_index(axis)
     pos = lax.rem(me // stride, size)
 
@@ -40,8 +40,15 @@
     lax.fori_loop(1, size, greet, 0)
     pl.semaphore_wait(barrier, size - 1)
 
+    def chunk(j):
+        if bcast:
+            return x_ref
+        if lanes:
+            return x_ref.at[:, pl.ds(pl.multiple_of(j * lanes, lanes), lanes)]
+        return x_ref.at[j]
+
     def desc(j, slot):
-        src = x_ref if bcast else x_ref.at[j]
+        src = chunk(j)
         return pltpu.make_async_remote_copy(
             src_ref=src,
             dst_ref=buf.at[slot],
@@ -57,10 +64,7 @@
         return carry
 
     lax.fori_loop(1, size, send, 0)
-    if bcast:
-        buf[pos] = x_ref[...]
-    else:
-        buf[pos] = x_ref[pos]
+    buf[pos] = chunk(pos)[...]
 
     def finish(k, carry):
         j = lax.rem(pos + k, size)
@@ -75,12 +79,17 @@
         y_ref[...] = buf[...]
 
 
-def exchange(x, ident, axis, size, stride=1, bcast=False, reduce=False):
-    block = x.shape if bcast else x.shape[1:]
+def exchange(x, ident, axis, size, stride=1, bcast=False, reduce=False, lanes=0):
+    if bcast:
+        block = x.shape
+    elif lanes:
+        block = (x.shape[0], lanes)
+    else:
+        block = x.shape[1:]
     out_shape = block if reduce else (size,) + block
     out_dtype = jnp.float32 if reduce else x.dtype
     return pl.pallas_call(
-        functools.partial(exchange_kernel, axis, size, stride, bcast, reduce),
+        functools.partial(exchange_kernel, axis, size, stride, bcast, reduce, lanes),
         out_shape=jax.ShapeDtypeStruct(out_shape, out_dtype),
         in_specs=[pl.BlockSpec(memory_space=pltpu.VMEM)],
         out_specs=pl.BlockSpec(memory_space=pltpu.VMEM),
@@ -160,8 +169,7 @@
         .at[:, neighbours.reshape(-1)]
         .add(spread.reshape(col_width, -1))
     )
-    contrib_blocks = contrib.reshape(col_width, n_dom, part_rows).transpose(1, 0, 2)
-    back = exchange(contrib_blocks, 5, "dom", n_dom, reduce=True)
+    back = exchange(contrib.astype(jnp.bfloat16), 5, "dom", n_dom, reduce=True, lanes=part_rows)
     grad_feat = (own_term + my_fresh.astype(jnp.float32) * back).astype(jnp.bfloat16)
     return (activation, grad_feat, grad_self, grad_nbr, grad_bias)
 

time: 202 us -> 187 us (0.926)
  Pallas kernels: 128 us -> 114 us
    pallas_call x6, Pallas kernels: 128 us -> 114 us  [exchange(): pl.pallas_call(functools.partial(exchange_kernel, axis, size, stride, bca...]
    reshape x1 -> x0, local copies, waits for them, and re-layouts: 6.04 us -> none  [per_device(): contrib.reshape(col_width, n_dom, part_rows).transpose(1, 0, 2)]
    scatter-add x0 -> x1, local copies, waits for them, and re-layouts: none -> 5.37 us  [per_device(): contrib = jnp.zeros((col_width, total_rows), jnp.float32).at[:, neighbour...]
where the time goes in v2:
time: 187 us; the launch traced here: 186 us
  Pallas kernels  114 us (61%)
  other arithmetic  35 us (19%)
  local copies, waits for them, and re-layouts  28.9 us (15%)
  matrix products  5.8 us (3%)
  between operations  2.12 us (1%)
    pallas_call x6, Pallas kernels, exchange(): pl.pallas_call(functools.partial(exchange_kernel, axis, size, stride, bca...  114 us
    scatter-add x1, other arithmetic, per_device(): contrib = jnp.zeros((col_width, total_rows), jnp.float32).at[:, neighbour...  26.1 us
    gather x1, local copies, waits for them, and re-layouts, per_device(): gathered = sources[:, neighbours].astype(jnp.float32)  13.8 us
    scatter-add x1, local copies, waits for them, and re-layouts, per_device(): contrib = jnp.zeros((col_width, total_rows), jnp.float32).at[:, neighbour...  5.37 us
    reshape x1, local copies, waits for them, and re-layouts, per_device(): sources = blocks.transpose(1, 0, 2).reshape(col_width, n_dom * part_rows)  4.48 us

profile of v2, /device:TPU:1, one launch (start us, length us, event | category | flops | bytes accessed | tf_op | source)
XLA Modules:
  0.0 186.2 jit_solution(6330699005050977015)
XLA Ops:
  0.7 1.2 dynamic_slice.9
  1.9 0.7 compare_convert_fusion
  2.6 0.6 dynamic_slice.10
  4.4 1.3 convert_divide_fusion
  5.8 0.7 compare_convert_fusion.1
  6.4 1.3 dynamic-slice_select_fusion.x_ref
  7.7 0.7 copy.24
  8.5 0.7 fusion.11
  9.3 0.7 fusion.13
  10.0 29.3 %shard_map.137 = bf16[64,16,256]{2,1,0:T(8,128)(2,1)} custom-call(bf16[16,256]{1,0:T(8,128)(2,1)} %dynamic-slice_select_fusion.x_ref), custom_call_target="tpu_custom_call" | custom-call | tf_op jit(solution)/shard_map/pallas_call | solution.py:91
  39.2 4.5 %copy.21 = bf16[16,64,256]{0,2,1:T(8,128)(2,1)} copy(bf16[16,64,256]{2,0,1:T(8,128)(2,1)} %bitcast.57) | data formatting | bytes 1048576 | tf_op jit(solution)/shard_map/reshape | solution.py:129
  43.7 13.8 %gather_fusion = bf16[4096,16]{1,0:T(8,128)(2,1)S(1)} fusion(bf16[16,16384]{0,1:T(8,128)(2,1)} %bitcast.52, s32[4096]{0:T(1024)S(1)} %broadcast_clamp_fusion), kind=kCustom, calls=%fused_computation | custom fusion | bytes 278528 | tf_op jit(solution)/shard_map/gather | solution.py:135
  57.5 0.7 fusion.2
  58.3 0.2 convolution_bitcast_fusion
  58.5 0.9 convolution_add_fusion
  59.4 15.8 %shard_map.138 = f32[32,256]{1,0:T(8,128)} custom-call(f32[8,32,256]{2,1,0:T(8,128)} %bitcast.59), custom_call_target="tpu_custom_call" | custom-call | tf_op jit(solution)/shard_map/pallas_call | solution.py:91
  75.3 1.6 convert_reduce_fusion
  76.8 11.3 %shard_map.139 = bf16[8,32,256]{2,1,0:T(8,128)(2,1)} custom-call(bf16[32,256]{1,0:T(8,128)(2,1)} %get-tuple-element.18.x_ref), custom_call_target="tpu_custom_call" | custom-call | tf_op jit(solution)/shard_map/pallas_call | solution.py:91
  88.2 1.1 fusion.15
  89.2 1.1 convolution_bitcast_fusion.2
  90.3 0.7 select_maximum_fusion.x_ref
  90.9 13.4 %shard_map.141.x_ref = f32[40,256]{1,0:T(8,128)} custom-call(f32[40,256]{1,0:T(8,128)} %select_maximum_fusion.x_ref), custom_call_target="tpu_custom_call" | custom-call | tf_op jit(solution)/shard_map/pallas_call | solution.py:91
  104.4 17.5 %shard_map.142 = f32[40,256]{1,0:T(8,128)} custom-call(f32[40,256]{1,0:T(8,128)} %shard_map.141.x_ref), custom_call_target="tpu_custom_call" | custom-call | tf_op jit(solution)/shard_map/pallas_call | solution.py:91
  121.9 1.2 slice_bitcast_fusion
  123.1 1.3 fusion.14
  124.4 1.0 fusion.7
  125.5 0.1 copy.19
  125.6 0.6 bitcast_multiply_fusion
  126.2 26.1 %scatter_custom_fusion = f32[16,16384]{0,1:T(8,128)} fusion(s32[4096]{0:T(1024)S(1)} %bitcast.64, f32[]{:T(128)} %constant.49.clone.1, f32[16,4096]{0,1:T(8,128)S(1)} %bitcast_multiply_fusion), kind=kCustom, calls=%fused_computation.2 | custom fusion | flops 65536 | bytes 3145732 | tf_op jit(solution)/shard_map/scatter-add | solution.py:170
  152.3 5.4 %copy.20.x_ref = bf16[16,16384]{1,0:T(8,128)(2,1)} copy(f32[16,16384]{0,1:T(8,128)} %scatter_custom_fusion) | data formatting | bytes 1572864 | tf_op jit(solution)/shard_map/scatter-add | solution.py:170
  157.7 27.0 %shard_map.140 = f32[16,256]{1,0:T(8,128)} custom-call(bf16[16,16384]{1,0:T(8,128)(2,1)} %copy.20.x_ref), custom_call_target="tpu_custom_call" | custom-call | tf_op jit(solution)/shard_map/pallas_call | solution.py:91
  184.7 1.5 fusion.5
  (16 shorter events, 0.1 us)
Async XLA Ops:
  0.6 57.6 %copy-start = (bf16[16,256]{1,0:T(8,128)(2,1)S(1)}, bf16[16,256]{1,0:T(8,128)(2,1)}, u32[]{:S(2)}) copy-start(bf16[16,256]{1,0:T(8,128)(2,1)} %param.19) | copy-start | bytes 24580
  43.7 14.8 %copy-start.2 = (bf16[16,256]{1,0:T(8,128)(2,1)S(1)}, bf16[16,256]{1,0:T(8,128)(2,1)}, u32[]{:S(2)}) copy-start(bf16[16,256]{1,0:T(8,128)(2,1)} %param.12) | copy-start | bytes 24580
  43.7 14.8 %copy-start.3 = (bf16[16,256]{1,0:T(8,128)(2,1)S(1)}, bf16[16,256]{1,0:T(8,128)(2,1)}, u32[]{:S(2)}) copy-start(bf16[16,256]{1,0:T(8,128)(2,1)} %param.18) | copy-start | bytes 24580
  43.7 31.5 %copy-start.4 = (bf16[32,256]{1,0:T(8,128)(2,1)S(1)}, bf16[32,256]{1,0:T(8,128)(2,1)}, u32[]{:S(2)}) copy-start(bf16[32,256]{1,0:T(8,128)(2,1)} %param.21) | copy-start | bytes 49156
  43.7 31.5 %copy-start.5 = (f32[32]{0:T(128)S(1)}, f32[32]{0:T(128)}, u32[]{:S(2)}) copy-start(f32[32]{0:T(128)} %param.20) | copy-start | bytes 388
  152.3 32.4 %copy-start.1 = (bf16[8,32,256]{2,1,0:T(8,128)(2,1)S(1)}, bf16[8,32,256]{2,1,0:T(8,128)(2,1)}, u32[]{:S(2)}) copy-start(bf16[8,32,256]{2,1,0:T(8,128)(2,1)} %shard_map.139) | copy-start | bytes 393220

commit v3 on v0

v3 whole, which is shorter than its diff:
```python
import functools

import jax
import jax.numpy as jnp
from jax import lax
from jax.experimental import pallas as pl
from jax.experimental.pallas import tpu as pltpu
from jax.sharding import PartitionSpec as P

LIMIT = 8
MESH = pl.DeviceIdType.MESH


def left_product(weight, data):
    return lax.dot_general(
        weight, data, (((0,), (0,)), ((), ())), preferred_element_type=jnp.float32
    )


def right_product(data, grads):
    return lax.dot_general(
        data, grads, (((1,), (1,)), ((), ())), preferred_element_type=jnp.float32
    )


def exchange_kernel(specs, *refs):
    count = len(specs)
    xs, ys = refs[:count], refs[count : 2 * count]
    scratch = refs[2 * count :]
    barrier = pltpu.get_barrier_semaphore()
    plans = []
    for e, (axis, size, stride, bcast, reduce, lanes) in enumerate(specs):
        x_ref, y_ref = xs[e], ys[e]
        buf, send_sem, recv_sem = scratch[3 * e : 3 * e + 3]
        me = lax.axis_index(axis)
        pos = lax.rem(me // stride, size)
        plans.append((axis, size, stride, bcast, reduce, lanes, x_ref, y_ref, buf, send_sem, recv_sem, me, pos))

    def member(plan, j):
        stride, me, pos = plan[2], plan[11], plan[12]
        return me + (j - pos) * stride

    def chunk(plan, j):
        bcast, lanes, x_ref = plan[3], plan[5], plan[6]
        if bcast:
            return x_ref
        if lanes:
            return x_ref.at[:, pl.ds(pl.multiple_of(j * lanes, lanes), lanes)]
        return x_ref.at[j]

    def desc(plan, j, slot):
        axis, buf, send_sem, recv_sem = plan[0], plan[8], plan[9], plan[10]
        return pltpu.make_async_remote_copy(
            src_ref=chunk(plan, j),
            dst_ref=buf.at[slot],
            send_sem=send_sem.at[j],
            recv_sem=recv_sem.at[slot],
            device_id={axis: member(plan, j)},
            device_id_type=MESH,
        )

    def each_peer(plan, body):
        size, pos = plan[1], plan[12]

        def step(k, carry):
            body(lax.rem(pos + k, size))
            return carry

        lax.fori_loop(1, size, step, 0)

    greetings = 0
    for plan in plans:
        each_peer(
            plan,
            lambda j, plan=plan: pl.semaphore_signal(
                barrier, 1, device_id={plan[0]: member(plan, j)}, device_id_type=MESH
            ),
        )
        greetings += plan[1] - 1
    pl.semaphore_wait(barrier, greetings)
    for plan in plans:
        each_peer(plan, lambda j, plan=plan: desc(plan, j, plan[12]).start())
    for plan in plans:
        buf, pos = plan[8], plan[12]
        buf[pos] = chunk(plan, pos)[...]
    for plan in plans:

        def finish(j, plan=plan):
            desc(plan, j, plan[12]).wait_send()
            desc(plan, j, j).wait_recv()

        each_peer(plan, finish)
    for plan in plans:
        reduce, y_ref, buf = plan[4], plan[7], plan[8]
        if reduce:
            y_ref[...] = jnp.sum(buf[...].astype(jnp.float32), axis=0)
        else:
            y_ref[...] = buf[...]


def exchange_many(ident, jobs):
    specs, out_shapes, scratch = [], [], []
    for x, axis, size, stride, bcast, reduce, lanes in jobs:
        if bcast:
            block = x.shape
        elif lanes:
            block = (x.shape[0], lanes)
        else:
            block = x.shape[1:]
        specs.append((axis, size, stride, bcast, reduce, lanes))
        out_shapes.append(
            jax.ShapeDtypeStruct(block if reduce else (size,) + block, jnp.float32 if reduce else x.dtype)
        )
        scratch += [
            pltpu.VMEM((size,) + block, x.dtype),
            pltpu.SemaphoreType.DMA((size,)),
            pltpu.SemaphoreType.DMA((size,)),
        ]
    return pl.pallas_call(
        functools.partial(exchange_kernel, tuple(specs)),
        out_shape=tuple(out_shapes),
        in_specs=[pl.BlockSpec(memory_space=pltpu.VMEM)] * len(jobs),
        out_specs=tuple(pl.BlockSpec(memory_space=pltpu.VMEM) for _ in jobs),
        scratch_shapes=scratch,
        compiler_params=pltpu.CompilerParams(collective_id=ident, has_side_effects=True),
    )(*[job[0] for job in jobs])


def exchange(x, ident, axis, size, stride=1, bcast=False, reduce=False, lanes=0):
    return exchange_many(ident, [(x, axis, size, stride, bcast, reduce, lanes)])[0]


def per_device(
    features,
    cached_embed,
    staleness,
    node_counts,
    neighbours,
    degrees,
    w_self,
    w_nbr,
    sage_bias,
    cotangent,
):
    n_dom = lax.axis_size("dom")
    n_col = lax.axis_size("col")
    col_width = features.shape[0]
    part_rows = features.shape[1]
    slot_count = neighbours.shape[0]
    hidden = w_self.shape[1]
    my_index = lax.axis_index("dom")
    fresh_flag = (staleness >= LIMIT).astype(jnp.int32)
    my_fresh = fresh_flag[my_index]
    own_cache = lax.dynamic_slice_in_dim(cached_embed, my_index * part_rows, part_rows, 1)
    own_source = jnp.where(my_fresh == 1, features, own_cache)
    col_inputs = jnp.concatenate([features, w_self, w_nbr, cotangent], axis=0)
    bias_block = jnp.zeros((8, 128), jnp.float32).at[0, : sage_bias.shape[0]].set(sage_bias)
    blocks, col_blocks, bias_blocks = exchange_many(
        0,
        [
            (own_source, "dom", n_dom, 1, True, False, 0),
            (col_inputs, "col", n_col, 1, True, False, 0),
            (bias_block, "col", n_col, 1, True, False, 0),
        ],
    )
    sources = blocks.transpose(1, 0, 2).reshape(col_width, n_dom * part_rows)
    feat_full = col_blocks[:, :col_width].reshape(n_col * col_width, part_rows)
    w_self_full = col_blocks[:, col_width : 2 * col_width].reshape(n_col * col_width, hidden)
    w_nbr_full = col_blocks[:, 2 * col_width : 3 * col_width].reshape(n_col * col_width, hidden)
    cot_full = col_blocks[:, 3 * col_width :].reshape(hidden, part_rows)
    bias_full = bias_blocks[:, 0, : sage_bias.shape[0]].reshape(hidden)
    local_slot = jnp.arange(part_rows, dtype=jnp.int32)
    live_rows = (local_slot < node_counts[my_index]).astype(jnp.float32)
    slot_index = jnp.arange(slot_count, dtype=jnp.int32)
    used = (slot_index[:, None] < degrees[None, :]).astype(jnp.float32)
    weights = used * (live_rows / degrees.astype(jnp.float32))[None, :]
    gathered = sources[:, neighbours].astype(jnp.float32)
    aggregated = jnp.sum(weights[None, :, :] * gathered, axis=1).astype(jnp.bfloat16)
    agg_full = exchange(aggregated, 1, "col", n_col, bcast=True).reshape(n_col * col_width, part_rows)
    pre_full = (
        left_product(w_self_full, feat_full)
        + left_product(w_nbr_full, agg_full)
        + bias_full[:, None]
    )
    sig_full = 1.0 / (1.0 + jnp.exp(-pre_full))
    my_col = lax.axis_index("col")
    block_rows = hidden // n_col
    pre_act = lax.dynamic_slice_in_dim(pre_full, my_col * block_rows, block_rows, 0)
    sigmoid = lax.dynamic_slice_in_dim(sig_full, my_col * block_rows, block_rows, 0)
    activation = (live_rows[None, :] * pre_act * sigmoid).astype(jnp.bfloat16)
    grad_full = (
        live_rows[None, :]
        * cot_full.astype(jnp.float32)
        * sig_full
        * (1.0 + pre_full * (1.0 - sig_full))
    ).astype(jnp.bfloat16)
    grad_pre = lax.dynamic_slice_in_dim(grad_full, my_col * block_rows, block_rows, 0)
    self_part = right_product(features, grad_full)
    nbr_part = right_product(aggregated, grad_full)
    bias_part = jnp.sum(grad_pre.astype(jnp.float32), axis=1)
    bias_rows = jnp.zeros((8, hidden), jnp.float32).at[0, : bias_part.shape[0]].set(bias_part)
    packed = jnp.concatenate([self_part, nbr_part, bias_rows], axis=0)
    group = 8 if n_dom % 8 == 0 else n_dom
    summed = exchange(packed, 3, "dom", group, bcast=True, reduce=True)
    if group < n_dom:
        summed = exchange(summed, 4, "dom", n_dom // group, stride=group, bcast=True, reduce=True)
    grad_self = summed[:col_width]
    grad_nbr = summed[col_width : 2 * col_width]
    grad_bias = summed[2 * col_width, : bias_part.shape[0]]
    grad_agg = jnp.dot(w_nbr, grad_full, preferred_element_type=jnp.float32).astype(jnp.bfloat16)
    own_term = jnp.dot(w_self, grad_full, preferred_element_type=jnp.float32)
    spread = weights[None, :, :] * grad_agg.astype(jnp.float32)[:, None, :]
    total_rows = cached_embed.shape[1]
    contrib = (
        jnp.zeros((col_width, total_rows), jnp.float32)
        .at[:, neighbours.reshape(-1)]
        .add(spread.reshape(col_width, -1))
    )
    back = exchange(contrib.astype(jnp.bfloat16), 5, "dom", n_dom, reduce=True, lanes=part_rows)
    grad_feat = (own_term + my_fresh.astype(jnp.float32) * back).astype(jnp.bfloat16)
    return (activation, grad_feat, grad_self, grad_nbr, grad_bias)


def solution(mesh):
    placed = (
        P("col", "dom"),
        P("col", None),
        P(),
        P(),
        P(None, "dom"),
        P("dom"),
        P("col", None),
        P("col", None),
        P("col"),
        P("col", "dom"),
    )
    return jax.shard_map(
        per_device,
        mesh=mesh,
        in_specs=placed,
        out_specs=(P("col", "dom"), P("col", "dom"), P("col", None), P("col", None), P("col")),
        check_vma=False,
    )
```

time: 578 us -> 179 us (0.31)
  blocking collectives: 406 us -> 0 us
  Pallas kernels: 0 us -> 107 us
  waiting for transfers between devices: 93.4 us -> 0 us
  between operations: 15.5 us -> 2.15 us
  local copies, waits for them, and re-layouts: 22.8 us -> 31.9 us
    psum x1 -> x0, blocking collectives: 268 us -> none  [per_device(): lax.psum((self_part, nbr_part, bias_part), 'dom')]
    all_gather x2 -> x0, blocking collectives: 138 us -> none  [the longest x1 100 us: per_device(): sources = lax.all_gather(own_source, 'dom', axis=1, tiled=True)]
    pallas_call x0 -> x5, Pallas kernels: none -> 107 us  [exchange_many(): pl.pallas_call(functools.partial(exchange_kernel, tuple(specs)), out_shap...]
    reduce_scatter x2 -> x0, waiting for transfers between devices: 93.4 us -> none  [the longest x1 81.8 us: per_device(): lax.psum_scatter(partial_pre.astype(jnp.bfloat16), 'col', scatter_dimensi...]
  transfers between devices with their start and end apart: 2 -> 0, of which waited for: 2 -> 0; matrix products, arithmetic and copies ran while one was open for 0% -> 0% of each run, Pallas kernels for 0% -> 0%
where the time goes in v3:
time: 179 us; the launch traced here: 178 us
  Pallas kernels  107 us (60%)
  other arithmetic  33.5 us (19%)
  local copies, waits for them, and re-layouts  31.9 us (18%)
  matrix products  3.28 us (2%)
  between operations  2.15 us (1%)
    pallas_call x5, Pallas kernels, exchange_many(): pl.pallas_call(functools.partial(exchange_kernel, tuple(specs)), out_shap...  107 us
    scatter-add x1, other arithmetic, per_device(): contrib = jnp.zeros((col_width, total_rows), jnp.float32).at[:, neighbour...  26.1 us
    gather x1, local copies, waits for them, and re-layouts, per_device(): gathered = sources[:, neighbours].astype(jnp.float32)  13.8 us
    scatter-add x1, local copies, waits for them, and re-layouts, per_device(): contrib = jnp.zeros((col_width, total_rows), jnp.float32).at[:, neighbour...  5.38 us
    reshape x1, local copies, waits for them, and re-layouts, per_device(): sources = blocks.transpose(1, 0, 2).reshape(col_width, n_dom * part_rows)  4.5 us

profile of v3, /device:TPU:1, one launch (start us, length us, event | category | flops | bytes accessed | tf_op | source)
XLA Modules:
  0.0 177.6 jit_solution(16461715356638682535)
XLA Ops:
  0.6 0.7 compare_convert_fusion
  1.3 0.6 dynamic_slice.19
  2.5 1.3 dynamic-slice_select_fusion.refs_0_
  3.8 1.4 pad_maximum_fusion.refs_1_
  5.2 1.3 scatter.6.refs_2_
  6.5 42.6 %shard_map.137 = (bf16[64,16,256]{2,1,0:T(8,128)(2,1)}, bf16[8,80,256]{2,1,0:T(8,128)(2,1)}, f32[8,8,128]{2,1,0:T(8,128)}) custom-call(bf16[16,256]{1,0:T(8,128)(2,1)} %dynamic-slice_select_fusion.refs_0_, bf16[80,256]{1,0:T(8,128)(2,1)} %pad_maximum_fusion.refs_1_, f32[8,128]{1,0:T(8,128)} %scatter.6.refs_2_), custom_call_target="tpu_custom_call" | custom-call | tf_op jit(solution)/shard_map/pallas_call | solution.py:119
  49.1 0.9 slice.60
  50.0 1.2 dynamic_slice.18
  51.3 0.6 compare_convert_fusion.1
  51.9 0.8 slice_reduce_fusion
  52.8 4.5 %copy.26 = bf16[16,64,256]{0,2,1:T(8,128)(2,1)} copy(bf16[16,64,256]{2,0,1:T(8,128)(2,1)} %bitcast.62) | data formatting | bytes 1048576 | tf_op jit(solution)/shard_map/reshape | solution.py:166
  57.3 13.8 %gather_fusion = bf16[4096,16]{1,0:T(8,128)(2,1)S(1)} fusion(bf16[16,16384]{0,1:T(8,128)(2,1)} %bitcast.60, s32[4096]{0:T(1024)S(1)} %broadcast_clamp_fusion), kind=kCustom, calls=%fused_computation | custom fusion | bytes 278528 | tf_op jit(solution)/shard_map/gather | solution.py:177
  71.1 0.7 convert_divide_fusion
  71.8 0.7 fusion.2
  72.5 0.7 copy.23
  73.2 11.1 %shard_map.138 = bf16[8,16,256]{2,1,0:T(8,128)(2,1)} custom-call(bf16[16,256]{1,0:T(8,128)(2,1)} %bitcast.63), custom_call_target="tpu_custom_call" | custom-call | tf_op jit(solution)/shard_map/pallas_call | solution.py:119
  84.3 1.0 convolution_bitcast_fusion
  85.4 0.3 fusion.12
  85.7 0.7 convert_reduce_fusion
  86.5 0.1 fusion.9
  86.7 0.6 bitcast_multiply_fusion
  87.3 26.1 %scatter_custom_fusion = f32[16,16384]{0,1:T(8,128)} fusion(s32[4096]{0:T(1024)S(1)} %bitcast.68, f32[]{:T(128)} %constant.78.clone.1, f32[16,4096]{0,1:T(8,128)S(1)} %bitcast_multiply_fusion), kind=kCustom, calls=%fused_computation.2 | custom fusion | flops 65536 | bytes 3145732 | tf_op jit(solution)/shard_map/scatter-add | solution.py:217
  113.4 5.4 %copy.25.refs_0_ = bf16[16,16384]{1,0:T(8,128)(2,1)} copy(f32[16,16384]{0,1:T(8,128)} %scatter_custom_fusion) | data formatting | bytes 1572864 | tf_op jit(solution)/shard_map/scatter-add | solution.py:217
  118.8 24.0 %shard_map.139 = f32[16,256]{1,0:T(8,128)} custom-call(bf16[16,16384]{1,0:T(8,128)(2,1)} %copy.25.refs_0_), custom_call_target="tpu_custom_call" | custom-call | tf_op jit(solution)/shard_map/pallas_call | solution.py:119
  143.5 1.5 fusion.7
  144.9 0.1 fusion.22
  145.1 0.2 convolution_bitcast_fusion.3
  145.3 0.7 select_maximum_fusion.refs_0_
  145.9 11.9 %shard_map.140.refs_0_ = f32[40,256]{1,0:T(8,128)} custom-call(f32[40,256]{1,0:T(8,128)} %select_maximum_fusion.refs_0_), custom_call_target="tpu_custom_call" | custom-call | tf_op jit(solution)/shard_map/pallas_call | solution.py:119
  157.8 17.3 %shard_map.141 = f32[40,256]{1,0:T(8,128)} custom-call(f32[40,256]{1,0:T(8,128)} %shard_map.140.refs_0_), custom_call_target="tpu_custom_call" | custom-call | tf_op jit(solution)/shard_map/pallas_call | solution.py:119
  175.1 1.3 fusion.21
  176.4 1.2 slice_bitcast_fusion
  (23 shorter events, 0.3 us)
Async XLA Ops:
  52.8 4.5 %copy-start.2 = (s32[16,256]{1,0:T(8,128)S(1)}, s32[16,256]{1,0:T(8,128)}, u32[]{:S(2)}) copy-start(s32[16,256]{1,0:T(8,128)} %param.18) | copy-start | bytes 49156
  52.8 18.4 %copy-start.6 = (s32[256]{0:T(256)S(1)}, s32[256]{0:T(256)}, u32[]{:S(2)}) copy-start(s32[256]{0:T(256)} %param.19) | copy-start | bytes 3076
  57.3 27.0 %copy-start.3 = (bf16[8,80,256]{2,1,0:T(8,128)(2,1)S(1)}, bf16[8,80,256]{2,1,0:T(8,128)(2,1)}, u32[]{:S(2)}) copy-start(bf16[8,80,256]{2,1,0:T(8,128)(2,1)} %get-tuple-element.32) | copy-start | bytes 983044
  71.8 14.6 %copy-start.4 = (bf16[16,256]{1,0:T(8,128)(2,1)S(1)}, bf16[16,256]{1,0:T(8,128)(2,1)}, u32[]{:S(2)}) copy-start(bf16[16,256]{1,0:T(8,128)(2,1)} %param.21) | copy-start | bytes 24580
  113.4 30.0 %copy-start.5 = (bf16[16,256]{1,0:T(8,128)(2,1)S(1)}, bf16[16,256]{1,0:T(8,128)(2,1)}, u32[]{:S(2)}) copy-start(bf16[16,256]{1,0:T(8,128)(2,1)} %param.20) | copy-start | bytes 24580
  113.4 31.5 %copy-start.1 = (bf16[256,16]{0,1:T(8,128)(2,1)S(1)}, bf16[256,16]{0,1:T(8,128)(2,1)}, u32[]{:S(2)}) copy-start(bf16[256,16]{0,1:T(8,128)(2,1)} %copy.23) | copy-start | bytes 24580
  113.4 31.7 %copy-start = (bf16[16,256]{1,0:T(8,128)(2,1)S(1)}, bf16[16,256]{1,0:T(8,128)(2,1)}, u32[]{:S(2)}) copy-start(bf16[16,256]{1,0:T(8,128)(2,1)} %param.14) | copy-start | bytes 24580

commit v4 on v3

--- a/solution.py
+++ b/solution.py
@@ -155,20 +155,8 @@
     own_source = jnp.where(my_fresh == 1, features, own_cache)
     col_inputs = jnp.concatenate([features, w_self, w_nbr, cotangent], axis=0)
     bias_block = jnp.zeros((8, 128), jnp.float32).at[0, : sage_bias.shape[0]].set(sage_bias)
-    blocks, col_blocks, bias_blocks = exchange_many(
-        0,
-        [
-            (own_source, "dom", n_dom, 1, True, False, 0),
-            (col_inputs, "col", n_col, 1, True, False, 0),
-            (bias_block, "col", n_col, 1, True, False, 0),
-        ],
-    )
+    blocks = exchange(own_source, 0, "dom", n_dom, bcast=True)
     sources = blocks.transpose(1, 0, 2).reshape(col_width, n_dom * part_rows)
-    feat_full = col_blocks[:, :col_width].reshape(n_col * col_width, part_rows)
-    w_self_full = col_blocks[:, col_width : 2 * col_width].reshape(n_col * col_width, hidden)
-    w_nbr_full = col_blocks[:, 2 * col_width : 3 * col_width].reshape(n_col * col_width, hidden)
-    cot_full = col_blocks[:, 3 * col_width :].reshape(hidden, part_rows)
-    bias_full = bias_blocks[:, 0, : sage_bias.shape[0]].reshape(hidden)
     local_slot = jnp.arange(part_rows, dtype=jnp.int32)
     live_rows = (local_slot < node_counts[my_index]).astype(jnp.float32)
     slot_index = jnp.arange(slot_count, dtype=jnp.int32)
@@ -176,7 +164,20 @@
     weights = used * (live_rows / degrees.astype(jnp.float32))[None, :]
     gathered = sources[:, neighbours].astype(jnp.float32)
     aggregated = jnp.sum(weights[None, :, :] * gathered, axis=1).astype(jnp.bfloat16)
-    agg_full = exchange(aggregated, 1, "col", n_col, bcast=True).reshape(n_col * col_width, part_rows)
+    col_blocks, bias_blocks = exchange_many(
+        1,
+        [
+            (jnp.concatenate([aggregated, col_inputs], axis=0), "col", n_col, 1, True, False, 0),
+            (bias_block, "col", n_col, 1, True, False, 0),
+        ],
+    )
+    agg_full = col_blocks[:, :col_width].reshape(n_col * col_width, part_rows)
+    col_blocks = col_blocks[:, col_width:]
+    feat_full = col_blocks[:, :col_width].reshape(n_col * col_width, part_rows)
+    w_self_full = col_blocks[:, col_width : 2 * col_width].reshape(n_col * col_width, hidden)
+    w_nbr_full = col_blocks[:, 2 * col_width : 3 * col_width].reshape(n_col * col_width, hidden)
+    cot_full = col_blocks[:, 3 * col_width :].reshape(hidden, part_rows)
+    bias_full = bias_blocks[:, 0, : sage_bias.shape[0]].reshape(hidden)
     pre_full = (
         left_product(w_self_full, feat_full)
         + left_product(w_nbr_full, agg_full)
@@ -200,13 +201,6 @@
     bias_part = jnp.sum(grad_pre.astype(jnp.float32), axis=1)
     bias_rows = jnp.zeros((8, hidden), jnp.float32).at[0, : bias_part.shape[0]].set(bias_part)
     packed = jnp.concatenate([self_part, nbr_part, bias_rows], axis=0)
-    group = 8 if n_dom % 8 == 0 else n_dom
-    summed = exchange(packed, 3, "dom", group, bcast=True, reduce=True)
-    if group < n_dom:
-        summed = exchange(summed, 4, "dom", n_dom // group, stride=group, bcast=True, reduce=True)
-    grad_self = summed[:col_width]
-    grad_nbr = summed[col_width : 2 * col_width]
-    grad_bias = summed[2 * col_width, : bias_part.shape[0]]
     grad_agg = jnp.dot(w_nbr, grad_full, preferred_element_type=jnp.float32).astype(jnp.bfloat16)
     own_term = jnp.dot(w_self, grad_full, preferred_element_type=jnp.float32)
     spread = weights[None, :, :] * grad_agg.astype(jnp.float32)[:, None, :]
@@ -216,7 +210,19 @@
         .at[:, neighbours.reshape(-1)]
         .add(spread.reshape(col_width, -1))
     )
-    back = exchange(contrib.astype(jnp.bfloat16), 5, "dom", n_dom, reduce=True, lanes=part_rows)
+    group = 8 if n_dom % 8 == 0 else n_dom
+    back, summed = exchange_many(
+        5,
+        [
+            (contrib.astype(jnp.bfloat16), "dom", n_dom, 1, False, True, part_rows),
+            (packed, "dom", group, 1, True, True, 0),
+        ],
+    )
+    if group < n_dom:
+        summed = exchange(summed, 4, "dom", n_dom // group, stride=group, bcast=True, reduce=True)
+    grad_self = summed[:col_width]
+    grad_nbr = summed[col_width : 2 * col_width]
+    grad_bias = summed[2 * col_width, : bias_part.shape[0]]
     grad_feat = (own_term + my_fresh.astype(jnp.float32) * back).astype(jnp.bfloat16)
     return (activation, grad_feat, grad_self, grad_nbr, grad_bias)
 

time: 179 us -> 165 us (0.922)
  Pallas kernels: 107 us -> 93.7 us
  local copies, waits for them, and re-layouts: 31.9 us -> 29.9 us
    pallas_call x5 -> x4, Pallas kernels: 107 us -> 93.7 us  [exchange_many(): pl.pallas_call(functools.partial(exchange_kernel, tuple(specs)), out_shap...]
where the time goes in v4:
time: 165 us; the launch traced here: 162 us
  Pallas kernels  93.7 us (57%)
  other arithmetic  32.1 us (19%)
  local copies, waits for them, and re-layouts  29.9 us (18%)
  matrix products  4.19 us (3%)
  between operations  2.23 us (1%)
    pallas_call x4, Pallas kernels, exchange_many(): pl.pallas_call(functools.partial(exchange_kernel, tuple(specs)), out_shap...  93.7 us
    scatter-add x1, other arithmetic, per_device(): contrib = jnp.zeros((col_width, total_rows), jnp.float32).at[:, neighbour...  26.1 us
    gather x1, local copies, waits for them, and re-layouts, per_device(): gathered = sources[:, neighbours].astype(jnp.float32)  13.8 us
    scatter-add x1, local copies, waits for them, and re-layouts, per_device(): contrib = jnp.zeros((col_width, total_rows), jnp.float32).at[:, neighbour...  5.29 us
    reshape x1, local copies, waits for them, and re-layouts, per_device(): sources = blocks.transpose(1, 0, 2).reshape(col_width, n_dom * part_rows)  4.48 us

profile of v4, /device:TPU:1, one launch (start us, length us, event | category | flops | bytes accessed | tf_op | source)
XLA Modules:
  0.0 162.2 jit_solution(1256115179748282431)
XLA Ops:
  0.6 0.7 compare_convert_fusion
  1.3 0.6 dynamic_slice.19
  2.5 1.3 dynamic-slice_select_fusion.refs_0_
  3.9 29.2 %shard_map.137 = bf16[64,16,256]{2,1,0:T(8,128)(2,1)} custom-call(bf16[16,256]{1,0:T(8,128)(2,1)} %dynamic-slice_select_fusion.refs_0_), custom_call_target="tpu_custom_call" | custom-call | tf_op jit(solution)/shard_map/pallas_call | solution.py:119
  33.2 4.5 %copy.26 = bf16[16,64,256]{0,2,1:T(8,128)(2,1)} copy(bf16[16,64,256]{2,0,1:T(8,128)(2,1)} %bitcast.59) | data formatting | bytes 1048576 | tf_op jit(solution)/shard_map/reshape | solution.py:159
  37.7 13.8 %gather_fusion = bf16[4096,16]{1,0:T(8,128)(2,1)S(1)} fusion(bf16[16,16384]{0,1:T(8,128)(2,1)} %bitcast.58, s32[4096]{0:T(1024)S(1)} %broadcast_clamp_fusion), kind=kCustom, calls=%fused_computation | custom fusion | bytes 278528 | tf_op jit(solution)/shard_map/gather | solution.py:165
  51.5 0.6 dynamic_slice.18
  52.1 0.6 convert_divide_fusion
  52.8 0.7 fusion.2
  53.5 0.1 copy.23
  53.6 0.6 scatter.6.refs_1_
  54.2 17.9 %shard_map.138 = (bf16[8,96,256]{2,1,0:T(8,128)(2,1)}, f32[8,8,128]{2,1,0:T(8,128)}) custom-call(bf16[96,256]{1,0:T(8,128)(2,1)} %copy-done.1, f32[8,128]{1,0:T(8,128)} %scatter.6.refs_1_), custom_call_target="tpu_custom_call" | custom-call | tf_op jit(solution)/shard_map/pallas_call | solution.py:119
  72.2 0.9 slice.69
  73.1 0.7 compare_convert_fusion.1
  73.7 0.8 slice_reduce_fusion
  74.5 0.1 add.68
  74.6 1.1 convolution_bitcast_fusion
  75.7 1.2 fusion.12
  76.9 0.7 convert_reduce_fusion
  77.6 0.1 fusion.9
  77.8 0.1 copy.24
  77.9 0.6 bitcast_multiply_fusion
  78.5 26.1 %scatter_custom_fusion = f32[16,16384]{0,1:T(8,128)} fusion(s32[4096]{0:T(1024)S(1)} %bitcast.65, f32[]{:T(128)} %constant.74.clone.1, f32[16,4096]{0,1:T(8,128)S(1)} %bitcast_multiply_fusion), kind=kCustom, calls=%fused_computation.2 | custom fusion | flops 65536 | bytes 3145732 | tf_op jit(solution)/shard_map/scatter-add | solution.py:211
  104.6 5.3 %copy.25.refs_0_ = bf16[16,16384]{1,0:T(8,128)(2,1)} copy(f32[16,16384]{0,1:T(8,128)} %scatter_custom_fusion) | data formatting | bytes 1572864 | tf_op jit(solution)/shard_map/scatter-add | solution.py:211
  109.9 0.1 fusion.23
  110.1 0.2 convolution_bitcast_fusion.3
  110.3 0.7 select_maximum_fusion.refs_1_
  110.9 32.1 %shard_map.139 = (f32[16,256]{1,0:T(8,128)}, f32[40,256]{1,0:T(8,128)}) custom-call(bf16[16,16384]{1,0:T(8,128)(2,1)} %copy.25.refs_0_, f32[40,256]{1,0:T(8,128)} %select_maximum_fusion.refs_1_), custom_call_target="tpu_custom_call" | custom-call | tf_op jit(solution)/shard_map/pallas_call | solution.py:119
  143.7 1.5 fusion.7
  145.2 14.4 %shard_map.140 = f32[40,256]{1,0:T(8,128)} custom-call(f32[40,256]{1,0:T(8,128)} %get-tuple-element.36.refs_0_), custom_call_target="tpu_custom_call" | custom-call | tf_op jit(solution)/shard_map/pallas_call | solution.py:119
  159.6 1.3 fusion.22
  161.0 1.2 slice_bitcast_fusion
  (30 shorter events, 0.1 us)
Async XLA Ops:
  33.1 4.5 %copy-start.2 = (s32[16,256]{1,0:T(8,128)S(1)}, s32[16,256]{1,0:T(8,128)}, u32[]{:S(2)}) copy-start(s32[16,256]{1,0:T(8,128)} %param.18) | copy-start | bytes 49156
  33.1 18.4 %copy-start.8 = (s32[64]{0:T(128)S(1)}, s32[64]{0:T(128)}, u32[]{:S(2)}) copy-start(s32[64]{0:T(128)} %param.17) | copy-start | bytes 772
  33.1 18.9 %copy-start.6 = (s32[256]{0:T(256)S(1)}, s32[256]{0:T(256)}, u32[]{:S(2)}) copy-start(s32[256]{0:T(256)} %param.19) | copy-start | bytes 3076
  37.6 15.9 %copy-start = (bf16[16,256]{1,0:T(8,128)(2,1)S(1)}, bf16[16,256]{1,0:T(8,128)(2,1)}, u32[]{:S(2)}) copy-start(bf16[16,256]{1,0:T(8,128)(2,1)} %param.14) | copy-start | bytes 24580
  37.6 15.9 %copy-start.4 = (bf16[16,256]{1,0:T(8,128)(2,1)S(1)}, bf16[16,256]{1,0:T(8,128)(2,1)}, u32[]{:S(2)}) copy-start(bf16[16,256]{1,0:T(8,128)(2,1)} %param.20) | copy-start | bytes 24580
  37.6 16.0 %copy-start.3 = (bf16[16,256]{1,0:T(8,128)(2,1)S(1)}, bf16[16,256]{1,0:T(8,128)(2,1)}, u32[]{:S(2)}) copy-start(bf16[16,256]{1,0:T(8,128)(2,1)} %param.21) | copy-start | bytes 24580
  37.6 16.0 %copy-start.5 = (bf16[32,256]{1,0:T(8,128)(2,1)S(1)}, bf16[32,256]{1,0:T(8,128)(2,1)}, u32[]{:S(2)}) copy-start(bf16[32,256]{1,0:T(8,128)(2,1)} %param.23) | copy-start | bytes 49156
  37.6 16.0 %copy-start.7 = (f32[32]{0:T(128)S(1)}, f32[32]{0:T(128)}, u32[]{:S(2)}) copy-start(f32[32]{0:T(128)} %param.22) | copy-start | bytes 388
  53.6 0.6 copy-start.1

commit v5 on v4

--- a/solution.py
+++ b/solution.py
@@ -128,6 +128,17 @@
 
 def exchange(x, ident, axis, size, stride=1, bcast=False, reduce=False, lanes=0):
     return exchange_many(ident, [(x, axis, size, stride, bcast, reduce, lanes)])[0]
+
+
+def group_sum(x, axis, n, size, stride):
+    total = x
+    for k in range(1, size):
+        pairs = []
+        for d in range(n):
+            pos = (d // stride) % size
+            pairs.append((d, d + ((pos + k) % size - pos) * stride))
+        total = total + lax.ppermute(x, axis, pairs)
+    return total
 
 
 def per_device(
@@ -211,15 +222,11 @@
         .add(spread.reshape(col_width, -1))
     )
     group = 8 if n_dom % 8 == 0 else n_dom
-    back, summed = exchange_many(
-        5,
-        [
-            (contrib.astype(jnp.bfloat16), "dom", n_dom, 1, False, True, part_rows),
-            (packed, "dom", group, 1, True, True, 0),
-        ],
-    )
+    summed = group_sum(packed, "dom", n_dom, group, 1)
+    contrib_low, summed = lax.optimization_barrier((contrib.astype(jnp.bfloat16), summed))
+    back = exchange(contrib_low, 5, "dom", n_dom, reduce=True, lanes=part_rows)
     if group < n_dom:
-        summed = exchange(summed, 4, "dom", n_dom // group, stride=group, bcast=True, reduce=True)
+        summed = group_sum(summed, "dom", n_dom, n_dom // group, group)
     grad_self = summed[:col_width]
     grad_nbr = summed[col_width : 2 * col_width]
     grad_bias = summed[2 * col_width, : bias_part.shape[0]]

time: 165 us -> 199 us (1.21)
  starting transfers between devices: 0 us -> 52.7 us
  Pallas kernels: 93.7 us -> 72.9 us
  waiting for transfers between devices: 0 us -> 5.69 us
    ppermute x0 -> x14, starting transfers between devices: none -> 52.7 us  [group_sum(): total = total + lax.ppermute(x, axis, pairs)]
    pallas_call x4 -> x3, Pallas kernels: 93.7 us -> 72.9 us  [exchange_many(): pl.pallas_call(functools.partial(exchange_kernel, tuple(specs)), out_shap...]
    ppermute x0 -> x14, waiting for transfers between devices: none -> 5.69 us  [group_sum(): total = total + lax.ppermute(x, axis, pairs)]
  transfers between devices with their start and end apart: 0 -> 14, of which waited for: 0 -> 1; matrix products, arithmetic and copies ran while one was open for 0% -> 17% of each run, Pallas kernels for 0% -> 13%
where the time goes in v5:
time: 199 us; the launch traced here: 198 us
  Pallas kernels  72.9 us (37%)
  starting transfers between devices  52.7 us (26%)
  other arithmetic  31.5 us (16%)
  local copies, waits for them, and re-layouts  28.5 us (14%)
  waiting for transfers between devices  5.69 us (3%)
  matrix products  4.19 us (2%)
  between operations  2.43 us (1%)
    pallas_call x3, Pallas kernels, exchange_many(): pl.pallas_call(functools.partial(exchange_kernel, tuple(specs)), out_shap...  72.9 us
    ppermute x14, starting transfers between devices, group_sum(): total = total + lax.ppermute(x, axis, pairs)  52.7 us
    scatter-add x1, other arithmetic, per_device(): contrib = jnp.zeros((col_width, total_rows), jnp.float32).at[:, neighbour...  26.1 us
    gather x1, local copies, waits for them, and re-layouts, per_device(): gathered = sources[:, neighbours].astype(jnp.float32)  13.7 us
    ppermute x14, waiting for transfers between devices, group_sum(): total = total + lax.ppermute(x, axis, pairs)  5.69 us
    scatter-add x1, local copies, waits for them, and re-layouts, per_device(): contrib = jnp.zeros((col_width, total_rows), jnp.float32).at[:, neighbour...  5.3 us
    reshape x1, local copies, waits for them, and re-layouts, per_device(): sources = blocks.transpose(1, 0, 2).reshape(col_width, n_dom * part_rows)  4.5 us
  transfers between devices with their start and end apart: 14, of which 1 were waited for; matrix products, arithmetic and copies ran while one was open for 17% of the time, Pallas kernels for 13%

profile of v5, /device:TPU:1, one launch (start us, length us, event | category | flops | bytes accessed | tf_op | source)
XLA Modules:
  0.0 198.0 jit_solution(9517874880639998056)
XLA Ops:
  0.6 0.7 compare_convert_fusion
  2.5 1.3 dynamic-slice_select_fusion.refs_0_
  3.8 29.2 %shard_map.137 = bf16[64,16,256]{2,1,0:T(8,128)(2,1)} custom-call(bf16[16,256]{1,0:T(8,128)(2,1)} %dynamic-slice_select_fusion.refs_0_), custom_call_target="tpu_custom_call" | custom-call | tf_op jit(solution)/shard_map/pallas_call | solution.py:119
  33.1 4.5 %copy.26 = bf16[16,64,256]{0,2,1:T(8,128)(2,1)} copy(bf16[16,64,256]{2,0,1:T(8,128)(2,1)} %bitcast.59) | data formatting | bytes 1048576 | tf_op jit(solution)/shard_map/reshape | solution.py:170
  38.3 0.6 compare_convert_fusion.1
  39.0 0.7 convert_divide_fusion
  39.7 13.7 %gather_fusion = bf16[4096,16]{1,0:T(8,128)(2,1)S(1)} fusion(bf16[16,16384]{0,1:T(8,128)(2,1)} %bitcast.58, s32[4096]{0:T(1024)S(1)} %broadcast_clamp_fusion), kind=kCustom, calls=%fused_computation | custom fusion | bytes 278528 | tf_op jit(solution)/shard_map/gather | solution.py:176
  53.4 0.7 fusion.2
  54.9 17.9 %shard_map.138 = (bf16[8,96,256]{2,1,0:T(8,128)(2,1)}, f32[8,8,128]{2,1,0:T(8,128)}) custom-call(bf16[96,256]{1,0:T(8,128)(2,1)} %copy-done.1, f32[8,128]{1,0:T(8,128)} %scatter.6.refs_1_), custom_call_target="tpu_custom_call" | custom-call | tf_op jit(solution)/shard_map/pallas_call | solution.py:119
  72.8 0.9 slice.69
  73.7 1.1 convolution_bitcast_fusion
  74.8 0.8 slice_reduce_fusion
  75.7 1.2 fusion.12
  77.4 3.7 %collective-permute-start.6 = (f32[40,256]{1,0:T(8,128)S(1)}, f32[40,256]{1,0:T(8,128)S(1)}, u32[]{:S(2)}, u32[]{:S(2)}) collective-permute-start(f32[40,256]{1,0:T(8,128)S(1)} %select_maximum_fusion), channel_id=1, source_target_pairs={{0,56},{8,0},{16,8},{24,16},{32,24},{40,32},{48,40},{56,48},{64,12... | collective-permute-start | bytes 122888 | tf_op jit(solution)/shard_map/ppermute | solution.py:140
  81.1 3.0 %collective-permute-start.5 = (f32[40,256]{1,0:T(8,128)S(1)}, f32[40,256]{1,0:T(8,128)S(1)}, u32[]{:S(2)}, u32[]{:S(2)}) collective-permute-start(f32[40,256]{1,0:T(8,128)S(1)} %select_maximum_fusion), channel_id=1, source_target_pairs={{0,48},{8,56},{16,0},{24,8},{32,16},{40,24},{48,32},{56,40},{64,11... | collective-permute-start | bytes 122888 | tf_op jit(solution)/shard_map/ppermute | solution.py:140
  84.1 4.0 %collective-permute-start.4 = (f32[40,256]{1,0:T(8,128)S(1)}, f32[40,256]{1,0:T(8,128)S(1)}, u32[]{:S(2)}, u32[]{:S(2)}) collective-permute-start(f32[40,256]{1,0:T(8,128)S(1)} %select_maximum_fusion), channel_id=1, source_target_pairs={{0,40},{8,48},{16,56},{24,0},{32,8},{40,16},{48,24},{56,32},{64,10... | collective-permute-start | bytes 122888 | tf_op jit(solution)/shard_map/ppermute | solution.py:140
  88.1 1.9 collective-permute-start.3
  90.0 3.5 %collective-permute-start.2 = (f32[40,256]{1,0:T(8,128)S(1)}, f32[40,256]{1,0:T(8,128)S(1)}, u32[]{:S(2)}, u32[]{:S(2)}) collective-permute-start(f32[40,256]{1,0:T(8,128)S(1)} %select_maximum_fusion), channel_id=1, source_target_pairs={{0,24},{8,32},{16,40},{24,48},{32,56},{40,0},{48,8},{56,16},{64,88... | collective-permute-start | bytes 122888 | tf_op jit(solution)/shard_map/ppermute | solution.py:140
  93.6 3.3 %collective-permute-start.1 = (f32[40,256]{1,0:T(8,128)S(1)}, f32[40,256]{1,0:T(8,128)S(1)}, u32[]{:S(2)}, u32[]{:S(2)}) collective-permute-start(f32[40,256]{1,0:T(8,128)S(1)} %select_maximum_fusion), channel_id=1, source_target_pairs={{0,16},{8,24},{16,32},{24,40},{32,48},{40,56},{48,0},{56,8},{64,80... | collective-permute-start | bytes 122888 | tf_op jit(solution)/shard_map/ppermute | solution.py:140
  97.0 2.0 %collective-permute-start = (f32[40,256]{1,0:T(8,128)S(1)}, f32[40,256]{1,0:T(8,128)S(1)}, u32[]{:S(2)}, u32[]{:S(2)}) collective-permute-start(f32[40,256]{1,0:T(8,128)S(1)} %select_maximum_fusion), channel_id=1, source_target_pairs={{0,8},{8,16},{16,24},{24,32},{32,40},{40,48},{48,56},{56,0},{64,72... | collective-permute-start | bytes 122888 | tf_op jit(solution)/shard_map/ppermute | solution.py:140
  99.9 26.1 %scatter_custom_fusion = f32[16,16384]{0,1:T(8,128)} fusion(s32[4096]{0:T(1024)S(1)} %bitcast.65, f32[]{:T(128)} %constant.74.clone.1, f32[16,4096]{0,1:T(8,128)S(1)} %bitcast_multiply_fusion), kind=kCustom, calls=%fused_computation.2 | custom fusion | flops 65536 | bytes 3145732 | tf_op jit(solution)/shard_map/scatter-add | solution.py:222
  126.0 5.3 %copy.25.refs_0_ = bf16[16,16384]{1,0:T(8,128)(2,1)} copy(f32[16,16384]{0,1:T(8,128)} %scatter_custom_fusion) | data formatting | bytes 1572864 | tf_op jit(solution)/shard_map/scatter-add | solution.py:222
  131.3 9.0 %collective-permute-start.13 = (f32[40,256]{1,0:T(8,128)S(1)}, f32[40,256]{1,0:T(8,128)S(1)}, u32[]{:S(2)}, u32[]{:S(2)}) collective-permute-start(f32[40,256]{1,0:T(8,128)S(1)} %add_add_fusion.1), channel_id=1, source_target_pairs={{0,448},{8,456},{16,464},{24,472},{32,480},{40,488},{48,496},{56,5... | collective-permute-start | bytes 122888 | tf_op jit(solution)/shard_map/ppermute | solution.py:140
  140.3 3.4 %collective-permute-start.12 = (f32[40,256]{1,0:T(8,128)S(1)}, f32[40,256]{1,0:T(8,128)S(1)}, u32[]{:S(2)}, u32[]{:S(2)}) collective-permute-start(f32[40,256]{1,0:T(8,128)S(1)} %add_add_fusion.1), channel_id=1, source_target_pairs={{0,384},{8,392},{16,400},{24,408},{32,416},{40,424},{48,432},{56,4... | collective-permute-start | bytes 122888 | tf_op jit(solution)/shard_map/ppermute | solution.py:140
  145.0 3.6 %collective-permute-start.11 = (f32[40,256]{1,0:T(8,128)S(1)}, f32[40,256]{1,0:T(8,128)S(1)}, u32[]{:S(2)}, u32[]{:S(2)}) collective-permute-start(f32[40,256]{1,0:T(8,128)S(1)} %add_add_fusion.1), channel_id=1, source_target_pairs={{0,320},{8,328},{16,336},{24,344},{32,352},{40,360},{48,368},{56,3... | collective-permute-start | bytes 122888 | tf_op jit(solution)/shard_map/ppermute | solution.py:140
  148.6 3.3 %collective-permute-start.10 = (f32[40,256]{1,0:T(8,128)S(1)}, f32[40,256]{1,0:T(8,128)S(1)}, u32[]{:S(2)}, u32[]{:S(2)}) collective-permute-start(f32[40,256]{1,0:T(8,128)S(1)} %add_add_fusion.1), channel_id=1, source_target_pairs={{0,256},{8,264},{16,272},{24,280},{32,288},{40,296},{48,304},{56,3... | collective-permute-start | bytes 122888 | tf_op jit(solution)/shard_map/ppermute | solution.py:140
  151.9 5.2 %collective-permute-start.9 = (f32[40,256]{1,0:T(8,128)S(1)}, f32[40,256]{1,0:T(8,128)S(1)}, u32[]{:S(2)}, u32[]{:S(2)}) collective-permute-start(f32[40,256]{1,0:T(8,128)S(1)} %add_add_fusion.1), channel_id=1, source_target_pairs={{0,192},{8,200},{16,208},{24,216},{32,224},{40,232},{48,240},{56,2... | collective-permute-start | bytes 122888 | tf_op jit(solution)/shard_map/ppermute | solution.py:140
  157.1 25.8 %shard_map.139 = f32[16,256]{1,0:T(8,128)} custom-call(bf16[16,16384]{1,0:T(8,128)(2,1)} %copy.25.refs_0_), custom_call_target="tpu_custom_call" | custom-call | tf_op jit(solution)/shard_map/pallas_call | solution.py:119
  182.9 2.5 %collective-permute-start.8 = (f32[40,256]{1,0:T(8,128)S(1)}, f32[40,256]{1,0:T(8,128)S(1)}, u32[]{:S(2)}, u32[]{:S(2)}) collective-permute-start(f32[40,256]{1,0:T(8,128)S(1)} %add_add_fusion.1), channel_id=1, source_target_pairs={{0,128},{8,136},{16,144},{24,152},{32,160},{40,168},{48,176},{56,1... | collective-permute-start | bytes 122888 | tf_op jit(solution)/shard_map/ppermute | solution.py:140
  185.4 4.3 %collective-permute-start.7 = (f32[40,256]{1,0:T(8,128)S(1)}, f32[40,256]{1,0:T(8,128)S(1)}, u32[]{:S(2)}, u32[]{:S(2)}) collective-permute-start(f32[40,256]{1,0:T(8,128)S(1)} %add_add_fusion.1), channel_id=1, source_target_pairs={{0,64},{8,72},{16,80},{24,88},{32,96},{40,104},{48,112},{56,120},{... | collective-permute-start | bytes 122888 | tf_op jit(solution)/shard_map/ppermute | solution.py:140
  189.7 1.5 fusion.7
  191.2 5.7 %collective-permute-done.7 = f32[40,256]{1,0:T(8,128)S(1)} collective-permute-done((f32[40,256]{1,0:T(8,128)S(1)}, f32[40,256]{1,0:T(8,128)S(1)}, u32[]{:S(2)}, u32[]{:S(2)}) %collective-permute-start.7) | collective-permute-done | bytes 40992 | tf_op jit(solution)/shard_map/ppermute | solution.py:140
  (60 shorter events, 5.2 us)
Async XLA Ops:
  33.1 4.5 %copy-start.2 = (s32[16,256]{1,0:T(8,128)S(1)}, s32[16,256]{1,0:T(8,128)}, u32[]{:S(2)}) copy-start(s32[16,256]{1,0:T(8,128)} %param.18) | copy-start | bytes 49156
  33.1 4.6 %copy-start.8 = (s32[64]{0:T(128)S(1)}, s32[64]{0:T(128)}, u32[]{:S(2)}) copy-start(s32[64]{0:T(128)} %param.17) | copy-start | bytes 772
  33.1 5.9 %copy-start.6 = (s32[256]{0:T(256)S(1)}, s32[256]{0:T(256)}, u32[]{:S(2)}) copy-start(s32[256]{0:T(256)} %param.19) | copy-start | bytes 3076
  37.6 16.6 %copy-start = (bf16[16,256]{1,0:T(8,128)(2,1)S(1)}, bf16[16,256]{1,0:T(8,128)(2,1)}, u32[]{:S(2)}) copy-start(bf16[16,256]{1,0:T(8,128)(2,1)} %param.14) | copy-start | bytes 24580
  37.6 16.6 %copy-start.4 = (bf16[16,256]{1,0:T(8,128)(2,1)S(1)}, bf16[16,256]{1,0:T(8,128)(2,1)}, u32[]{:S(2)}) copy-start(bf16[16,256]{1,0:T(8,128)(2,1)} %param.20) | copy-start | bytes 24580
  37.6 16.6 %copy-start.3 = (bf16[16,256]{1,0:T(8,128)(2,1)S(1)}, bf16[16,256]{1,0:T(8,128)(2,1)}, u32[]{:S(2)}) copy-start(bf16[16,256]{1,0:T(8,128)(2,1)} %param.21) | copy-start | bytes 24580
  37.7 16.6 %copy-start.5 = (bf16[32,256]{1,0:T(8,128)(2,1)S(1)}, bf16[32,256]{1,0:T(8,128)(2,1)}, u32[]{:S(2)}) copy-start(bf16[32,256]{1,0:T(8,128)(2,1)} %param.23) | copy-start | bytes 49156
  37.7 16.6 %copy-start.7 = (f32[32]{0:T(128)S(1)}, f32[32]{0:T(128)}, u32[]{:S(2)}) copy-start(f32[32]{0:T(128)} %param.22) | copy-start | bytes 388
  54.3 0.6 copy-start.1
  77.4 16.3 %collective-permute-start.6 = (f32[40,256]{1,0:T(8,128)S(1)}, f32[40,256]{1,0:T(8,128)S(1)}, u32[]{:S(2)}, u32[]{:S(2)}) collective-permute-start(f32[40,256]{1,0:T(8,128)S(1)} %select_maximum_fusion), channel_id=1, source_target_pairs={{0,56},{8,0},{16,8},{24,16},{32,24},{40,32},{48,40},{56,48},{64,12... | collective-permute-start | bytes 122888 | tf_op jit(solution)/shard_map/ppermute | solution.py:140
  81.1 15.9 %collective-permute-start.5 = (f32[40,256]{1,0:T(8,128)S(1)}, f32[40,256]{1,0:T(8,128)S(1)}, u32[]{:S(2)}, u32[]{:S(2)}) collective-permute-start(f32[40,256]{1,0:T(8,128)S(1)} %select_maximum_fusion), channel_id=1, source_target_pairs={{0,48},{8,56},{16,0},{24,8},{32,16},{40,24},{48,32},{56,40},{64,11... | collective-permute-start | bytes 122888 | tf_op jit(solution)/shard_map/ppermute | solution.py:140
  84.1 47.2 %collective-permute-start.4 = (f32[40,256]{1,0:T(8,128)S(1)}, f32[40,256]{1,0:T(8,128)S(1)}, u32[]{:S(2)}, u32[]{:S(2)}) collective-permute-start(f32[40,256]{1,0:T(8,128)S(1)} %select_maximum_fusion), channel_id=1, source_target_pairs={{0,40},{8,48},{16,56},{24,0},{32,8},{40,16},{48,24},{56,32},{64,10... | collective-permute-start | bytes 122888 | tf_op jit(solution)/shard_map/ppermute | solution.py:140
  88.1 43.2 %collective-permute-start.3 = (f32[40,256]{1,0:T(8,128)S(1)}, f32[40,256]{1,0:T(8,128)S(1)}, u32[]{:S(2)}, u32[]{:S(2)}) collective-permute-start(f32[40,256]{1,0:T(8,128)S(1)} %select_maximum_fusion), channel_id=1, source_target_pairs={{0,32},{8,40},{16,48},{24,56},{32,0},{40,8},{48,16},{56,24},{64,96... | collective-permute-start | bytes 122888 | tf_op jit(solution)/shard_map/ppermute | solution.py:140
  90.0 41.2 %collective-permute-start.2 = (f32[40,256]{1,0:T(8,128)S(1)}, f32[40,256]{1,0:T(8,128)S(1)}, u32[]{:S(2)}, u32[]{:S(2)}) collective-permute-start(f32[40,256]{1,0:T(8,128)S(1)} %select_maximum_fusion), channel_id=1, source_target_pairs={{0,24},{8,32},{16,40},{24,48},{32,56},{40,0},{48,8},{56,16},{64,88... | collective-permute-start | bytes 122888 | tf_op jit(solution)/shard_map/ppermute | solution.py:140
  93.6 37.7 %collective-permute-start.1 = (f32[40,256]{1,0:T(8,128)S(1)}, f32[40,256]{1,0:T(8,128)S(1)}, u32[]{:S(2)}, u32[]{:S(2)}) collective-permute-start(f32[40,256]{1,0:T(8,128)S(1)} %select_maximum_fusion), channel_id=1, source_target_pairs={{0,16},{8,24},{16,32},{24,40},{32,48},{40,56},{48,0},{56,8},{64,80... | collective-permute-start | bytes 122888 | tf_op jit(solution)/shard_map/ppermute | solution.py:140
  97.0 34.3 %collective-permute-start = (f32[40,256]{1,0:T(8,128)S(1)}, f32[40,256]{1,0:T(8,128)S(1)}, u32[]{:S(2)}, u32[]{:S(2)}) collective-permute-start(f32[40,256]{1,0:T(8,128)S(1)} %select_maximum_fusion), channel_id=1, source_target_pairs={{0,8},{8,16},{16,24},{24,32},{32,40},{40,48},{48,56},{56,0},{64,72... | collective-permute-start | bytes 122888 | tf_op jit(solution)/shard_map/ppermute | solution.py:140
  131.3 51.5 %collective-permute-start.13 = (f32[40,256]{1,0:T(8,128)S(1)}, f32[40,256]{1,0:T(8,128)S(1)}, u32[]{:S(2)}, u32[]{:S(2)}) collective-permute-start(f32[40,256]{1,0:T(8,128)S(1)} %add_add_fusion.1), channel_id=1, source_target_pairs={{0,448},{8,456},{16,464},{24,472},{32,480},{40,488},{48,496},{56,5... | collective-permute-start | bytes 122888 | tf_op jit(solution)/shard_map/ppermute | solution.py:140
  140.3 45.0 %collective-permute-start.12 = (f32[40,256]{1,0:T(8,128)S(1)}, f32[40,256]{1,0:T(8,128)S(1)}, u32[]{:S(2)}, u32[]{:S(2)}) collective-permute-start(f32[40,256]{1,0:T(8,128)S(1)} %add_add_fusion.1), channel_id=1, source_target_pairs={{0,384},{8,392},{16,400},{24,408},{32,416},{40,424},{48,432},{56,4... | collective-permute-start | bytes 122888 | tf_op jit(solution)/shard_map/ppermute | solution.py:140
  145.0 46.1 %collective-permute-start.11 = (f32[40,256]{1,0:T(8,128)S(1)}, f32[40,256]{1,0:T(8,128)S(1)}, u32[]{:S(2)}, u32[]{:S(2)}) collective-permute-start(f32[40,256]{1,0:T(8,128)S(1)} %add_add_fusion.1), channel_id=1, source_target_pairs={{0,320},{8,328},{16,336},{24,344},{32,352},{40,360},{48,368},{56,3... | collective-permute-start | bytes 122888 | tf_op jit(solution)/shard_map/ppermute | solution.py:140
  148.6 42.6 %collective-permute-start.10 = (f32[40,256]{1,0:T(8,128)S(1)}, f32[40,256]{1,0:T(8,128)S(1)}, u32[]{:S(2)}, u32[]{:S(2)}) collective-permute-start(f32[40,256]{1,0:T(8,128)S(1)} %add_add_fusion.1), channel_id=1, source_target_pairs={{0,256},{8,264},{16,272},{24,280},{32,288},{40,296},{48,304},{56,3... | collective-permute-start | bytes 122888 | tf_op jit(solution)/shard_map/ppermute | solution.py:140
  151.9 39.2 %collective-permute-start.9 = (f32[40,256]{1,0:T(8,128)S(1)}, f32[40,256]{1,0:T(8,128)S(1)}, u32[]{:S(2)}, u32[]{:S(2)}) collective-permute-start(f32[40,256]{1,0:T(8,128)S(1)} %add_add_fusion.1), channel_id=1, source_target_pairs={{0,192},{8,200},{16,208},{24,216},{32,224},{40,232},{48,240},{56,2... | collective-permute-start | bytes 122888 | tf_op jit(solution)/shard_map/ppermute | solution.py:140
  182.9 8.3 %collective-permute-start.8 = (f32[40,256]{1,0:T(8,128)S(1)}, f32[40,256]{1,0:T(8,128)S(1)}, u32[]{:S(2)}, u32[]{:S(2)}) collective-permute-start(f32[40,256]{1,0:T(8,128)S(1)} %add_add_fusion.1), channel_id=1, source_target_pairs={{0,128},{8,136},{16,144},{24,152},{32,160},{40,168},{48,176},{56,1... | collective-permute-start | bytes 122888 | tf_op jit(solution)/shard_map/ppermute | solution.py:140
  185.4 11.4 %collective-permute-start.7 = (f32[40,256]{1,0:T(8,128)S(1)}, f32[40,256]{1,0:T(8,128)S(1)}, u32[]{:S(2)}, u32[]{:S(2)}) collective-permute-start(f32[40,256]{1,0:T(8,128)S(1)} %add_add_fusion.1), channel_id=1, source_target_pairs={{0,64},{8,72},{16,80},{24,88},{32,96},{40,104},{48,112},{56,120},{... | collective-permute-start | bytes 122888 | tf_op jit(solution)/shard_map/ppermute | solution.py:140

commit v6 on v4

--- a/solution.py
+++ b/solution.py
@@ -29,7 +29,8 @@
     scratch = refs[2 * count :]
     barrier = pltpu.get_barrier_semaphore()
     plans = []
-    for e, (axis, size, stride, bcast, reduce, lanes) in enumerate(specs):
+    extra = scratch[3 * count :]
+    for e, (axis, size, stride, bcast, reduce, lanes, _, _) in enumerate(specs):
         x_ref, y_ref = xs[e], ys[e]
         buf, send_sem, recv_sem = scratch[3 * e : 3 * e + 3]
         me = lax.axis_index(axis)
@@ -68,8 +69,16 @@
 
         lax.fori_loop(1, size, step, 0)
 
+    seconds = []
+    for e, spec in enumerate(specs):
+        if spec[6] > 1:
+            stage, buf2, send2, recv2 = extra[4 * len(seconds) : 4 * len(seconds) + 4]
+            me = plans[e][11]
+            second = (spec[0], spec[6], spec[7], True, True, 0, stage, None, buf2, send2, recv2, me,
+                      lax.rem(me // spec[7], spec[6]))
+            seconds.append((e, second))
     greetings = 0
-    for plan in plans:
+    for plan in plans + [second for _, second in seconds]:
         each_peer(
             plan,
             lambda j, plan=plan: pl.semaphore_signal(
@@ -83,15 +92,49 @@
     for plan in plans:
         buf, pos = plan[8], plan[12]
         buf[pos] = chunk(plan, pos)[...]
-    for plan in plans:
-
-        def finish(j, plan=plan):
+    for e, second in seconds:
+        plan = plans[e]
+
+        def finish_first(j, plan=plan):
             desc(plan, j, plan[12]).wait_send()
             desc(plan, j, j).wait_recv()
 
-        each_peer(plan, finish)
-    for plan in plans:
+        each_peer(plan, finish_first)
+        second[6][...] = jnp.sum(plan[8][...].astype(jnp.float32), axis=0)
+    for e, plan in enumerate(plans):
+        if specs[e][6] > 1:
+            continue
+        for k in range(1, min(plan[1], 9)):
+            desc(plan, lax.rem(plan[12] + k, plan[1]), plan[12]).wait_send()
+    for _, second in seconds:
+        each_peer(second, lambda j, second=second: desc(second, j, second[12]).start())
+        second[8][second[12]] = second[6][...]
+    for e, plan in enumerate(plans):
+        if specs[e][6] > 1:
+            continue
+
+        def finish(k, carry, plan=plan):
+            j = lax.rem(plan[12] + k, plan[1])
+            desc(plan, j, plan[12]).wait_send()
+            return carry
+
+        lax.fori_loop(min(plan[1], 9), plan[1], finish, 0)
+
+        def arrive(j, plan=plan):
+            desc(plan, j, j).wait_recv()
+
+        each_peer(plan, arrive)
+    for _, second in seconds:
+
+        def finish_second(j, second=second):
+            desc(second, j, second[12]).wait_send()
+            desc(second, j, j).wait_recv()
+
+        each_peer(second, finish_second)
+    for e, plan in enumerate(plans):
         reduce, y_ref, buf = plan[4], plan[7], plan[8]
+        if specs[e][6] > 1:
+            buf = dict(seconds)[e][8]
         if reduce:
             y_ref[...] = jnp.sum(buf[...].astype(jnp.float32), axis=0)
         else:
@@ -99,15 +142,24 @@
 
 
 def exchange_many(ident, jobs):
-    specs, out_shapes, scratch = [], [], []
-    for x, axis, size, stride, bcast, reduce, lanes in jobs:
+    specs, out_shapes, scratch, extra = [], [], [], []
+    for job in jobs:
+        x, axis, size, stride, bcast, reduce, lanes = job[:7]
+        size2, stride2 = job[7:] if len(job) > 7 else (1, 1)
         if bcast:
             block = x.shape
         elif lanes:
             block = (x.shape[0], lanes)
         else:
             block = x.shape[1:]
-        specs.append((axis, size, stride, bcast, reduce, lanes))
+        specs.append((axis, size, stride, bcast, reduce, lanes, size2, stride2))
+        if size2 > 1:
+            extra += [
+                pltpu.VMEM(block, jnp.float32),
+                pltpu.VMEM((size2,) + block, jnp.float32),
+                pltpu.SemaphoreType.DMA((size2,)),
+                pltpu.SemaphoreType.DMA((size2,)),
+            ]
         out_shapes.append(
             jax.ShapeDtypeStruct(block if reduce else (size,) + block, jnp.float32 if reduce else x.dtype)
         )
@@ -121,7 +173,7 @@
         out_shape=tuple(out_shapes),
         in_specs=[pl.BlockSpec(memory_space=pltpu.VMEM)] * len(jobs),
         out_specs=tuple(pl.BlockSpec(memory_space=pltpu.VMEM) for _ in jobs),
-        scratch_shapes=scratch,
+        scratch_shapes=scratch + extra,
         compiler_params=pltpu.CompilerParams(collective_id=ident, has_side_effects=True),
     )(*[job[0] for job in jobs])
 
@@ -215,11 +267,9 @@
         5,
         [
             (contrib.astype(jnp.bfloat16), "dom", n_dom, 1, False, True, part_rows),
-            (packed, "dom", group, 1, True, True, 0),
+            (packed, "dom", group, 1, True, True, 0, n_dom // group, group),
         ],
     )
-    if group < n_dom:
-        summed = exchange(summed, 4, "dom", n_dom // group, stride=group, bcast=True, reduce=True)
     grad_self = summed[:col_width]
     grad_nbr = summed[col_width : 2 * col_width]
     grad_bias = summed[2 * col_width, : bias_part.shape[0]]

time: 165 us -> 160 us (0.970); the launches traced: 162 us -> 159 us
  Pallas kernels: 93.7 us -> 90.4 us
    pallas_call x4 -> x3, Pallas kernels: 93.7 us -> 90.4 us  [exchange_many(): pl.pallas_call(functools.partial(exchange_kernel, tuple(specs)), out_shap...]
where the time goes in v6:
time: 160 us; the launch traced here: 159 us
  Pallas kernels  90.4 us (56%)
  other arithmetic  32.1 us (20%)
  local copies, waits for them, and re-layouts  29.9 us (19%)
  matrix products  4.19 us (3%)
  between operations  2.22 us (1%)
    pallas_call x3, Pallas kernels, exchange_many(): pl.pallas_call(functools.partial(exchange_kernel, tuple(specs)), out_shap...  90.4 us
    scatter-add x1, other arithmetic, per_device(): contrib = jnp.zeros((col_width, total_rows), jnp.float32).at[:, neighbour...  26.1 us
    gather x1, local copies, waits for them, and re-layouts, per_device(): gathered = sources[:, neighbours].astype(jnp.float32)  13.8 us
    scatter-add x1, local copies, waits for them, and re-layouts, per_device(): contrib = jnp.zeros((col_width, total_rows), jnp.float32).at[:, neighbour...  5.29 us
    reshape x1, local copies, waits for them, and re-layouts, per_device(): sources = blocks.transpose(1, 0, 2).reshape(col_width, n_dom * part_rows)  4.48 us

profile of v6, /device:TPU:1, one launch (start us, length us, event | category | flops | bytes accessed | tf_op | source)
XLA Modules:
  0.0 158.8 jit_solution(618751318252440528)
XLA Ops:
  0.6 0.7 compare_convert_fusion
  1.3 0.6 dynamic_slice.19
  2.5 1.3 dynamic-slice_select_fusion.refs_0_
  3.8 29.2 %shard_map.137 = bf16[64,16,256]{2,1,0:T(8,128)(2,1)} custom-call(bf16[16,256]{1,0:T(8,128)(2,1)} %dynamic-slice_select_fusion.refs_0_), custom_call_target="tpu_custom_call" | custom-call | tf_op jit(solution)/shard_map/pallas_call | solution.py:171
  33.0 0.0 copy-start.2
  33.1 4.5 %copy.26 = bf16[16,64,256]{0,2,1:T(8,128)(2,1)} copy(bf16[16,64,256]{2,0,1:T(8,128)(2,1)} %bitcast.59) | data formatting | bytes 1048576 | tf_op jit(solution)/shard_map/reshape | solution.py:211
  37.6 13.8 %gather_fusion = bf16[4096,16]{1,0:T(8,128)(2,1)S(1)} fusion(bf16[16,16384]{0,1:T(8,128)(2,1)} %bitcast.58, s32[4096]{0:T(1024)S(1)} %broadcast_clamp_fusion), kind=kCustom, calls=%fused_computation | custom fusion | bytes 278528 | tf_op jit(solution)/shard_map/gather | solution.py:217
  51.4 0.6 dynamic_slice.18
  52.0 0.6 convert_divide_fusion
  52.7 0.7 fusion.2
  53.4 0.1 copy.23
  53.5 0.6 scatter.6.refs_1_
  54.2 17.9 %shard_map.138 = (bf16[8,96,256]{2,1,0:T(8,128)(2,1)}, f32[8,8,128]{2,1,0:T(8,128)}) custom-call(bf16[96,256]{1,0:T(8,128)(2,1)} %copy-done.1, f32[8,128]{1,0:T(8,128)} %scatter.6.refs_1_), custom_call_target="tpu_custom_call" | custom-call | tf_op jit(solution)/shard_map/pallas_call | solution.py:171
  72.0 0.9 slice.69
  72.9 0.7 compare_convert_fusion.1
  73.6 0.8 slice_reduce_fusion
  74.4 0.1 add.68
  74.5 1.1 convolution_bitcast_fusion
  75.5 1.2 fusion.12
  76.7 0.7 convert_reduce_fusion
  77.5 0.1 fusion.9
  77.6 0.1 copy.24
  77.8 0.6 bitcast_multiply_fusion
  78.4 26.1 %scatter_custom_fusion = f32[16,16384]{0,1:T(8,128)} fusion(s32[4096]{0:T(1024)S(1)} %bitcast.65, f32[]{:T(128)} %constant.74.clone.1, f32[16,4096]{0,1:T(8,128)S(1)} %bitcast_multiply_fusion), kind=kCustom, calls=%fused_computation.2 | custom fusion | flops 65536 | bytes 3145732 | tf_op jit(solution)/shard_map/scatter-add | solution.py:263
  104.5 5.3 %copy.25.refs_0_ = bf16[16,16384]{1,0:T(8,128)(2,1)} copy(f32[16,16384]{0,1:T(8,128)} %scatter_custom_fusion) | data formatting | bytes 1572864 | tf_op jit(solution)/shard_map/scatter-add | solution.py:263
  109.8 0.1 fusion.23
  109.9 0.2 convolution_bitcast_fusion.3
  110.1 0.7 select_maximum_fusion.refs_1_
  110.8 43.4 %shard_map.139 = (f32[16,256]{1,0:T(8,128)}, f32[40,256]{1,0:T(8,128)}) custom-call(bf16[16,16384]{1,0:T(8,128)(2,1)} %copy.25.refs_0_, f32[40,256]{1,0:T(8,128)} %select_maximum_fusion.refs_1_), custom_call_target="tpu_custom_call" | custom-call | tf_op jit(solution)/shard_map/pallas_call | solution.py:171
  154.8 1.5 fusion.7
  156.3 1.3 fusion.22
  157.6 1.2 slice_bitcast_fusion
  (29 shorter events, 0.1 us)
Async XLA Ops:
  33.0 4.5 %copy-start.2 = (s32[16,256]{1,0:T(8,128)S(1)}, s32[16,256]{1,0:T(8,128)}, u32[]{:S(2)}) copy-start(s32[16,256]{1,0:T(8,128)} %param.18) | copy-start | bytes 49156
  33.0 18.3 %copy-start.8 = (s32[64]{0:T(128)S(1)}, s32[64]{0:T(128)}, u32[]{:S(2)}) copy-start(s32[64]{0:T(128)} %param.17) | copy-start | bytes 772
  33.0 18.9 %copy-start.6 = (s32[256]{0:T(256)S(1)}, s32[256]{0:T(256)}, u32[]{:S(2)}) copy-start(s32[256]{0:T(256)} %param.19) | copy-start | bytes 3076
  37.5 15.9 %copy-start = (bf16[16,256]{1,0:T(8,128)(2,1)S(1)}, bf16[16,256]{1,0:T(8,128)(2,1)}, u32[]{:S(2)}) copy-start(bf16[16,256]{1,0:T(8,128)(2,1)} %param.14) | copy-start | bytes 24580
  37.5 15.9 %copy-start.4 = (bf16[16,256]{1,0:T(8,128)(2,1)S(1)}, bf16[16,256]{1,0:T(8,128)(2,1)}, u32[]{:S(2)}) copy-start(bf16[16,256]{1,0:T(8,128)(2,1)} %param.20) | copy-start | bytes 24580
  37.5 15.9 %copy-start.3 = (bf16[16,256]{1,0:T(8,128)(2,1)S(1)}, bf16[16,256]{1,0:T(8,128)(2,1)}, u32[]{:S(2)}) copy-start(bf16[16,256]{1,0:T(8,128)(2,1)} %param.21) | copy-start | bytes 24580
  37.5 16.0 %copy-start.5 = (bf16[32,256]{1,0:T(8,128)(2,1)S(1)}, bf16[32,256]{1,0:T(8,128)(2,1)}, u32[]{:S(2)}) copy-start(bf16[32,256]{1,0:T(8,128)(2,1)} %param.23) | copy-start | bytes 49156
  37.5 16.0 %copy-start.7 = (f32[32]{0:T(128)S(1)}, f32[32]{0:T(128)}, u32[]{:S(2)}) copy-start(f32[32]{0:T(128)} %param.22) | copy-start | bytes 388
  53.5 0.6 copy-start.1

commit v7 on v6

--- a/solution.py
+++ b/solution.py
@@ -21,6 +21,21 @@
     return lax.dot_general(
         data, grads, (((1,), (1,)), ((), ())), preferred_element_type=jnp.float32
     )
+
+
+def group_pos(me, digits):
+    pos, scale = 0, 1
+    for radix, stride in digits:
+        pos = pos + lax.rem(me // stride, radix) * scale
+        scale *= radix
+    return pos
+
+
+def group_member(me, pos, j, digits):
+    for radix, stride in digits:
+        me = me + (lax.rem(j, radix) - lax.rem(pos, radix)) * stride
+        j, pos = j // radix, pos // radix
+    return me
 
 
 def exchange_kernel(specs, *refs):
@@ -34,12 +49,12 @@
         x_ref, y_ref = xs[e], ys[e]
         buf, send_sem, recv_sem = scratch[3 * e : 3 * e + 3]
         me = lax.axis_index(axis)
-        pos = lax.rem(me // stride, size)
+        pos = group_pos(me, stride)
         plans.append((axis, size, stride, bcast, reduce, lanes, x_ref, y_ref, buf, send_sem, recv_sem, me, pos))
 
     def member(plan, j):
         stride, me, pos = plan[2], plan[11], plan[12]
-        return me + (j - pos) * stride
+        return group_member(me, pos, j, stride)
 
     def chunk(plan, j):
         bcast, lanes, x_ref = plan[3], plan[5], plan[6]
@@ -75,7 +90,7 @@
             stage, buf2, send2, recv2 = extra[4 * len(seconds) : 4 * len(seconds) + 4]
             me = plans[e][11]
             second = (spec[0], spec[6], spec[7], True, True, 0, stage, None, buf2, send2, recv2, me,
-                      lax.rem(me // spec[7], spec[6]))
+                      group_pos(me, spec[7]))
             seconds.append((e, second))
     greetings = 0
     for plan in plans + [second for _, second in seconds]:
@@ -145,7 +160,7 @@
     specs, out_shapes, scratch, extra = [], [], [], []
     for job in jobs:
         x, axis, size, stride, bcast, reduce, lanes = job[:7]
-        size2, stride2 = job[7:] if len(job) > 7 else (1, 1)
+        size2, stride2 = job[7:] if len(job) > 7 else (1, ((1, 1),))
         if bcast:
             block = x.shape
         elif lanes:
@@ -178,7 +193,8 @@
     )(*[job[0] for job in jobs])
 
 
-def exchange(x, ident, axis, size, stride=1, bcast=False, reduce=False, lanes=0):
+def exchange(x, ident, axis, size, stride=None, bcast=False, reduce=False, lanes=0):
+    stride = ((size, 1),) if stride is None else stride
     return exchange_many(ident, [(x, axis, size, stride, bcast, reduce, lanes)])[0]
 
 
@@ -219,8 +235,8 @@
     col_blocks, bias_blocks = exchange_many(
         1,
         [
-            (jnp.concatenate([aggregated, col_inputs], axis=0), "col", n_col, 1, True, False, 0),
-            (bias_block, "col", n_col, 1, True, False, 0),
+            (jnp.concatenate([aggregated, col_inputs], axis=0), "col", n_col, ((n_col, 1),), True, False, 0),
+            (bias_block, "col", n_col, ((n_col, 1),), True, False, 0),
         ],
     )
     agg_full = col_blocks[:, :col_width].reshape(n_col * col_width, part_rows)
@@ -262,12 +278,13 @@
         .at[:, neighbours.reshape(-1)]
         .add(spread.reshape(col_width, -1))
     )
-    group = 8 if n_dom % 8 == 0 else n_dom
+    ys = 8 if n_dom % 16 == 0 else 1
+    first = ((2, 1), (n_dom // (2 * ys), 2 * ys))
     back, summed = exchange_many(
         5,
         [
-            (contrib.astype(jnp.bfloat16), "dom", n_dom, 1, False, True, part_rows),
-            (packed, "dom", group, 1, True, True, 0, n_dom // group, group),
+            (contrib.astype(jnp.bfloat16), "dom", n_dom, ((n_dom, 1),), False, True, part_rows),
+            (packed, "dom", n_dom // ys, first, True, True, 0, ys, ((ys, 2),)),
         ],
     )
     grad_self = summed[:col_width]

time: 160 us -> 158 us (0.988)
  no operation moved by 1% of the time
where the time goes in v7:
time: 158 us; the launch traced here: 157 us
  Pallas kernels  88.9 us (56%)
  other arithmetic  32.1 us (20%)
  local copies, waits for them, and re-layouts  29.9 us (19%)
  matrix products  4.19 us (3%)
  between operations  2.22 us (1%)
    pallas_call x3, Pallas kernels, exchange_many(): pl.pallas_call(functools.partial(exchange_kernel, tuple(specs)), out_shap...  88.9 us
    scatter-add x1, other arithmetic, per_device(): contrib = jnp.zeros((col_width, total_rows), jnp.float32).at[:, neighbour...  26.1 us
    gather x1, local copies, waits for them, and re-layouts, per_device(): gathered = sources[:, neighbours].astype(jnp.float32)  13.8 us
    scatter-add x1, local copies, waits for them, and re-layouts, per_device(): contrib = jnp.zeros((col_width, total_rows), jnp.float32).at[:, neighbour...  5.29 us
    reshape x1, local copies, waits for them, and re-layouts, per_device(): sources = blocks.transpose(1, 0, 2).reshape(col_width, n_dom * part_rows)  4.48 us

profile of v7, /device:TPU:1, one launch (start us, length us, event | category | flops | bytes accessed | tf_op | source)
XLA Modules:
  0.0 157.3 jit_solution(2223624320985233731)
XLA Ops:
  0.6 0.7 compare_convert_fusion
  1.3 0.6 dynamic_slice.19
  2.5 1.3 dynamic-slice_select_fusion.refs_0_
  3.8 29.2 %shard_map.137 = bf16[64,16,256]{2,1,0:T(8,128)(2,1)} custom-call(bf16[16,256]{1,0:T(8,128)(2,1)} %dynamic-slice_select_fusion.refs_0_), custom_call_target="tpu_custom_call" | custom-call | tf_op jit(solution)/shard_map/pallas_call | solution.py:186
  33.1 0.0 copy-start.2
  33.1 4.5 %copy.26 = bf16[16,64,256]{0,2,1:T(8,128)(2,1)} copy(bf16[16,64,256]{2,0,1:T(8,128)(2,1)} %bitcast.59) | data formatting | bytes 1048576 | tf_op jit(solution)/shard_map/reshape | solution.py:227
  37.7 13.8 %gather_fusion = bf16[4096,16]{1,0:T(8,128)(2,1)S(1)} fusion(bf16[16,16384]{0,1:T(8,128)(2,1)} %bitcast.58, s32[4096]{0:T(1024)S(1)} %broadcast_clamp_fusion), kind=kCustom, calls=%fused_computation | custom fusion | bytes 278528 | tf_op jit(solution)/shard_map/gather | solution.py:233
  51.4 0.6 dynamic_slice.18
  52.0 0.6 convert_divide_fusion
  52.7 0.7 fusion.2
  53.4 0.1 copy.23
  53.6 0.6 scatter.6.refs_1_
  54.2 17.9 %shard_map.138 = (bf16[8,96,256]{2,1,0:T(8,128)(2,1)}, f32[8,8,128]{2,1,0:T(8,128)}) custom-call(bf16[96,256]{1,0:T(8,128)(2,1)} %copy-done.1, f32[8,128]{1,0:T(8,128)} %scatter.6.refs_1_), custom_call_target="tpu_custom_call" | custom-call | tf_op jit(solution)/shard_map/pallas_call | solution.py:186
  72.1 0.9 slice.69
  73.0 0.7 compare_convert_fusion.1
  73.7 0.8 slice_reduce_fusion
  74.4 0.1 add.68
  74.5 1.1 convolution_bitcast_fusion
  75.6 1.2 fusion.12
  76.8 0.7 convert_reduce_fusion
  77.6 0.1 fusion.9
  77.7 0.1 copy.24
  77.8 0.6 bitcast_multiply_fusion
  78.4 26.1 %scatter_custom_fusion = f32[16,16384]{0,1:T(8,128)} fusion(s32[4096]{0:T(1024)S(1)} %bitcast.65, f32[]{:T(128)} %constant.74.clone.1, f32[16,4096]{0,1:T(8,128)S(1)} %bitcast_multiply_fusion), kind=kCustom, calls=%fused_computation.2 | custom fusion | flops 65536 | bytes 3145732 | tf_op jit(solution)/shard_map/scatter-add | solution.py:279
  104.5 5.3 %copy.25.refs_0_ = bf16[16,16384]{1,0:T(8,128)(2,1)} copy(f32[16,16384]{0,1:T(8,128)} %scatter_custom_fusion) | data formatting | bytes 1572864 | tf_op jit(solution)/shard_map/scatter-add | solution.py:279
  109.8 0.1 fusion.23
  110.0 0.2 convolution_bitcast_fusion.3
  110.2 0.7 select_maximum_fusion.refs_1_
  110.8 41.8 %shard_map.139 = (f32[16,256]{1,0:T(8,128)}, f32[40,256]{1,0:T(8,128)}) custom-call(bf16[16,16384]{1,0:T(8,128)(2,1)} %copy.25.refs_0_, f32[40,256]{1,0:T(8,128)} %select_maximum_fusion.refs_1_), custom_call_target="tpu_custom_call" | custom-call | tf_op jit(solution)/shard_map/pallas_call | solution.py:186
  153.3 1.5 fusion.7
  154.7 1.3 fusion.22
  156.1 1.2 slice_bitcast_fusion
  (29 shorter events, 0.1 us)
Async XLA Ops:
  33.1 4.5 %copy-start.2 = (s32[16,256]{1,0:T(8,128)S(1)}, s32[16,256]{1,0:T(8,128)}, u32[]{:S(2)}) copy-start(s32[16,256]{1,0:T(8,128)} %param.18) | copy-start | bytes 49156
  33.1 18.3 %copy-start.8 = (s32[64]{0:T(128)S(1)}, s32[64]{0:T(128)}, u32[]{:S(2)}) copy-start(s32[64]{0:T(128)} %param.17) | copy-start | bytes 772
  33.1 18.9 %copy-start.6 = (s32[256]{0:T(256)S(1)}, s32[256]{0:T(256)}, u32[]{:S(2)}) copy-start(s32[256]{0:T(256)} %param.19) | copy-start | bytes 3076
  37.6 15.9 %copy-start = (bf16[16,256]{1,0:T(8,128)(2,1)S(1)}, bf16[16,256]{1,0:T(8,128)(2,1)}, u32[]{:S(2)}) copy-start(bf16[16,256]{1,0:T(8,128)(2,1)} %param.14) | copy-start | bytes 24580
  37.6 15.9 %copy-start.4 = (bf16[16,256]{1,0:T(8,128)(2,1)S(1)}, bf16[16,256]{1,0:T(8,128)(2,1)}, u32[]{:S(2)}) copy-start(bf16[16,256]{1,0:T(8,128)(2,1)} %param.20) | copy-start | bytes 24580
  37.6 15.9 %copy-start.3 = (bf16[16,256]{1,0:T(8,128)(2,1)S(1)}, bf16[16,256]{1,0:T(8,128)(2,1)}, u32[]{:S(2)}) copy-start(bf16[16,256]{1,0:T(8,128)(2,1)} %param.21) | copy-start | bytes 24580
  37.6 16.0 %copy-start.5 = (bf16[32,256]{1,0:T(8,128)(2,1)S(1)}, bf16[32,256]{1,0:T(8,128)(2,1)}, u32[]{:S(2)}) copy-start(bf16[32,256]{1,0:T(8,128)(2,1)} %param.23) | copy-start | bytes 49156
  37.6 16.0 %copy-start.7 = (f32[32]{0:T(128)S(1)}, f32[32]{0:T(128)}, u32[]{:S(2)}) copy-start(f32[32]{0:T(128)} %param.22) | copy-start | bytes 388
  53.6 0.6 copy-start.1

commit v8 on v7

--- a/solution.py
+++ b/solution.py
@@ -115,7 +115,7 @@
             desc(plan, j, j).wait_recv()
 
         each_peer(plan, finish_first)
-        second[6][...] = jnp.sum(plan[8][...].astype(jnp.float32), axis=0)
+        second[6][...] = jnp.sum(plan[8][...].astype(jnp.float32), axis=0).astype(second[6].dtype)
     for e, plan in enumerate(plans):
         if specs[e][6] > 1:
             continue
@@ -170,8 +170,8 @@
         specs.append((axis, size, stride, bcast, reduce, lanes, size2, stride2))
         if size2 > 1:
             extra += [
-                pltpu.VMEM(block, jnp.float32),
-                pltpu.VMEM((size2,) + block, jnp.float32),
+                pltpu.VMEM(block, x.dtype),
+                pltpu.VMEM((size2,) + block, x.dtype),
                 pltpu.SemaphoreType.DMA((size2,)),
                 pltpu.SemaphoreType.DMA((size2,)),
             ]
@@ -284,7 +284,7 @@
         5,
         [
             (contrib.astype(jnp.bfloat16), "dom", n_dom, ((n_dom, 1),), False, True, part_rows),
-            (packed, "dom", n_dom // ys, first, True, True, 0, ys, ((ys, 2),)),
+            (packed.astype(jnp.bfloat16), "dom", n_dom // ys, first, True, True, 0, ys, ((ys, 2),)),
         ],
     )
     grad_self = summed[:col_width]

time: 158 us -> 151 us (0.956)
  Pallas kernels: 88.9 us -> 82.2 us
    pallas_call x3, Pallas kernels: 88.9 us -> 82.2 us  [exchange_many(): pl.pallas_call(functools.partial(exchange_kernel, tuple(specs)), out_shap...]
where the time goes in v8:
time: 151 us
  Pallas kernels  82.2 us (54%)
  other arithmetic  32.1 us (21%)
  local copies, waits for them, and re-layouts  29.9 us (20%)
  matrix products  4.19 us (3%)
  between operations  2.22 us (1%)
    pallas_call x3, Pallas kernels, exchange_many(): pl.pallas_call(functools.partial(exchange_kernel, tuple(specs)), out_shap...  82.2 us
    scatter-add x1, other arithmetic, per_device(): contrib = jnp.zeros((col_width, total_rows), jnp.float32).at[:, neighbour...  26.1 us
    gather x1, local copies, waits for them, and re-layouts, per_device(): gathered = sources[:, neighbours].astype(jnp.float32)  13.8 us
    scatter-add x1, local copies, waits for them, and re-layouts, per_device(): contrib = jnp.zeros((col_width, total_rows), jnp.float32).at[:, neighbour...  5.3 us
    reshape x1, local copies, waits for them, and re-layouts, per_device(): sources = blocks.transpose(1, 0, 2).reshape(col_width, n_dom * part_rows)  4.47 us

profile of v8, /device:TPU:1, one launch (start us, length us, event | category | flops | bytes accessed | tf_op | source)
XLA Modules:
  0.0 150.6 jit_solution(17241047783017070527)
XLA Ops:
  0.6 0.7 compare_convert_fusion
  1.3 0.6 dynamic_slice.19
  2.5 1.3 dynamic-slice_select_fusion.refs_0_
  3.8 29.2 %shard_map.137 = bf16[64,16,256]{2,1,0:T(8,128)(2,1)} custom-call(bf16[16,256]{1,0:T(8,128)(2,1)} %dynamic-slice_select_fusion.refs_0_), custom_call_target="tpu_custom_call" | custom-call | tf_op jit(solution)/shard_map/pallas_call | solution.py:186
  33.1 4.5 %copy.26 = bf16[16,64,256]{0,2,1:T(8,128)(2,1)} copy(bf16[16,64,256]{2,0,1:T(8,128)(2,1)} %bitcast.59) | data formatting | bytes 1048576 | tf_op jit(solution)/shard_map/reshape | solution.py:227
  37.6 13.8 %gather_fusion = bf16[4096,16]{1,0:T(8,128)(2,1)S(1)} fusion(bf16[16,16384]{0,1:T(8,128)(2,1)} %bitcast.58, s32[4096]{0:T(1024)S(1)} %broadcast_clamp_fusion), kind=kCustom, calls=%fused_computation | custom fusion | bytes 278528 | tf_op jit(solution)/shard_map/gather | solution.py:233
  51.4 0.6 dynamic_slice.18
  52.0 0.6 convert_divide_fusion
  52.7 0.7 fusion.2
  53.4 0.1 copy.23
  53.6 0.6 scatter.6.refs_1_
  54.2 17.9 %shard_map.138 = (bf16[8,96,256]{2,1,0:T(8,128)(2,1)}, f32[8,8,128]{2,1,0:T(8,128)}) custom-call(bf16[96,256]{1,0:T(8,128)(2,1)} %copy-done.1, f32[8,128]{1,0:T(8,128)} %scatter.6.refs_1_), custom_call_target="tpu_custom_call" | custom-call | tf_op jit(solution)/shard_map/pallas_call | solution.py:186
  72.0 0.9 slice.69
  73.0 0.7 compare_convert_fusion.1
  73.6 0.8 slice_reduce_fusion
  74.4 0.1 add.68
  74.5 1.1 convolution_bitcast_fusion
  75.6 1.2 fusion.13
  76.7 0.6 multiply_convert_fusion
  77.4 0.1 fusion.9
  77.5 0.1 copy.24
  77.7 0.6 bitcast_multiply_fusion
  78.3 26.1 %scatter_custom_fusion = f32[16,16384]{0,1:T(8,128)} fusion(s32[4096]{0:T(1024)S(1)} %bitcast.65, f32[]{:T(128)} %constant.75.clone.1, f32[16,4096]{0,1:T(8,128)S(1)} %bitcast_multiply_fusion), kind=kCustom, calls=%fused_computation.2 | custom fusion | flops 65536 | bytes 3145732 | tf_op jit(solution)/shard_map/scatter-add | solution.py:279
  104.4 5.3 %copy.25.refs_0_ = bf16[16,16384]{1,0:T(8,128)(2,1)} copy(f32[16,16384]{0,1:T(8,128)} %scatter_custom_fusion) | data formatting | bytes 1572864 | tf_op jit(solution)/shard_map/scatter-add | solution.py:279
  109.7 0.1 dynamic-slice_reduce_fusion
  109.8 0.2 convolution_convert_fusion.1
  110.0 0.2 fusion.10
  110.1 0.6 fusion.19.refs_1_
  110.8 35.2 %shard_map.139 = (f32[16,256]{1,0:T(8,128)}, f32[40,256]{1,0:T(8,128)}) custom-call(bf16[16,16384]{1,0:T(8,128)(2,1)} %copy.25.refs_0_, bf16[40,256]{1,0:T(8,128)(2,1)} %fusion.19.refs_1_), custom_call_target="tpu_custom_call" | custom-call | tf_op jit(solution)/shard_map/pallas_call | solution.py:186
  146.6 1.5 fusion.7
  148.1 1.3 fusion.24
  149.4 1.2 slice_bitcast_fusion
  (30 shorter events, 0.1 us)
Async XLA Ops:
  33.1 4.5 %copy-start.2 = (s32[16,256]{1,0:T(8,128)S(1)}, s32[16,256]{1,0:T(8,128)}, u32[]{:S(2)}) copy-start(s32[16,256]{1,0:T(8,128)} %param.18) | copy-start | bytes 49156
  33.1 18.3 %copy-start.8 = (s32[64]{0:T(128)S(1)}, s32[64]{0:T(128)}, u32[]{:S(2)}) copy-start(s32[64]{0:T(128)} %param.17) | copy-start | bytes 772
  33.1 18.9 %copy-start.6 = (s32[256]{0:T(256)S(1)}, s32[256]{0:T(256)}, u32[]{:S(2)}) copy-start(s32[256]{0:T(256)} %param.19) | copy-start | bytes 3076
  37.6 15.9 %copy-start = (bf16[16,256]{1,0:T(8,128)(2,1)S(1)}, bf16[16,256]{1,0:T(8,128)(2,1)}, u32[]{:S(2)}) copy-start(bf16[16,256]{1,0:T(8,128)(2,1)} %param.14) | copy-start | bytes 24580
  37.6 15.9 %copy-start.4 = (bf16[16,256]{1,0:T(8,128)(2,1)S(1)}, bf16[16,256]{1,0:T(8,128)(2,1)}, u32[]{:S(2)}) copy-start(bf16[16,256]{1,0:T(8,128)(2,1)} %param.20) | copy-start | bytes 24580
  37.6 15.9 %copy-start.3 = (bf16[16,256]{1,0:T(8,128)(2,1)S(1)}, bf16[16,256]{1,0:T(8,128)(2,1)}, u32[]{:S(2)}) copy-start(bf16[16,256]{1,0:T(8,128)(2,1)} %param.21) | copy-start | bytes 24580
  37.6 16.0 %copy-start.5 = (bf16[32,256]{1,0:T(8,128)(2,1)S(1)}, bf16[32,256]{1,0:T(8,128)(2,1)}, u32[]{:S(2)}) copy-start(bf16[32,256]{1,0:T(8,128)(2,1)} %param.23) | copy-start | bytes 49156
  37.6 16.0 %copy-start.7 = (f32[32]{0:T(128)S(1)}, f32[32]{0:T(128)}, u32[]{:S(2)}) copy-start(f32[32]{0:T(128)} %param.22) | copy-start | bytes 388
  53.6 0.6 copy-start.1

commit v9 on v8

--- a/solution.py
+++ b/solution.py
@@ -8,6 +8,7 @@
 from jax.sharding import PartitionSpec as P
 
 LIMIT = 8
+FRESH = 16
 MESH = pl.DeviceIdType.MESH
 
 
@@ -272,18 +273,29 @@
     grad_agg = jnp.dot(w_nbr, grad_full, preferred_element_type=jnp.float32).astype(jnp.bfloat16)
     own_term = jnp.dot(w_self, grad_full, preferred_element_type=jnp.float32)
     spread = weights[None, :, :] * grad_agg.astype(jnp.float32)[:, None, :]
-    total_rows = cached_embed.shape[1]
+    fresh_rank = jnp.cumsum(fresh_flag) - 1
+    nbr_part = neighbours // part_rows
+    compact = jnp.where(
+        fresh_flag[nbr_part] == 1,
+        fresh_rank[nbr_part] * part_rows + neighbours % part_rows,
+        FRESH * part_rows,
+    )
     contrib = (
-        jnp.zeros((col_width, total_rows), jnp.float32)
-        .at[:, neighbours.reshape(-1)]
-        .add(spread.reshape(col_width, -1))
-    )
+        jnp.zeros((col_width, FRESH * part_rows), jnp.float32)
+        .at[:, compact.reshape(-1)]
+        .add(spread.reshape(col_width, -1), mode="drop")
+    )
+    padded = jnp.concatenate(
+        [contrib.astype(jnp.bfloat16), jnp.zeros((col_width, part_rows), jnp.bfloat16)], axis=1
+    ).reshape(col_width, FRESH + 1, part_rows)
+    block_of = jnp.where(fresh_flag == 1, fresh_rank, FRESH)
+    contrib = jnp.take(padded, block_of, axis=1).reshape(col_width, n_dom * part_rows)
     ys = 8 if n_dom % 16 == 0 else 1
     first = ((2, 1), (n_dom // (2 * ys), 2 * ys))
     back, summed = exchange_many(
         5,
         [
-            (contrib.astype(jnp.bfloat16), "dom", n_dom, ((n_dom, 1),), False, True, part_rows),
+            (contrib, "dom", n_dom, ((n_dom, 1),), False, True, part_rows),
             (packed.astype(jnp.bfloat16), "dom", n_dom // ys, first, True, True, 0, ys, ((ys, 2),)),
         ],
     )

time: 151 us -> 198 us (1.31)
  local copies, waits for them, and re-layouts: 29.9 us -> 75.4 us
    gather x0 -> x4, local copies, waits for them, and re-layouts: none -> 50 us  [the longest x1 24.7 us: per_device(): fresh_rank[nbr_part] * part_rows + neighbours % part_rows]
    scatter-add x1 -> x0, local copies, waits for them, and re-layouts: 5.3 us -> none  [per_device(): contrib = jnp.zeros((col_width, total_rows), jnp.float32).at[:, neighbour...]
    scatter-add x1, other arithmetic: 26.1 us -> 23.8 us  [per_device(): contrib = jnp.zeros((col_width, FRESH * part_rows), jnp.float32).at[:, co...]
where the time goes in v9:
time: 198 us
  Pallas kernels  82.2 us (42%)
  local copies, waits for them, and re-layouts  75.4 us (38%)
  other arithmetic  33.3 us (17%)
  matrix products  4.16 us (2%)
  between operations  2.36 us (1%)
    pallas_call x3, Pallas kernels, exchange_many(): pl.pallas_call(functools.partial(exchange_kernel, tuple(specs)), out_shap...  82.2 us
    gather x1, local copies, waits for them, and re-layouts, per_device(): fresh_rank[nbr_part] * part_rows + neighbours % part_rows  24.7 us
    gather x1, local copies, waits for them, and re-layouts, per_device(): fresh_flag[nbr_part] == 1  24.7 us
    scatter-add x1, other arithmetic, per_device(): contrib = jnp.zeros((col_width, FRESH * part_rows), jnp.float32).at[:, co...  23.8 us
    gather x1, local copies, waits for them, and re-layouts, per_device(): gathered = sources[:, neighbours].astype(jnp.float32)  13.8 us
    reshape x1, local copies, waits for them, and re-layouts, per_device(): sources = blocks.transpose(1, 0, 2).reshape(col_width, n_dom * part_rows)  4.48 us

profile of v9, /device:TPU:1, one launch (start us, length us, event | category | flops | bytes accessed | tf_op | source)
XLA Modules:
  0.0 197.5 jit_solution(2306375137804992547)
XLA Ops:
  0.6 0.7 fusion.30
  1.6 0.7 compare_and_fusion
  2.3 0.6 dynamic_slice.19
  3.5 1.3 dynamic-slice_select_fusion.refs_0_
  4.8 29.2 %shard_map.137 = bf16[64,16,256]{2,1,0:T(8,128)(2,1)} custom-call(bf16[16,256]{1,0:T(8,128)(2,1)} %dynamic-slice_select_fusion.refs_0_), custom_call_target="tpu_custom_call" | custom-call | tf_op jit(solution)/shard_map/pallas_call | solution.py:187
  34.1 4.5 %copy.30 = bf16[16,64,256]{0,2,1:T(8,128)(2,1)} copy(bf16[16,64,256]{2,0,1:T(8,128)(2,1)} %bitcast.70) | data formatting | bytes 1048576 | tf_op jit(solution)/shard_map/reshape | solution.py:228
  38.6 24.7 %gather_fusion.1 = s32[4096]{0:T(1024)S(1)} fusion(s32[64]{0:T(128)S(1)} %get-tuple-element.47, s32[4096]{0:T(1024)S(1)} %broadcast_clamp_fusion), kind=kCustom, calls=%fused_computation.1 | custom fusion | bytes 49152 | tf_op jit(solution)/shard_map/gather | solution.py:279
  63.4 24.7 %gather_fusion.2 = s32[4096]{0:T(1024)S(1)} fusion(s32[64]{0:T(128)S(1)} %add_reduce_fusion, s32[4096]{0:T(1024)S(1)} %broadcast_clamp_fusion), kind=kCustom, calls=%fused_computation.2 | custom fusion | bytes 49152 | tf_op jit(solution)/shard_map/gather | solution.py:280
  88.2 13.8 %gather_fusion = bf16[4096,16]{1,0:T(8,128)(2,1)S(1)} fusion(bf16[16,16384]{0,1:T(8,128)(2,1)} %bitcast.68, s32[4096]{0:T(1024)S(1)} %broadcast_clamp_fusion.1), kind=kCustom, calls=%fused_computation | custom fusion | bytes 278528 | tf_op jit(solution)/shard_map/gather | solution.py:234
  102.0 0.6 dynamic_slice.18
  102.6 0.6 convert_divide_fusion
  103.2 0.7 fusion
  104.1 0.6 scatter.6.refs_1_
  104.7 17.8 %shard_map.138 = (bf16[8,96,256]{2,1,0:T(8,128)(2,1)}, f32[8,8,128]{2,1,0:T(8,128)}) custom-call(bf16[96,256]{1,0:T(8,128)(2,1)} %copy-done.1, f32[8,128]{1,0:T(8,128)} %scatter.6.refs_1_), custom_call_target="tpu_custom_call" | custom-call | tf_op jit(solution)/shard_map/pallas_call | solution.py:187
  122.5 1.1 convolution_bitcast_fusion
  123.6 0.9 slice.69
  124.5 0.8 slice_reduce_fusion
  125.4 0.6 compare_convert_fusion.1
  126.1 1.2 fusion.13
  127.7 0.6 fusion.19.refs_1_
  128.6 0.6 bitcast_multiply_fusion
  129.3 23.8 %scatter_custom_fusion = f32[16,4096]{0,1:T(8,128)} fusion(s32[4096]{0:T(1024)S(1)} %bitcast.78, f32[16,4096]{0,1:T(8,128)S(1)} %bitcast_multiply_fusion, f32[]{:T(128)} %constant.119.clone.1), kind=kCustom, calls=%fused_computation.7 | custom fusion | flops 65536 | bytes 2359300 | tf_op jit(solution)/shard_map/scatter-add | solution.py:286
  153.1 1.7 convert_element_type.72
  154.8 0.2 concatenate.15
  155.0 0.3 copy.28
  155.4 0.6 gather_fusion.3
  156.1 0.9 broadcast_select_fusion.refs_0_
  157.0 35.2 %shard_map.139 = (f32[16,256]{1,0:T(8,128)}, f32[40,256]{1,0:T(8,128)}) custom-call(bf16[16,16384]{1,0:T(8,128)(2,1)} %broadcast_select_fusion.refs_0_, bf16[40,256]{1,0:T(8,128)(2,1)} %fusion.19.refs_1_), custom_call_target="tpu_custom_call" | custom-call | tf_op jit(solution)/shard_map/pallas_call | solution.py:187
  192.2 1.3 fusion.31
  194.2 1.5 fusion.6
  195.7 1.2 slice_bitcast_fusion
  196.9 0.6 multiply_convert_fusion
  (51 shorter events, 1.5 us)
Async XLA Ops:
  34.0 4.5 %copy-start.2 = (s32[16,256]{1,0:T(8,128)S(1)}, s32[16,256]{1,0:T(8,128)}, u32[]{:S(2)}) copy-start(s32[16,256]{1,0:T(8,128)} %param.18) | copy-start | bytes 49156
  63.3 38.6 %copy-start.8 = (s32[64]{0:T(128)S(1)}, s32[64]{0:T(128)}, u32[]{:S(2)}) copy-start(s32[64]{0:T(128)} %param.17) | copy-start | bytes 772
  63.3 39.2 %copy-start.6 = (s32[256]{0:T(256)S(1)}, s32[256]{0:T(256)}, u32[]{:S(2)}) copy-start(s32[256]{0:T(256)} %param.19) | copy-start | bytes 3076
  88.1 16.0 %copy-start = (bf16[16,256]{1,0:T(8,128)(2,1)S(1)}, bf16[16,256]{1,0:T(8,128)(2,1)}, u32[]{:S(2)}) copy-start(bf16[16,256]{1,0:T(8,128)(2,1)} %param.14) | copy-start | bytes 24580
  88.1 16.0 %copy-start.4 = (bf16[16,256]{1,0:T(8,128)(2,1)S(1)}, bf16[16,256]{1,0:T(8,128)(2,1)}, u32[]{:S(2)}) copy-start(bf16[16,256]{1,0:T(8,128)(2,1)} %param.20) | copy-start | bytes 24580
  88.1 16.0 %copy-start.3 = (bf16[16,256]{1,0:T(8,128)(2,1)S(1)}, bf16[16,256]{1,0:T(8,128)(2,1)}, u32[]{:S(2)}) copy-start(bf16[16,256]{1,0:T(8,128)(2,1)} %param.21) | copy-start | bytes 24580
  88.1 16.0 %copy-start.5 = (bf16[32,256]{1,0:T(8,128)(2,1)S(1)}, bf16[32,256]{1,0:T(8,128)(2,1)}, u32[]{:S(2)}) copy-start(bf16[32,256]{1,0:T(8,128)(2,1)} %param.23) | copy-start | bytes 49156
  88.1 16.0 %copy-start.7 = (f32[32]{0:T(128)S(1)}, f32[32]{0:T(128)}, u32[]{:S(2)}) copy-start(f32[32]{0:T(128)} %param.22) | copy-start | bytes 388
  104.1 0.6 copy-start.1

commit v10 on v9

--- a/solution.py
+++ b/solution.py
@@ -275,9 +275,12 @@
     spread = weights[None, :, :] * grad_agg.astype(jnp.float32)[:, None, :]
     fresh_rank = jnp.cumsum(fresh_flag) - 1
     nbr_part = neighbours // part_rows
+    owner = nbr_part[:, :, None] == jnp.arange(n_dom, dtype=jnp.int32)
+    nbr_fresh = jnp.sum(jnp.where(owner, fresh_flag, 0), axis=2)
+    nbr_rank = jnp.sum(jnp.where(owner, fresh_rank, 0), axis=2)
     compact = jnp.where(
-        fresh_flag[nbr_part] == 1,
-        fresh_rank[nbr_part] * part_rows + neighbours % part_rows,
+        nbr_fresh == 1,
+        nbr_rank * part_rows + neighbours % part_rows,
         FRESH * part_rows,
     )
     contrib = (

time: 198 us -> 149 us (0.75)
  local copies, waits for them, and re-layouts: 75.4 us -> 26 us
    gather x2 -> x0, local copies, waits for them, and re-layouts: 49.4 us -> none  [the longest x1 24.7 us: per_device(): fresh_rank[nbr_part] * part_rows + neighbours % part_rows]
where the time goes in v10:
time: 149 us; the launch traced here: 148 us
  Pallas kernels  82.2 us (55%)
  other arithmetic  33.7 us (23%)
  local copies, waits for them, and re-layouts  26 us (17%)
  matrix products  4.17 us (3%)
  between operations  2.3 us (2%)
    pallas_call x3, Pallas kernels, exchange_many(): pl.pallas_call(functools.partial(exchange_kernel, tuple(specs)), out_shap...  82.2 us
    scatter-add x1, other arithmetic, per_device(): contrib = jnp.zeros((col_width, FRESH * part_rows), jnp.float32).at[:, co...  23.8 us
    gather x1, local copies, waits for them, and re-layouts, per_device(): gathered = sources[:, neighbours].astype(jnp.float32)  13.8 us
    reshape x1, local copies, waits for them, and re-layouts, per_device(): sources = blocks.transpose(1, 0, 2).reshape(col_width, n_dom * part_rows)  4.49 us

profile of v10, /device:TPU:1, one launch (start us, length us, event | category | flops | bytes accessed | tf_op | source)
XLA Modules:
  0.0 148.3 jit_solution(2375382082606319468)
XLA Ops:
  0.6 0.7 fusion.29
  1.6 0.7 compare_and_fusion
  2.3 0.6 dynamic_slice.19
  3.5 1.3 dynamic-slice_select_fusion.refs_0_
  4.8 29.2 %shard_map.137 = bf16[64,16,256]{2,1,0:T(8,128)(2,1)} custom-call(bf16[16,256]{1,0:T(8,128)(2,1)} %dynamic-slice_select_fusion.refs_0_), custom_call_target="tpu_custom_call" | custom-call | tf_op jit(solution)/shard_map/pallas_call | solution.py:187
  34.1 4.5 %copy.37 = bf16[16,64,256]{0,2,1:T(8,128)(2,1)} copy(bf16[16,64,256]{2,0,1:T(8,128)(2,1)} %bitcast.67) | data formatting | bytes 1048576 | tf_op jit(solution)/shard_map/reshape | solution.py:228
  38.6 0.3 select_reduce_fusion.1
  39.0 13.8 %gather_fusion = bf16[4096,16]{1,0:T(8,128)(2,1)S(1)} fusion(bf16[16,16384]{0,1:T(8,128)(2,1)} %bitcast.65, s32[4096]{0:T(1024)S(1)} %broadcast_clamp_fusion), kind=kCustom, calls=%fused_computation | custom fusion | bytes 278528 | tf_op jit(solution)/shard_map/gather | solution.py:234
  52.8 0.6 dynamic_slice.18
  53.4 0.6 convert_divide_fusion
  54.1 0.7 fusion
  54.9 0.6 scatter.6.refs_1_
  55.5 17.8 %shard_map.138 = (bf16[8,96,256]{2,1,0:T(8,128)(2,1)}, f32[8,8,128]{2,1,0:T(8,128)}) custom-call(bf16[96,256]{1,0:T(8,128)(2,1)} %copy-done.1, f32[8,128]{1,0:T(8,128)} %scatter.6.refs_1_), custom_call_target="tpu_custom_call" | custom-call | tf_op jit(solution)/shard_map/pallas_call | solution.py:187
  73.3 1.1 convolution_bitcast_fusion
  74.4 0.9 slice.69
  75.4 0.8 slice_reduce_fusion
  76.2 0.6 compare_convert_fusion.1
  76.9 1.2 fusion.13
  78.3 0.2 fusion.9
  78.5 0.6 fusion.19.refs_1_
  79.4 0.6 bitcast_multiply_fusion
  80.1 23.8 %scatter_custom_fusion = f32[16,4096]{0,1:T(8,128)} fusion(s32[4096]{0:T(1024)S(1)} %bitcast.74, f32[16,4096]{0,1:T(8,128)S(1)} %bitcast_multiply_fusion, f32[]{:T(128)} %constant.118.clone.1), kind=kCustom, calls=%fused_computation.5 | custom fusion | flops 65536 | bytes 2359300 | tf_op jit(solution)/shard_map/scatter-add | solution.py:289
  103.9 1.7 %convert_element_type.72 = bf16[16,4096]{0,1:T(8,128)(2,1)S(1)} convert(f32[16,4096]{0,1:T(8,128)} %scatter_custom_fusion) | non-fusion elementwise | flops 65536 | bytes 393216 | tf_op jit(solution)/shard_map/convert_element_type | solution.py:292
  105.6 0.2 concatenate.15
  105.8 0.3 copy.35
  106.2 0.6 gather_fusion.1
  106.9 0.9 broadcast_select_fusion.refs_0_
  107.8 35.2 %shard_map.139 = (f32[16,256]{1,0:T(8,128)}, f32[40,256]{1,0:T(8,128)}) custom-call(bf16[16,16384]{1,0:T(8,128)(2,1)} %broadcast_select_fusion.refs_0_, bf16[40,256]{1,0:T(8,128)(2,1)} %fusion.19.refs_1_), custom_call_target="tpu_custom_call" | custom-call | tf_op jit(solution)/shard_map/pallas_call | solution.py:187
  143.0 1.3 fusion.30
  145.0 1.5 fusion.6
  146.5 1.2 slice_bitcast_fusion
  147.7 0.6 multiply_convert_fusion
  (44 shorter events, 1.3 us)
Async XLA Ops:
  34.0 4.6 %copy-start.2 = (s32[16,256]{1,0:T(8,128)S(1)}, s32[16,256]{1,0:T(8,128)}, u32[]{:S(2)}) copy-start(s32[16,256]{1,0:T(8,128)} %param.18) | copy-start | bytes 49156
  34.1 18.7 %copy-start.8 = (s32[64]{0:T(128)S(1)}, s32[64]{0:T(128)}, u32[]{:S(2)}) copy-start(s32[64]{0:T(128)} %param.17) | copy-start | bytes 772
  34.1 19.3 %copy-start.6 = (s32[256]{0:T(256)S(1)}, s32[256]{0:T(256)}, u32[]{:S(2)}) copy-start(s32[256]{0:T(256)} %param.19) | copy-start | bytes 3076
  38.6 16.3 %copy-start = (bf16[16,256]{1,0:T(8,128)(2,1)S(1)}, bf16[16,256]{1,0:T(8,128)(2,1)}, u32[]{:S(2)}) copy-start(bf16[16,256]{1,0:T(8,128)(2,1)} %param.14) | copy-start | bytes 24580
  38.6 16.3 %copy-start.4 = (bf16[16,256]{1,0:T(8,128)(2,1)S(1)}, bf16[16,256]{1,0:T(8,128)(2,1)}, u32[]{:S(2)}) copy-start(bf16[16,256]{1,0:T(8,128)(2,1)} %param.20) | copy-start | bytes 24580
  38.6 16.3 %copy-start.3 = (bf16[16,256]{1,0:T(8,128)(2,1)S(1)}, bf16[16,256]{1,0:T(8,128)(2,1)}, u32[]{:S(2)}) copy-start(bf16[16,256]{1,0:T(8,128)(2,1)} %param.21) | copy-start | bytes 24580
  38.6 16.3 %copy-start.5 = (bf16[32,256]{1,0:T(8,128)(2,1)S(1)}, bf16[32,256]{1,0:T(8,128)(2,1)}, u32[]{:S(2)}) copy-start(bf16[32,256]{1,0:T(8,128)(2,1)} %param.23) | copy-start | bytes 49156
  38.6 16.4 %copy-start.7 = (f32[32]{0:T(128)S(1)}, f32[32]{0:T(128)}, u32[]{:S(2)}) copy-start(f32[32]{0:T(128)} %param.22) | copy-start | bytes 388
  54.9 0.6 copy-start.1

commit v11 on v10

--- a/solution.py
+++ b/solution.py
@@ -295,11 +295,11 @@
     contrib = jnp.take(padded, block_of, axis=1).reshape(col_width, n_dom * part_rows)
     ys = 8 if n_dom % 16 == 0 else 1
     first = ((2, 1), (n_dom // (2 * ys), 2 * ys))
-    back, summed = exchange_many(
+    summed, back = exchange_many(
         5,
         [
+            (packed.astype(jnp.bfloat16), "dom", n_dom // ys, first, True, True, 0, ys, ((ys, 2),)),
             (contrib, "dom", n_dom, ((n_dom, 1),), False, True, part_rows),
-            (packed.astype(jnp.bfloat16), "dom", n_dom // ys, first, True, True, 0, ys, ((ys, 2),)),
         ],
     )
     grad_self = summed[:col_width]

time: 149 us -> 149 us (level)
  no operation moved by 1% of the time
where the time goes in v11:
time: 149 us; the launch traced here: 148 us
  Pallas kernels  81.7 us (55%)
  other arithmetic  33.7 us (23%)
  local copies, waits for them, and re-layouts  26 us (17%)
  matrix products  4.16 us (3%)
  between operations  2.3 us (2%)
    pallas_call x3, Pallas kernels, exchange_many(): pl.pallas_call(functools.partial(exchange_kernel, tuple(specs)), out_shap...  81.7 us
    scatter-add x1, other arithmetic, per_device(): contrib = jnp.zeros((col_width, FRESH * part_rows), jnp.float32).at[:, co...  23.8 us
    gather x1, local copies, waits for them, and re-layouts, per_device(): gathered = sources[:, neighbours].astype(jnp.float32)  13.8 us
    reshape x1, local copies, waits for them, and re-layouts, per_device(): sources = blocks.transpose(1, 0, 2).reshape(col_width, n_dom * part_rows)  4.49 us

profile of v11, /device:TPU:1, one launch (start us, length us, event | category | flops | bytes accessed | tf_op | source)
XLA Modules:
  0.0 147.8 jit_solution(11100042945792314402)
XLA Ops:
  0.6 0.7 fusion.29
  1.6 0.7 compare_and_fusion
  2.3 0.6 dynamic_slice.19
  3.5 1.3 dynamic-slice_select_fusion.refs_0_
  4.8 29.2 %shard_map.137 = bf16[64,16,256]{2,1,0:T(8,128)(2,1)} custom-call(bf16[16,256]{1,0:T(8,128)(2,1)} %dynamic-slice_select_fusion.refs_0_), custom_call_target="tpu_custom_call" | custom-call | tf_op jit(solution)/shard_map/pallas_call | solution.py:187
  34.1 4.5 %copy.37 = bf16[16,64,256]{0,2,1:T(8,128)(2,1)} copy(bf16[16,64,256]{2,0,1:T(8,128)(2,1)} %bitcast.67) | data formatting | bytes 1048576 | tf_op jit(solution)/shard_map/reshape | solution.py:228
  38.6 0.3 select_reduce_fusion.1
  39.0 13.8 %gather_fusion = bf16[4096,16]{1,0:T(8,128)(2,1)S(1)} fusion(bf16[16,16384]{0,1:T(8,128)(2,1)} %bitcast.65, s32[4096]{0:T(1024)S(1)} %broadcast_clamp_fusion), kind=kCustom, calls=%fused_computation | custom fusion | bytes 278528 | tf_op jit(solution)/shard_map/gather | solution.py:234
  52.8 0.6 dynamic_slice.18
  53.4 0.6 convert_divide_fusion
  54.1 0.7 fusion
  54.9 0.6 scatter.6.refs_1_
  55.5 17.8 %shard_map.138 = (bf16[8,96,256]{2,1,0:T(8,128)(2,1)}, f32[8,8,128]{2,1,0:T(8,128)}) custom-call(bf16[96,256]{1,0:T(8,128)(2,1)} %copy-done.1, f32[8,128]{1,0:T(8,128)} %scatter.6.refs_1_), custom_call_target="tpu_custom_call" | custom-call | tf_op jit(solution)/shard_map/pallas_call | solution.py:187
  73.4 1.1 convolution_bitcast_fusion
  74.4 0.9 slice.69
  75.4 0.8 slice_reduce_fusion
  76.2 0.6 compare_convert_fusion.1
  76.9 1.2 fusion.13
  78.3 0.6 bitcast_multiply_fusion
  79.0 23.8 %scatter_custom_fusion = f32[16,4096]{0,1:T(8,128)} fusion(s32[4096]{0:T(1024)S(1)} %bitcast.74, f32[16,4096]{0,1:T(8,128)S(1)} %bitcast_multiply_fusion, f32[]{:T(128)} %constant.118.clone.1), kind=kCustom, calls=%fused_computation.5 | custom fusion | flops 65536 | bytes 2359300 | tf_op jit(solution)/shard_map/scatter-add | solution.py:289
  102.8 1.7 %convert_element_type.73 = bf16[16,4096]{0,1:T(8,128)(2,1)S(1)} convert(f32[16,4096]{0,1:T(8,128)} %scatter_custom_fusion) | non-fusion elementwise | flops 65536 | bytes 393216 | tf_op jit(solution)/shard_map/convert_element_type | solution.py:292
  104.5 0.2 concatenate.16
  104.7 0.3 copy.35
  105.1 0.6 gather_fusion.1
  105.9 0.9 broadcast_select_fusion.refs_1_
  107.0 0.2 fusion.9
  107.2 0.7 fusion.19.refs_0_
  107.9 34.7 %shard_map.139 = (f32[40,256]{1,0:T(8,128)}, f32[16,256]{1,0:T(8,128)}) custom-call(bf16[40,256]{1,0:T(8,128)(2,1)} %fusion.19.refs_0_, bf16[16,16384]{1,0:T(8,128)(2,1)} %broadcast_select_fusion.refs_1_), custom_call_target="tpu_custom_call" | custom-call | tf_op jit(solution)/shard_map/pallas_call | solution.py:187
  142.6 1.3 fusion.30
  144.6 1.5 fusion.6
  146.0 1.2 slice_bitcast_fusion
  147.2 0.6 multiply_convert_fusion
  (44 shorter events, 1.3 us)
Async XLA Ops:
  34.0 4.6 %copy-start.2 = (s32[16,256]{1,0:T(8,128)S(1)}, s32[16,256]{1,0:T(8,128)}, u32[]{:S(2)}) copy-start(s32[16,256]{1,0:T(8,128)} %param.18) | copy-start | bytes 49156
  34.1 18.7 %copy-start.8 = (s32[64]{0:T(128)S(1)}, s32[64]{0:T(128)}, u32[]{:S(2)}) copy-start(s32[64]{0:T(128)} %param.17) | copy-start | bytes 772
  34.1 19.3 %copy-start.6 = (s32[256]{0:T(256)S(1)}, s32[256]{0:T(256)}, u32[]{:S(2)}) copy-start(s32[256]{0:T(256)} %param.19) | copy-start | bytes 3076
  38.6 16.3 %copy-start = (bf16[16,256]{1,0:T(8,128)(2,1)S(1)}, bf16[16,256]{1,0:T(8,128)(2,1)}, u32[]{:S(2)}) copy-start(bf16[16,256]{1,0:T(8,128)(2,1)} %param.14) | copy-start | bytes 24580
  38.6 16.3 %copy-start.4 = (bf16[16,256]{1,0:T(8,128)(2,1)S(1)}, bf16[16,256]{1,0:T(8,128)(2,1)}, u32[]{:S(2)}) copy-start(bf16[16,256]{1,0:T(8,128)(2,1)} %param.20) | copy-start | bytes 24580
  38.6 16.3 %copy-start.3 = (bf16[16,256]{1,0:T(8,128)(2,1)S(1)}, bf16[16,256]{1,0:T(8,128)(2,1)}, u32[]{:S(2)}) copy-start(bf16[16,256]{1,0:T(8,128)(2,1)} %param.21) | copy-start | bytes 24580
  38.6 16.3 %copy-start.5 = (bf16[32,256]{1,0:T(8,128)(2,1)S(1)}, bf16[32,256]{1,0:T(8,128)(2,1)}, u32[]{:S(2)}) copy-start(bf16[32,256]{1,0:T(8,128)(2,1)} %param.23) | copy-start | bytes 49156
  38.6 16.4 %copy-start.7 = (f32[32]{0:T(128)S(1)}, f32[32]{0:T(128)}, u32[]{:S(2)}) copy-start(f32[32]{0:T(128)} %param.22) | copy-start | bytes 388
  54.9 0.6 copy-start.1

commit v12 on v11

--- a/solution.py
+++ b/solution.py
@@ -120,7 +120,7 @@
     for e, plan in enumerate(plans):
         if specs[e][6] > 1:
             continue
-        for k in range(1, min(plan[1], 9)):
+        for k in range(1, min(plan[1], 3)):
             desc(plan, lax.rem(plan[12] + k, plan[1]), plan[12]).wait_send()
     for _, second in seconds:
         each_peer(second, lambda j, second=second: desc(second, j, second[12]).start())
@@ -134,7 +134,7 @@
             desc(plan, j, plan[12]).wait_send()
             return carry
 
-        lax.fori_loop(min(plan[1], 9), plan[1], finish, 0)
+        lax.fori_loop(min(plan[1], 3), plan[1], finish, 0)
 
         def arrive(j, plan=plan):
             desc(plan, j, j).wait_recv()

time: 149 us -> 149 us (level)
  no operation moved by 1% of the time
where the time goes in v12:
time: 149 us; the launch traced here: 148 us
  Pallas kernels  81.7 us (55%)
  other arithmetic  33.7 us (23%)
  local copies, waits for them, and re-layouts  26 us (17%)
  matrix products  4.16 us (3%)
  between operations  2.3 us (2%)
    pallas_call x3, Pallas kernels, exchange_many(): pl.pallas_call(functools.partial(exchange_kernel, tuple(specs)), out_shap...  81.7 us
    scatter-add x1, other arithmetic, per_device(): contrib = jnp.zeros((col_width, FRESH * part_rows), jnp.float32).at[:, co...  23.8 us
    gather x1, local copies, waits for them, and re-layouts, per_device(): gathered = sources[:, neighbours].astype(jnp.float32)  13.8 us
    reshape x1, local copies, waits for them, and re-layouts, per_device(): sources = blocks.transpose(1, 0, 2).reshape(col_width, n_dom * part_rows)  4.49 us

profile of v12, /device:TPU:1, one launch (start us, length us, event | category | flops | bytes accessed | tf_op | source)
XLA Modules:
  0.0 147.9 jit_solution(5172141449395919514)
XLA Ops:
  0.6 0.7 fusion.29
  1.6 0.7 compare_and_fusion
  2.3 0.6 dynamic_slice.19
  3.5 1.3 dynamic-slice_select_fusion.refs_0_
  4.8 29.2 %shard_map.137 = bf16[64,16,256]{2,1,0:T(8,128)(2,1)} custom-call(bf16[16,256]{1,0:T(8,128)(2,1)} %dynamic-slice_select_fusion.refs_0_), custom_call_target="tpu_custom_call" | custom-call | tf_op jit(solution)/shard_map/pallas_call | solution.py:187
  34.1 4.5 %copy.37 = bf16[16,64,256]{0,2,1:T(8,128)(2,1)} copy(bf16[16,64,256]{2,0,1:T(8,128)(2,1)} %bitcast.67) | data formatting | bytes 1048576 | tf_op jit(solution)/shard_map/reshape | solution.py:228
  38.6 0.3 select_reduce_fusion.1
  39.0 13.8 %gather_fusion = bf16[4096,16]{1,0:T(8,128)(2,1)S(1)} fusion(bf16[16,16384]{0,1:T(8,128)(2,1)} %bitcast.65, s32[4096]{0:T(1024)S(1)} %broadcast_clamp_fusion), kind=kCustom, calls=%fused_computation | custom fusion | bytes 278528 | tf_op jit(solution)/shard_map/gather | solution.py:234
  52.8 0.6 dynamic_slice.18
  53.4 0.6 convert_divide_fusion
  54.0 0.7 fusion
  54.9 0.6 scatter.6.refs_1_
  55.5 17.8 %shard_map.138 = (bf16[8,96,256]{2,1,0:T(8,128)(2,1)}, f32[8,8,128]{2,1,0:T(8,128)}) custom-call(bf16[96,256]{1,0:T(8,128)(2,1)} %copy-done.1, f32[8,128]{1,0:T(8,128)} %scatter.6.refs_1_), custom_call_target="tpu_custom_call" | custom-call | tf_op jit(solution)/shard_map/pallas_call | solution.py:187
  73.3 1.1 convolution_bitcast_fusion
  74.4 0.9 slice.69
  75.3 0.8 slice_reduce_fusion
  76.2 0.6 compare_convert_fusion.1
  76.9 1.2 fusion.13
  78.3 0.6 bitcast_multiply_fusion
  79.0 23.8 %scatter_custom_fusion = f32[16,4096]{0,1:T(8,128)} fusion(s32[4096]{0:T(1024)S(1)} %bitcast.74, f32[16,4096]{0,1:T(8,128)S(1)} %bitcast_multiply_fusion, f32[]{:T(128)} %constant.118.clone.1), kind=kCustom, calls=%fused_computation.5 | custom fusion | flops 65536 | bytes 2359300 | tf_op jit(solution)/shard_map/scatter-add | solution.py:289
  102.8 1.7 %convert_element_type.73 = bf16[16,4096]{0,1:T(8,128)(2,1)S(1)} convert(f32[16,4096]{0,1:T(8,128)} %scatter_custom_fusion) | non-fusion elementwise | flops 65536 | bytes 393216 | tf_op jit(solution)/shard_map/convert_element_type | solution.py:292
  104.5 0.2 concatenate.16
  104.7 0.3 copy.35
  105.1 0.6 gather_fusion.1
  105.8 0.9 broadcast_select_fusion.refs_1_
  107.0 0.2 fusion.9
  107.2 0.7 fusion.19.refs_0_
  107.8 34.7 %shard_map.139 = (f32[40,256]{1,0:T(8,128)}, f32[16,256]{1,0:T(8,128)}) custom-call(bf16[40,256]{1,0:T(8,128)(2,1)} %fusion.19.refs_0_, bf16[16,16384]{1,0:T(8,128)(2,1)} %broadcast_select_fusion.refs_1_), custom_call_target="tpu_custom_call" | custom-call | tf_op jit(solution)/shard_map/pallas_call | solution.py:187
  142.6 1.3 fusion.30
  144.6 1.5 fusion.6
  146.1 1.2 slice_bitcast_fusion
  147.2 0.6 multiply_convert_fusion
  (44 shorter events, 1.3 us)
Async XLA Ops:
  34.0 4.6 %copy-start.2 = (s32[16,256]{1,0:T(8,128)S(1)}, s32[16,256]{1,0:T(8,128)}, u32[]{:S(2)}) copy-start(s32[16,256]{1,0:T(8,128)} %param.18) | copy-start | bytes 49156
  34.1 18.7 %copy-start.8 = (s32[64]{0:T(128)S(1)}, s32[64]{0:T(128)}, u32[]{:S(2)}) copy-start(s32[64]{0:T(128)} %param.17) | copy-start | bytes 772
  34.1 19.3 %copy-start.6 = (s32[256]{0:T(256)S(1)}, s32[256]{0:T(256)}, u32[]{:S(2)}) copy-start(s32[256]{0:T(256)} %param.19) | copy-start | bytes 3076
  38.6 16.3 %copy-start = (bf16[16,256]{1,0:T(8,128)(2,1)S(1)}, bf16[16,256]{1,0:T(8,128)(2,1)}, u32[]{:S(2)}) copy-start(bf16[16,256]{1,0:T(8,128)(2,1)} %param.14) | copy-start | bytes 24580
  38.6 16.3 %copy-start.4 = (bf16[16,256]{1,0:T(8,128)(2,1)S(1)}, bf16[16,256]{1,0:T(8,128)(2,1)}, u32[]{:S(2)}) copy-start(bf16[16,256]{1,0:T(8,128)(2,1)} %param.20) | copy-start | bytes 24580
  38.6 16.3 %copy-start.3 = (bf16[16,256]{1,0:T(8,128)(2,1)S(1)}, bf16[16,256]{1,0:T(8,128)(2,1)}, u32[]{:S(2)}) copy-start(bf16[16,256]{1,0:T(8,128)(2,1)} %param.21) | copy-start | bytes 24580
  38.6 16.3 %copy-start.5 = (bf16[32,256]{1,0:T(8,128)(2,1)S(1)}, bf16[32,256]{1,0:T(8,128)(2,1)}, u32[]{:S(2)}) copy-start(bf16[32,256]{1,0:T(8,128)(2,1)} %param.23) | copy-start | bytes 49156
  38.6 16.4 %copy-start.7 = (f32[32]{0:T(128)S(1)}, f32[32]{0:T(128)}, u32[]{:S(2)}) copy-start(f32[32]{0:T(128)} %param.22) | copy-start | bytes 388
  54.9 0.6 copy-start.1

commit v13 on v9

--- a/solution.py
+++ b/solution.py
@@ -220,12 +220,14 @@
     my_index = lax.axis_index("dom")
     fresh_flag = (staleness >= LIMIT).astype(jnp.int32)
     my_fresh = fresh_flag[my_index]
-    own_cache = lax.dynamic_slice_in_dim(cached_embed, my_index * part_rows, part_rows, 1)
-    own_source = jnp.where(my_fresh == 1, features, own_cache)
     col_inputs = jnp.concatenate([features, w_self, w_nbr, cotangent], axis=0)
     bias_block = jnp.zeros((8, 128), jnp.float32).at[0, : sage_bias.shape[0]].set(sage_bias)
-    blocks = exchange(own_source, 0, "dom", n_dom, bcast=True)
-    sources = blocks.transpose(1, 0, 2).reshape(col_width, n_dom * part_rows)
+    blocks = exchange(features, 0, "dom", n_dom, bcast=True)
+    sources = jnp.where(
+        fresh_flag[None, :, None] == 1,
+        blocks.transpose(1, 0, 2),
+        cached_embed.reshape(col_width, n_dom, part_rows),
+    ).reshape(col_width, n_dom * part_rows)
     local_slot = jnp.arange(part_rows, dtype=jnp.int32)
     live_rows = (local_slot < node_counts[my_index]).astype(jnp.float32)
     slot_index = jnp.arange(slot_count, dtype=jnp.int32)
@@ -274,12 +276,10 @@
     own_term = jnp.dot(w_self, grad_full, preferred_element_type=jnp.float32)
     spread = weights[None, :, :] * grad_agg.astype(jnp.float32)[:, None, :]
     fresh_rank = jnp.cumsum(fresh_flag) - 1
-    nbr_part = neighbours // part_rows
-    compact = jnp.where(
-        fresh_flag[nbr_part] == 1,
-        fresh_rank[nbr_part] * part_rows + neighbours % part_rows,
-        FRESH * part_rows,
-    )
+    slot_base = jnp.where(fresh_flag == 1, fresh_rank * part_rows, -part_rows)
+    owner = (neighbours // part_rows)[:, :, None] == jnp.arange(n_dom, dtype=jnp.int32)
+    compact = jnp.sum(jnp.where(owner, slot_base, 0), axis=2) + neighbours % part_rows
+    compact = jnp.where(compact >= 0, compact, FRESH * part_rows)
     contrib = (
         jnp.zeros((col_width, FRESH * part_rows), jnp.float32)
         .at[:, compact.reshape(-1)]

time: 198 us -> 147 us (0.74)
  local copies, waits for them, and re-layouts: 75.4 us -> 24.6 us
    gather x2 -> x0, local copies, waits for them, and re-layouts: 49.4 us -> none  [the longest x1 24.7 us: per_device(): fresh_rank[nbr_part] * part_rows + neighbours % part_rows]
where the time goes in v13:
time: 147 us; the launch traced here: 146 us
  Pallas kernels  82.2 us (56%)
  other arithmetic  33.6 us (23%)
  local copies, waits for them, and re-layouts  24.6 us (17%)
  matrix products  4.19 us (3%)
  between operations  1.66 us (1%)
    pallas_call x3, Pallas kernels, exchange_many(): pl.pallas_call(functools.partial(exchange_kernel, tuple(specs)), out_shap...  82.2 us
    scatter-add x1, other arithmetic, per_device(): contrib = jnp.zeros((col_width, FRESH * part_rows), jnp.float32).at[:, co...  23.8 us
    gather x1, local copies, waits for them, and re-layouts, per_device(): gathered = sources[:, neighbours].astype(jnp.float32)  13.8 us
    reshape x1, local copies, waits for them, and re-layouts, per_device(): sources = jnp.where(fresh_flag[None, :, None] == 1, blocks.transpose(1, 0...  3.11 us

profile of v13, /device:TPU:1, one launch (start us, length us, event | category | flops | bytes accessed | tf_op | source)
XLA Modules:
  0.0 146.3 jit_solution(13129525328214271343)
XLA Ops:
  0.6 29.2 %shard_map.137 = bf16[64,16,256]{2,1,0:T(8,128)(2,1)} custom-call(bf16[16,256]{1,0:T(8,128)(2,1)} %refs_0_.1), custom_call_target="tpu_custom_call" | custom-call | tf_op jit(solution)/shard_map/pallas_call | solution.py:187
  29.8 0.7 fusion.28
  30.8 0.7 compare_and_fusion
  31.5 1.3 bitcast_select_fusion
  32.9 3.1 %copy.40 = bf16[16,64,256]{0,2,1:T(8,128)(2,1)} copy(bf16[16,64,256]{2,0,1:T(8,128)(2,1)S(1)} %bitcast_select_fusion) | data formatting | bytes 1048576 | tf_op jit(solution)/shard_map/reshape | solution.py:230
  36.0 0.2 select_reduce_fusion
  36.3 13.8 %gather_fusion = bf16[4096,16]{1,0:T(8,128)(2,1)S(1)} fusion(bf16[16,16384]{0,1:T(8,128)(2,1)} %bitcast.68, s32[4096]{0:T(1024)S(1)} %broadcast_clamp_fusion), kind=kCustom, calls=%fused_computation | custom fusion | bytes 278528 | tf_op jit(solution)/shard_map/gather | solution.py:236
  50.1 0.6 dynamic_slice.15
  50.7 0.6 convert_divide_fusion
  51.4 0.7 fusion
  52.3 0.6 scatter.6.refs_1_
  52.9 17.8 %shard_map.138 = (bf16[8,96,256]{2,1,0:T(8,128)(2,1)}, f32[8,8,128]{2,1,0:T(8,128)}) custom-call(bf16[96,256]{1,0:T(8,128)(2,1)} %copy-done.1, f32[8,128]{1,0:T(8,128)} %scatter.6.refs_1_), custom_call_target="tpu_custom_call" | custom-call | tf_op jit(solution)/shard_map/pallas_call | solution.py:187
  70.7 0.9 slice.69
  71.6 0.7 compare_convert_fusion.1
  72.3 0.8 slice_reduce_fusion
  73.2 1.1 convolution_bitcast_fusion
  74.2 1.2 fusion.13
  75.4 0.6 multiply_convert_fusion
  76.4 0.6 bitcast_multiply_fusion
  77.0 23.8 %scatter_custom_fusion = f32[16,4096]{0,1:T(8,128)} fusion(s32[4096]{0:T(1024)S(1)} %bitcast.77, f32[16,4096]{0,1:T(8,128)S(1)} %bitcast_multiply_fusion, f32[]{:T(128)} %constant.116.clone.1), kind=kCustom, calls=%fused_computation.5 | custom fusion | flops 65536 | bytes 2359300 | tf_op jit(solution)/shard_map/scatter-add | solution.py:286
  100.8 1.7 %convert_element_type.72 = bf16[16,4096]{0,1:T(8,128)(2,1)S(1)} convert(f32[16,4096]{0,1:T(8,128)} %scatter_custom_fusion) | non-fusion elementwise | flops 65536 | bytes 393216 | tf_op jit(solution)/shard_map/convert_element_type | solution.py:289
  102.5 0.2 concatenate.15
  102.7 0.3 copy.38
  103.1 0.6 gather_fusion.1
  103.8 0.9 broadcast_select_fusion.refs_0_
  105.0 0.2 fusion.9
  105.2 0.7 fusion.19.refs_1_
  105.8 35.2 %shard_map.139 = (f32[16,256]{1,0:T(8,128)}, f32[40,256]{1,0:T(8,128)}) custom-call(bf16[16,16384]{1,0:T(8,128)(2,1)} %broadcast_select_fusion.refs_0_, bf16[40,256]{1,0:T(8,128)(2,1)} %fusion.19.refs_1_), custom_call_target="tpu_custom_call" | custom-call | tf_op jit(solution)/shard_map/pallas_call | solution.py:187
  141.0 0.6 dynamic_slice.18
  142.3 1.5 %fusion.6 = bf16[16,256]{1,0:T(8,128)(2,1)} fusion(bf16[16,256]{1,0:T(8,128)(2,1)S(1)} %copy-done.4, bf16[256,256]{1,0:T(8,128)(2,1)S(1)} %get-tuple-element.39, f32[16,256]{1,0:T(8,128)} %get-tuple-element.35, f32[]{:T(128)} %bitcast.10), kind=kOutput, calls=%fused_computation.14 | convolution fusion | flops 2109440 | bytes 163844 | tf_op jit(solution)/shard_map/dot_general | solution.py:276
  143.7 1.3 fusion.29
  145.1 1.2 slice_bitcast_fusion
  (47 shorter events, 1.3 us)
Async XLA Ops:
  32.8 3.2 %copy-start.8 = (s32[64]{0:T(128)S(1)}, s32[64]{0:T(128)}, u32[]{:S(2)}) copy-start(s32[64]{0:T(128)} %param.16) | copy-start | bytes 772
  32.8 3.2 %copy-start.2 = (s32[16,256]{1,0:T(8,128)S(1)}, s32[16,256]{1,0:T(8,128)}, u32[]{:S(2)}) copy-start(s32[16,256]{1,0:T(8,128)} %param.18) | copy-start | bytes 49156
  32.8 17.3 %copy-start.9 = (s32[64]{0:T(128)S(1)}, s32[64]{0:T(128)}, u32[]{:S(2)}) copy-start(s32[64]{0:T(128)} %param.17) | copy-start | bytes 772
  32.8 17.9 %copy-start.6 = (s32[256]{0:T(256)S(1)}, s32[256]{0:T(256)}, u32[]{:S(2)}) copy-start(s32[256]{0:T(256)} %param.19) | copy-start | bytes 3076
  36.0 16.2 %copy-start = (bf16[16,256]{1,0:T(8,128)(2,1)S(1)}, bf16[16,256]{1,0:T(8,128)(2,1)}, u32[]{:S(2)}) copy-start(bf16[16,256]{1,0:T(8,128)(2,1)} %refs_0_.1) | copy-start | bytes 24580
  36.0 16.2 %copy-start.4 = (bf16[16,256]{1,0:T(8,128)(2,1)S(1)}, bf16[16,256]{1,0:T(8,128)(2,1)}, u32[]{:S(2)}) copy-start(bf16[16,256]{1,0:T(8,128)(2,1)} %param.20) | copy-start | bytes 24580
  36.0 16.3 %copy-start.3 = (bf16[16,256]{1,0:T(8,128)(2,1)S(1)}, bf16[16,256]{1,0:T(8,128)(2,1)}, u32[]{:S(2)}) copy-start(bf16[16,256]{1,0:T(8,128)(2,1)} %param.21) | copy-start | bytes 24580
  36.0 16.3 %copy-start.5 = (bf16[32,256]{1,0:T(8,128)(2,1)S(1)}, bf16[32,256]{1,0:T(8,128)(2,1)}, u32[]{:S(2)}) copy-start(bf16[32,256]{1,0:T(8,128)(2,1)} %param.23) | copy-start | bytes 49156
  36.0 16.3 %copy-start.7 = (f32[32]{0:T(128)S(1)}, f32[32]{0:T(128)}, u32[]{:S(2)}) copy-start(f32[32]{0:T(128)} %param.22) | copy-start | bytes 388
  52.3 0.6 copy-start.1

commit v14 on v13

--- a/solution.py
+++ b/solution.py
@@ -285,11 +285,9 @@
         .at[:, compact.reshape(-1)]
         .add(spread.reshape(col_width, -1), mode="drop")
     )
-    padded = jnp.concatenate(
-        [contrib.astype(jnp.bfloat16), jnp.zeros((col_width, part_rows), jnp.bfloat16)], axis=1
-    ).reshape(col_width, FRESH + 1, part_rows)
-    block_of = jnp.where(fresh_flag == 1, fresh_rank, FRESH)
-    contrib = jnp.take(padded, block_of, axis=1).reshape(col_width, n_dom * part_rows)
+    compact_blocks = contrib.astype(jnp.bfloat16).reshape(col_width, FRESH, part_rows)
+    block_of = jnp.clip(fresh_rank, 0, FRESH - 1)
+    contrib = jnp.take(compact_blocks, block_of, axis=1, mode="clip").reshape(col_width, n_dom * part_rows)
     ys = 8 if n_dom % 16 == 0 else 1
     first = ((2, 1), (n_dom // (2 * ys), 2 * ys))
     back, summed = exchange_many(

time: 147 us -> 146 us (level)
  other arithmetic: 33.6 us -> 32 us
where the time goes in v14:
time: 146 us; the launch traced here: 145 us
  Pallas kernels  82.2 us (56%)
  other arithmetic  32 us (22%)
  local copies, waits for them, and re-layouts  25.1 us (17%)
  matrix products  4.19 us (3%)
  between operations  1.63 us (1%)
    pallas_call x3, Pallas kernels, exchange_many(): pl.pallas_call(functools.partial(exchange_kernel, tuple(specs)), out_shap...  82.2 us
    scatter-add x1, other arithmetic, per_device(): contrib = jnp.zeros((col_width, FRESH * part_rows), jnp.float32).at[:, co...  23.8 us
    gather x1, local copies, waits for them, and re-layouts, per_device(): gathered = sources[:, neighbours].astype(jnp.float32)  13.8 us
    reshape x1, local copies, waits for them, and re-layouts, per_device(): sources = jnp.where(fresh_flag[None, :, None] == 1, blocks.transpose(1, 0...  3.11 us

profile of v14, /device:TPU:1, one launch (start us, length us, event | category | flops | bytes accessed | tf_op | source)
XLA Modules:
  0.0 145.2 jit_solution(3480476268307474977)
XLA Ops:
  0.6 29.2 %shard_map.137 = bf16[64,16,256]{2,1,0:T(8,128)(2,1)} custom-call(bf16[16,256]{1,0:T(8,128)(2,1)} %refs_0_.1), custom_call_target="tpu_custom_call" | custom-call | tf_op jit(solution)/shard_map/pallas_call | solution.py:187
  29.8 0.7 compare_convert_fusion
  30.5 1.3 bitcast_select_fusion
  31.9 3.1 %copy.40 = bf16[16,64,256]{0,2,1:T(8,128)(2,1)} copy(bf16[16,64,256]{2,0,1:T(8,128)(2,1)S(1)} %bitcast_select_fusion) | data formatting | bytes 1048576 | tf_op jit(solution)/shard_map/reshape | solution.py:230
  35.4 0.2 select_reduce_fusion
  35.7 13.8 %gather_fusion = bf16[4096,16]{1,0:T(8,128)(2,1)S(1)} fusion(bf16[16,16384]{0,1:T(8,128)(2,1)} %bitcast.68, s32[4096]{0:T(1024)S(1)} %broadcast_clamp_fusion), kind=kCustom, calls=%fused_computation | custom fusion | bytes 278528 | tf_op jit(solution)/shard_map/gather | solution.py:236
  49.5 0.6 dynamic_slice.15
  50.0 0.6 convert_divide_fusion
  50.7 0.7 fusion
  51.6 0.6 scatter.6.refs_1_
  52.2 17.8 %shard_map.138 = (bf16[8,96,256]{2,1,0:T(8,128)(2,1)}, f32[8,8,128]{2,1,0:T(8,128)}) custom-call(bf16[96,256]{1,0:T(8,128)(2,1)} %copy-done.1, f32[8,128]{1,0:T(8,128)} %scatter.6.refs_1_), custom_call_target="tpu_custom_call" | custom-call | tf_op jit(solution)/shard_map/pallas_call | solution.py:187
  70.1 0.9 slice.69
  71.0 0.7 compare_convert_fusion.1
  71.6 0.8 slice_reduce_fusion
  72.5 1.1 convolution_bitcast_fusion
  73.6 1.2 fusion.13
  74.8 0.6 multiply_convert_fusion
  75.4 0.1 fusion.8
  75.7 0.6 bitcast_multiply_fusion
  76.3 23.8 %scatter_custom_fusion = f32[16,4096]{0,1:T(8,128)} fusion(s32[4096]{0:T(1024)S(1)} %bitcast.77, f32[16,4096]{0,1:T(8,128)S(1)} %bitcast_multiply_fusion, f32[]{:T(128)} %constant.103.clone.1), kind=kCustom, calls=%fused_computation.5 | custom fusion | flops 65536 | bytes 2359300 | tf_op jit(solution)/shard_map/scatter-add | solution.py:286
  100.1 1.7 %convert_element_type.72 = bf16[16,4096]{0,1:T(8,128)(2,1)S(1)} convert(f32[16,4096]{0,1:T(8,128)} %scatter_custom_fusion) | non-fusion elementwise | flops 65536 | bytes 393216 | tf_op jit(solution)/shard_map/convert_element_type | solution.py:288
  101.8 0.3 copy.38
  102.2 0.6 gather_fusion.1
  102.8 0.8 copy.43
  103.7 0.2 convolution_convert_fusion.1
  103.9 0.2 fusion.9
  104.0 0.7 fusion.19.refs_1_
  104.7 35.2 %shard_map.139 = (f32[16,256]{1,0:T(8,128)}, f32[40,256]{1,0:T(8,128)}) custom-call(bf16[16,16384]{1,0:T(8,128)(2,1)} %bitcast.70, bf16[40,256]{1,0:T(8,128)(2,1)} %fusion.19.refs_1_), custom_call_target="tpu_custom_call" | custom-call | tf_op jit(solution)/shard_map/pallas_call | solution.py:187
  139.9 0.6 dynamic_slice.18
  141.1 1.5 %fusion.6 = bf16[16,256]{1,0:T(8,128)(2,1)} fusion(bf16[16,256]{1,0:T(8,128)(2,1)S(1)} %copy-done.4, bf16[256,256]{1,0:T(8,128)(2,1)S(1)} %get-tuple-element.39, f32[16,256]{1,0:T(8,128)} %get-tuple-element.35, f32[]{:T(128)} %bitcast.10), kind=kOutput, calls=%fused_computation.14 | convolution fusion | flops 2109440 | bytes 163844 | tf_op jit(solution)/shard_map/dot_general | solution.py:276
  142.6 1.3 fusion.29
  144.0 1.2 slice_bitcast_fusion
  (42 shorter events, 0.9 us)
Async XLA Ops:
  31.8 3.5 %copy-start.8 = (s32[64]{0:T(128)S(1)}, s32[64]{0:T(128)}, u32[]{:S(2)}) copy-start(s32[64]{0:T(128)} %param.16) | copy-start | bytes 772
  31.8 3.5 %copy-start.2 = (s32[16,256]{1,0:T(8,128)S(1)}, s32[16,256]{1,0:T(8,128)}, u32[]{:S(2)}) copy-start(s32[16,256]{1,0:T(8,128)} %param.18) | copy-start | bytes 49156
  31.9 17.6 %copy-start.9 = (s32[64]{0:T(128)S(1)}, s32[64]{0:T(128)}, u32[]{:S(2)}) copy-start(s32[64]{0:T(128)} %param.17) | copy-start | bytes 772
  31.9 18.2 %copy-start.6 = (s32[256]{0:T(256)S(1)}, s32[256]{0:T(256)}, u32[]{:S(2)}) copy-start(s32[256]{0:T(256)} %param.19) | copy-start | bytes 3076
  35.0 16.5 %copy-start = (bf16[16,256]{1,0:T(8,128)(2,1)S(1)}, bf16[16,256]{1,0:T(8,128)(2,1)}, u32[]{:S(2)}) copy-start(bf16[16,256]{1,0:T(8,128)(2,1)} %refs_0_.1) | copy-start | bytes 24580
  35.0 16.5 %copy-start.4 = (bf16[16,256]{1,0:T(8,128)(2,1)S(1)}, bf16[16,256]{1,0:T(8,128)(2,1)}, u32[]{:S(2)}) copy-start(bf16[16,256]{1,0:T(8,128)(2,1)} %param.20) | copy-start | bytes 24580
  35.0 16.6 %copy-start.3 = (bf16[16,256]{1,0:T(8,128)(2,1)S(1)}, bf16[16,256]{1,0:T(8,128)(2,1)}, u32[]{:S(2)}) copy-start(bf16[16,256]{1,0:T(8,128)(2,1)} %param.21) | copy-start | bytes 24580
  35.0 16.6 %copy-start.5 = (bf16[32,256]{1,0:T(8,128)(2,1)S(1)}, bf16[32,256]{1,0:T(8,128)(2,1)}, u32[]{:S(2)}) copy-start(bf16[32,256]{1,0:T(8,128)(2,1)} %param.23) | copy-start | bytes 49156
  35.0 16.6 %copy-start.7 = (f32[32]{0:T(128)S(1)}, f32[32]{0:T(128)}, u32[]{:S(2)}) copy-start(f32[32]{0:T(128)} %param.22) | copy-start | bytes 388
  51.6 0.6 copy-start.1

commit v15 on v14

--- a/solution.py
+++ b/solution.py
@@ -221,7 +221,7 @@
     fresh_flag = (staleness >= LIMIT).astype(jnp.int32)
     my_fresh = fresh_flag[my_index]
     col_inputs = jnp.concatenate([features, w_self, w_nbr, cotangent], axis=0)
-    bias_block = jnp.zeros((8, 128), jnp.float32).at[0, : sage_bias.shape[0]].set(sage_bias)
+    bias_block = sage_bias.reshape(1, -1)
     blocks = exchange(features, 0, "dom", n_dom, bcast=True)
     sources = jnp.where(
         fresh_flag[None, :, None] == 1,
@@ -248,7 +248,7 @@
     w_self_full = col_blocks[:, col_width : 2 * col_width].reshape(n_col * col_width, hidden)
     w_nbr_full = col_blocks[:, 2 * col_width : 3 * col_width].reshape(n_col * col_width, hidden)
     cot_full = col_blocks[:, 3 * col_width :].reshape(hidden, part_rows)
-    bias_full = bias_blocks[:, 0, : sage_bias.shape[0]].reshape(hidden)
+    bias_full = bias_blocks.reshape(hidden)
     pre_full = (
         left_product(w_self_full, feat_full)
         + left_product(w_nbr_full, agg_full)

time: 146 us -> 147 us (level)
  no operation moved by 1% of the time
where the time goes in v15:
time: 147 us; the launch traced here: 146 us
  Pallas kernels  81.8 us (56%)
  other arithmetic  33.4 us (23%)
  local copies, waits for them, and re-layouts  24.8 us (17%)
  matrix products  4.19 us (3%)
  between operations  1.62 us (1%)
    pallas_call x3, Pallas kernels, exchange_many(): pl.pallas_call(functools.partial(exchange_kernel, tuple(specs)), out_shap...  81.8 us
    scatter-add x1, other arithmetic, per_device(): contrib = jnp.zeros((col_width, FRESH * part_rows), jnp.float32).at[:, co...  23.8 us
    gather x1, local copies, waits for them, and re-layouts, per_device(): gathered = sources[:, neighbours].astype(jnp.float32)  13.8 us
    reshape x1, local copies, waits for them, and re-layouts, per_device(): sources = jnp.where(fresh_flag[None, :, None] == 1, blocks.transpose(1, 0...  3.11 us

profile of v15, /device:TPU:1, one launch (start us, length us, event | category | flops | bytes accessed | tf_op | source)
XLA Modules:
  0.0 145.8 jit_solution(12203980299591003269)
XLA Ops:
  0.6 29.2 %shard_map.137 = bf16[64,16,256]{2,1,0:T(8,128)(2,1)} custom-call(bf16[16,256]{1,0:T(8,128)(2,1)} %refs_0_.1), custom_call_target="tpu_custom_call" | custom-call | tf_op jit(solution)/shard_map/pallas_call | solution.py:187
  29.8 0.7 compare_convert_fusion
  30.5 1.3 bitcast_select_fusion
  31.9 3.1 %copy.40 = bf16[16,64,256]{0,2,1:T(8,128)(2,1)} copy(bf16[16,64,256]{2,0,1:T(8,128)(2,1)S(1)} %bitcast_select_fusion) | data formatting | bytes 1048576 | tf_op jit(solution)/shard_map/reshape | solution.py:230
  35.4 0.2 select_reduce_fusion
  35.7 13.8 %gather_fusion = bf16[4096,16]{1,0:T(8,128)(2,1)S(1)} fusion(bf16[16,16384]{0,1:T(8,128)(2,1)} %bitcast.68, s32[4096]{0:T(1024)S(1)} %broadcast_clamp_fusion), kind=kCustom, calls=%fused_computation | custom fusion | bytes 278528 | tf_op jit(solution)/shard_map/gather | solution.py:236
  49.4 0.6 dynamic_slice.15
  50.0 0.6 convert_divide_fusion
  50.7 0.7 fusion
  51.6 0.6 copy-done.1
  52.2 17.4 %shard_map.138 = (bf16[8,96,256]{2,1,0:T(8,128)(2,1)}, f32[8,1,32]{2,1,0:T(1,128)}) custom-call(bf16[96,256]{1,0:T(8,128)(2,1)} %copy-done.1, f32[1,32]{1,0:T(1,128)} %bitcast.79), custom_call_target="tpu_custom_call" | custom-call | tf_op jit(solution)/shard_map/pallas_call | solution.py:187
  69.6 0.9 slice.49
  70.5 0.7 compare_convert_fusion.1
  71.2 0.5 broadcast.172
  71.7 1.3 reduce.13
  73.1 1.1 convolution_bitcast_fusion
  74.2 1.2 fusion.13
  75.4 0.6 multiply_convert_fusion
  76.3 0.6 bitcast_multiply_fusion
  76.9 23.8 %scatter_custom_fusion = f32[16,4096]{0,1:T(8,128)} fusion(s32[4096]{0:T(1024)S(1)} %bitcast.77, f32[16,4096]{0,1:T(8,128)S(1)} %bitcast_multiply_fusion, f32[]{:T(128)} %constant.81.clone.1), kind=kCustom, calls=%fused_computation.5 | custom fusion | flops 65536 | bytes 2359300 | tf_op jit(solution)/shard_map/scatter-add | solution.py:286
  100.8 1.7 %convert_element_type.72 = bf16[16,4096]{0,1:T(8,128)(2,1)S(1)} convert(f32[16,4096]{0,1:T(8,128)} %scatter_custom_fusion) | non-fusion elementwise | flops 65536 | bytes 393216 | tf_op jit(solution)/shard_map/convert_element_type | solution.py:288
  102.5 0.3 copy.38
  102.8 0.6 gather_fusion.1
  103.4 0.8 copy.43
  104.3 0.2 convolution_convert_fusion.1
  104.5 0.2 fusion.9
  104.7 0.7 fusion.19.refs_1_
  105.3 35.2 %shard_map.139 = (f32[16,256]{1,0:T(8,128)}, f32[40,256]{1,0:T(8,128)}) custom-call(bf16[16,16384]{1,0:T(8,128)(2,1)} %bitcast.70, bf16[40,256]{1,0:T(8,128)(2,1)} %fusion.19.refs_1_), custom_call_target="tpu_custom_call" | custom-call | tf_op jit(solution)/shard_map/pallas_call | solution.py:187
  140.6 0.6 dynamic_slice.18
  141.8 1.5 %fusion.6 = bf16[16,256]{1,0:T(8,128)(2,1)} fusion(bf16[16,256]{1,0:T(8,128)(2,1)S(1)} %copy-done.4, bf16[256,256]{1,0:T(8,128)(2,1)S(1)} %get-tuple-element.27, f32[16,256]{1,0:T(8,128)} %get-tuple-element.23, f32[]{:T(128)} %bitcast.10), kind=kOutput, calls=%fused_computation.14 | convolution fusion | flops 2109440 | bytes 163844 | tf_op jit(solution)/shard_map/dot_general | solution.py:276
  143.3 1.3 fusion.29
  144.6 1.2 slice_bitcast_fusion
  (40 shorter events, 1.0 us)
Async XLA Ops:
  31.8 3.5 %copy-start.7 = (s32[64]{0:T(128)S(1)}, s32[64]{0:T(128)}, u32[]{:S(2)}) copy-start(s32[64]{0:T(128)} %param.14) | copy-start | bytes 772
  31.8 3.5 %copy-start.2 = (s32[16,256]{1,0:T(8,128)S(1)}, s32[16,256]{1,0:T(8,128)}, u32[]{:S(2)}) copy-start(s32[16,256]{1,0:T(8,128)} %param.16) | copy-start | bytes 49156
  31.9 17.6 %copy-start.8 = (s32[64]{0:T(128)S(1)}, s32[64]{0:T(128)}, u32[]{:S(2)}) copy-start(s32[64]{0:T(128)} %param.15) | copy-start | bytes 772
  31.9 18.2 %copy-start.6 = (s32[256]{0:T(256)S(1)}, s32[256]{0:T(256)}, u32[]{:S(2)}) copy-start(s32[256]{0:T(256)} %param.17) | copy-start | bytes 3076
  35.0 16.5 %copy-start = (bf16[16,256]{1,0:T(8,128)(2,1)S(1)}, bf16[16,256]{1,0:T(8,128)(2,1)}, u32[]{:S(2)}) copy-start(bf16[16,256]{1,0:T(8,128)(2,1)} %refs_0_.1) | copy-start | bytes 24580
  35.0 16.5 %copy-start.4 = (bf16[16,256]{1,0:T(8,128)(2,1)S(1)}, bf16[16,256]{1,0:T(8,128)(2,1)}, u32[]{:S(2)}) copy-start(bf16[16,256]{1,0:T(8,128)(2,1)} %param.18) | copy-start | bytes 24580
  35.0 16.5 %copy-start.3 = (bf16[16,256]{1,0:T(8,128)(2,1)S(1)}, bf16[16,256]{1,0:T(8,128)(2,1)}, u32[]{:S(2)}) copy-start(bf16[16,256]{1,0:T(8,128)(2,1)} %param.19) | copy-start | bytes 24580
  35.0 16.6 %copy-start.5 = (bf16[32,256]{1,0:T(8,128)(2,1)S(1)}, bf16[32,256]{1,0:T(8,128)(2,1)}, u32[]{:S(2)}) copy-start(bf16[32,256]{1,0:T(8,128)(2,1)} %param.21) | copy-start | bytes 49156
  51.6 0.6 copy-start.1

commit v16 on v14

--- a/solution.py
+++ b/solution.py
@@ -285,9 +285,10 @@
         .at[:, compact.reshape(-1)]
         .add(spread.reshape(col_width, -1), mode="drop")
     )
-    compact_blocks = contrib.astype(jnp.bfloat16).reshape(col_width, FRESH, part_rows)
+    compact_blocks = contrib.reshape(col_width, FRESH, part_rows)
     block_of = jnp.clip(fresh_rank, 0, FRESH - 1)
-    contrib = jnp.take(compact_blocks, block_of, axis=1, mode="clip").reshape(col_width, n_dom * part_rows)
+    contrib = jnp.take(compact_blocks, block_of, axis=1, mode="clip").astype(jnp.bfloat16)
+    contrib = contrib.reshape(col_width, n_dom * part_rows)
     ys = 8 if n_dom % 16 == 0 else 1
     first = ((2, 1), (n_dom // (2 * ys), 2 * ys))
     back, summed = exchange_many(

time: 146 us -> 146 us (level)
  other arithmetic: 32 us -> 30.4 us
  local copies, waits for them, and re-layouts: 25.1 us -> 26.6 us
    convert_element_type x1 -> x0, other arithmetic: 1.69 us -> none  [per_device(): contrib.astype(jnp.bfloat16).reshape(col_width, FRESH, part_rows)]
where the time goes in v16:
time: 146 us; the launch traced here: 145 us
  Pallas kernels  82.2 us (56%)
  other arithmetic  30.4 us (21%)
  local copies, waits for them, and re-layouts  26.6 us (18%)
  matrix products  4.19 us (3%)
  between operations  1.63 us (1%)
    pallas_call x3, Pallas kernels, exchange_many(): pl.pallas_call(functools.partial(exchange_kernel, tuple(specs)), out_shap...  82.2 us
    scatter-add x1, other arithmetic, per_device(): contrib = jnp.zeros((col_width, FRESH * part_rows), jnp.float32).at[:, co...  23.8 us
    gather x1, local copies, waits for them, and re-layouts, per_device(): gathered = sources[:, neighbours].astype(jnp.float32)  13.8 us
    reshape x1, local copies, waits for them, and re-layouts, per_device(): sources = jnp.where(fresh_flag[None, :, None] == 1, blocks.transpose(1, 0...  3.11 us

profile of v16, /device:TPU:1, one launch (start us, length us, event | category | flops | bytes accessed | tf_op | source)
XLA Modules:
  0.0 145.0 jit_solution(3092570791668953176)
XLA Ops:
  0.6 29.2 %shard_map.137 = bf16[64,16,256]{2,1,0:T(8,128)(2,1)} custom-call(bf16[16,256]{1,0:T(8,128)(2,1)} %refs_0_.1), custom_call_target="tpu_custom_call" | custom-call | tf_op jit(solution)/shard_map/pallas_call | solution.py:187
  29.8 0.7 compare_convert_fusion
  30.5 1.3 bitcast_select_fusion
  31.9 3.1 %copy.40 = bf16[16,64,256]{0,2,1:T(8,128)(2,1)} copy(bf16[16,64,256]{2,0,1:T(8,128)(2,1)S(1)} %bitcast_select_fusion) | data formatting | bytes 1048576 | tf_op jit(solution)/shard_map/reshape | solution.py:230
  35.2 0.1 clamp_reduce_fusion
  35.4 0.2 select_reduce_fusion
  35.7 13.8 %gather_fusion = bf16[4096,16]{1,0:T(8,128)(2,1)S(1)} fusion(bf16[16,16384]{0,1:T(8,128)(2,1)} %bitcast.71, s32[4096]{0:T(1024)S(1)} %broadcast_clamp_fusion), kind=kCustom, calls=%fused_computation | custom fusion | bytes 278528 | tf_op jit(solution)/shard_map/gather | solution.py:236
  49.5 0.6 dynamic_slice.15
  50.0 0.6 convert_divide_fusion
  50.7 0.7 fusion
  51.6 0.6 scatter.6.refs_1_
  52.2 17.8 %shard_map.138 = (bf16[8,96,256]{2,1,0:T(8,128)(2,1)}, f32[8,8,128]{2,1,0:T(8,128)}) custom-call(bf16[96,256]{1,0:T(8,128)(2,1)} %copy-done.1, f32[8,128]{1,0:T(8,128)} %scatter.6.refs_1_), custom_call_target="tpu_custom_call" | custom-call | tf_op jit(solution)/shard_map/pallas_call | solution.py:187
  70.1 0.9 slice.69
  71.0 0.7 compare_convert_fusion.1
  71.6 0.8 slice_reduce_fusion
  72.5 1.1 convolution_bitcast_fusion
  73.6 1.2 fusion.13
  74.8 0.6 multiply_convert_fusion
  75.4 0.1 fusion.8
  75.7 0.6 bitcast_multiply_fusion
  76.3 23.8 %scatter_custom_fusion = f32[16,4096]{0,1:T(8,128)} fusion(s32[4096]{0:T(1024)S(1)} %bitcast.79, f32[16,4096]{0,1:T(8,128)S(1)} %bitcast_multiply_fusion, f32[]{:T(128)} %constant.103.clone.1), kind=kCustom, calls=%fused_computation.5 | custom fusion | flops 65536 | bytes 2359300 | tf_op jit(solution)/shard_map/scatter-add | solution.py:286
  100.1 1.9 %copy.38 = bf16[16,16,256]{2,0,1:T(8,128)(2,1)S(1)} copy(f32[16,16,256]{0,2,1:T(8,128)} %bitcast.70) | data formatting | bytes 393216 | tf_op jit(solution)/shard_map/reshape | solution.py:288
  102.0 0.6 gather_fusion.1
  102.6 0.8 copy.43
  103.6 0.2 convolution_convert_fusion.1
  103.7 0.2 fusion.9
  103.9 0.7 fusion.19.refs_1_
  104.6 35.2 %shard_map.139 = (f32[16,256]{1,0:T(8,128)}, f32[40,256]{1,0:T(8,128)}) custom-call(bf16[16,16384]{1,0:T(8,128)(2,1)} %bitcast.72, bf16[40,256]{1,0:T(8,128)(2,1)} %fusion.19.refs_1_), custom_call_target="tpu_custom_call" | custom-call | tf_op jit(solution)/shard_map/pallas_call | solution.py:187
  139.8 0.6 dynamic_slice.18
  141.0 1.5 %fusion.6 = bf16[16,256]{1,0:T(8,128)(2,1)} fusion(bf16[16,256]{1,0:T(8,128)(2,1)S(1)} %copy-done.4, bf16[256,256]{1,0:T(8,128)(2,1)S(1)} %get-tuple-element.39, f32[16,256]{1,0:T(8,128)} %get-tuple-element.35, f32[]{:T(128)} %bitcast.10), kind=kOutput, calls=%fused_computation.14 | convolution fusion | flops 2109440 | bytes 163844 | tf_op jit(solution)/shard_map/dot_general | solution.py:276
  142.5 1.3 fusion.29
  143.8 1.2 slice_bitcast_fusion
  (41 shorter events, 0.7 us)
Async XLA Ops:
  31.8 3.5 %copy-start.8 = (s32[64]{0:T(128)S(1)}, s32[64]{0:T(128)}, u32[]{:S(2)}) copy-start(s32[64]{0:T(128)} %param.16) | copy-start | bytes 772
  31.8 3.5 %copy-start.2 = (s32[16,256]{1,0:T(8,128)S(1)}, s32[16,256]{1,0:T(8,128)}, u32[]{:S(2)}) copy-start(s32[16,256]{1,0:T(8,128)} %param.18) | copy-start | bytes 49156
  31.9 17.6 %copy-start.9 = (s32[64]{0:T(128)S(1)}, s32[64]{0:T(128)}, u32[]{:S(2)}) copy-start(s32[64]{0:T(128)} %param.17) | copy-start | bytes 772
  31.9 18.2 %copy-start.6 = (s32[256]{0:T(256)S(1)}, s32[256]{0:T(256)}, u32[]{:S(2)}) copy-start(s32[256]{0:T(256)} %param.19) | copy-start | bytes 3076
  35.0 16.5 %copy-start = (bf16[16,256]{1,0:T(8,128)(2,1)S(1)}, bf16[16,256]{1,0:T(8,128)(2,1)}, u32[]{:S(2)}) copy-start(bf16[16,256]{1,0:T(8,128)(2,1)} %refs_0_.1) | copy-start | bytes 24580
  35.0 16.5 %copy-start.4 = (bf16[16,256]{1,0:T(8,128)(2,1)S(1)}, bf16[16,256]{1,0:T(8,128)(2,1)}, u32[]{:S(2)}) copy-start(bf16[16,256]{1,0:T(8,128)(2,1)} %param.20) | copy-start | bytes 24580
  35.0 16.6 %copy-start.3 = (bf16[16,256]{1,0:T(8,128)(2,1)S(1)}, bf16[16,256]{1,0:T(8,128)(2,1)}, u32[]{:S(2)}) copy-start(bf16[16,256]{1,0:T(8,128)(2,1)} %param.21) | copy-start | bytes 24580
  35.0 16.6 %copy-start.5 = (bf16[32,256]{1,0:T(8,128)(2,1)S(1)}, bf16[32,256]{1,0:T(8,128)(2,1)}, u32[]{:S(2)}) copy-start(bf16[32,256]{1,0:T(8,128)(2,1)} %param.23) | copy-start | bytes 49156
  35.0 16.6 %copy-start.7 = (f32[32]{0:T(128)S(1)}, f32[32]{0:T(128)}, u32[]{:S(2)}) copy-start(f32[32]{0:T(128)} %param.22) | copy-start | bytes 388
  51.6 0.6 copy-start.1

commit v17 on v14

--- a/solution.py
+++ b/solution.py
@@ -219,7 +219,7 @@
     hidden = w_self.shape[1]
     my_index = lax.axis_index("dom")
     fresh_flag = (staleness >= LIMIT).astype(jnp.int32)
-    my_fresh = fresh_flag[my_index]
+    my_fresh = jnp.sum(jnp.where(jnp.arange(n_dom) == my_index, fresh_flag, 0))
     col_inputs = jnp.concatenate([features, w_self, w_nbr, cotangent], axis=0)
     bias_block = jnp.zeros((8, 128), jnp.float32).at[0, : sage_bias.shape[0]].set(sage_bias)
     blocks = exchange(features, 0, "dom", n_dom, bcast=True)

time: 146 us -> 146 us (level)
  no operation moved by 1% of the time
where the time goes in v17:
time: 146 us; the launch traced here: 145 us
  Pallas kernels  82.2 us (56%)
  other arithmetic  32.7 us (22%)
  local copies, waits for them, and re-layouts  24.5 us (17%)
  matrix products  4.19 us (3%)
  between operations  1.61 us (1%)
    pallas_call x3, Pallas kernels, exchange_many(): pl.pallas_call(functools.partial(exchange_kernel, tuple(specs)), out_shap...  82.2 us
    scatter-add x1, other arithmetic, per_device(): contrib = jnp.zeros((col_width, FRESH * part_rows), jnp.float32).at[:, co...  23.8 us
    gather x1, local copies, waits for them, and re-layouts, per_device(): gathered = sources[:, neighbours].astype(jnp.float32)  13.8 us
    reshape x1, local copies, waits for them, and re-layouts, per_device(): sources = jnp.where(fresh_flag[None, :, None] == 1, blocks.transpose(1, 0...  3.11 us

profile of v17, /device:TPU:1, one launch (start us, length us, event | category | flops | bytes accessed | tf_op | source)
XLA Modules:
  0.0 145.2 jit_solution(5995021847654169524)
XLA Ops:
  0.6 29.2 %shard_map.137 = bf16[64,16,256]{2,1,0:T(8,128)(2,1)} custom-call(bf16[16,256]{1,0:T(8,128)(2,1)} %refs_0_.1), custom_call_target="tpu_custom_call" | custom-call | tf_op jit(solution)/shard_map/pallas_call | solution.py:187
  29.8 0.7 fusion.29
  30.5 1.3 bitcast_select_fusion
  31.9 3.1 %copy.40 = bf16[16,64,256]{0,2,1:T(8,128)(2,1)} copy(bf16[16,64,256]{2,0,1:T(8,128)(2,1)S(1)} %bitcast_select_fusion) | data formatting | bytes 1048576 | tf_op jit(solution)/shard_map/reshape | solution.py:230
  35.3 0.6 fusion.28
  36.0 0.2 select_reduce_fusion
  36.3 13.8 %gather_fusion = bf16[4096,16]{1,0:T(8,128)(2,1)S(1)} fusion(bf16[16,16384]{0,1:T(8,128)(2,1)} %bitcast.67, s32[4096]{0:T(1024)S(1)} %broadcast_clamp_fusion), kind=kCustom, calls=%fused_computation | custom fusion | bytes 278528 | tf_op jit(solution)/shard_map/gather | solution.py:236
  50.1 0.6 dynamic_slice.12
  50.7 0.6 convert_divide_fusion
  51.3 0.7 fusion
  52.2 0.6 scatter.6.refs_1_
  52.8 17.8 %shard_map.138 = (bf16[8,96,256]{2,1,0:T(8,128)(2,1)}, f32[8,8,128]{2,1,0:T(8,128)}) custom-call(bf16[96,256]{1,0:T(8,128)(2,1)} %copy-done.1, f32[8,128]{1,0:T(8,128)} %scatter.6.refs_1_), custom_call_target="tpu_custom_call" | custom-call | tf_op jit(solution)/shard_map/pallas_call | solution.py:187
  70.6 0.9 slice.69
  71.6 0.7 compare_convert_fusion.1
  72.2 0.8 slice_reduce_fusion
  73.1 1.1 convolution_bitcast_fusion
  74.2 1.2 fusion.13
  75.4 0.6 multiply_convert_fusion
  76.0 0.1 fusion.8
  76.3 0.6 bitcast_multiply_fusion
  76.9 23.8 %scatter_custom_fusion = f32[16,4096]{0,1:T(8,128)} fusion(s32[4096]{0:T(1024)S(1)} %bitcast.76, f32[16,4096]{0,1:T(8,128)S(1)} %bitcast_multiply_fusion, f32[]{:T(128)} %constant.103.clone.1), kind=kCustom, calls=%fused_computation.5 | custom fusion | flops 65536 | bytes 2359300 | tf_op jit(solution)/shard_map/scatter-add | solution.py:286
  100.7 1.7 %convert_element_type.68 = bf16[16,4096]{0,1:T(8,128)(2,1)S(1)} convert(f32[16,4096]{0,1:T(8,128)} %scatter_custom_fusion) | non-fusion elementwise | flops 65536 | bytes 393216 | tf_op jit(solution)/shard_map/convert_element_type | solution.py:288
  102.4 0.3 copy.38
  102.8 0.6 gather_fusion.1
  103.4 0.8 copy.43
  104.3 0.2 convolution_convert_fusion.1
  104.4 0.2 fusion.9
  104.6 0.7 fusion.19.refs_1_
  105.3 35.2 %shard_map.139 = (f32[16,256]{1,0:T(8,128)}, f32[40,256]{1,0:T(8,128)}) custom-call(bf16[16,16384]{1,0:T(8,128)(2,1)} %bitcast.69, bf16[40,256]{1,0:T(8,128)(2,1)} %fusion.19.refs_1_), custom_call_target="tpu_custom_call" | custom-call | tf_op jit(solution)/shard_map/pallas_call | solution.py:187
  141.2 1.5 %fusion.6 = bf16[16,256]{1,0:T(8,128)(2,1)} fusion(bf16[16,256]{1,0:T(8,128)(2,1)S(1)} %copy-done.4, bf16[256,256]{1,0:T(8,128)(2,1)S(1)} %get-tuple-element.39, f32[16,256]{1,0:T(8,128)} %get-tuple-element.35, f32[]{:T(128)S(6)} %convert_element_type.64), kind=kOutput, calls=%fused_computation.14 | convolution fusion | flops 2109440 | bytes 163844 | tf_op jit(solution)/shard_map/dot_general | solution.py:276
  142.6 1.3 fusion.30
  144.0 1.2 slice_bitcast_fusion
  (41 shorter events, 0.9 us)
Async XLA Ops:
  31.8 3.5 %copy-start.7 = (s32[64]{0:T(128)S(1)}, s32[64]{0:T(128)}, u32[]{:S(2)}) copy-start(s32[64]{0:T(128)} %param.16) | copy-start | bytes 772
  31.8 4.1 %copy-start.2 = (s32[16,256]{1,0:T(8,128)S(1)}, s32[16,256]{1,0:T(8,128)}, u32[]{:S(2)}) copy-start(s32[16,256]{1,0:T(8,128)} %param.18) | copy-start | bytes 49156
  31.9 18.2 %copy-start.9 = (s32[64]{0:T(128)S(1)}, s32[64]{0:T(128)}, u32[]{:S(2)}) copy-start(s32[64]{0:T(128)} %param.17) | copy-start | bytes 772
  31.9 18.8 %copy-start.6 = (s32[256]{0:T(256)S(1)}, s32[256]{0:T(256)}, u32[]{:S(2)}) copy-start(s32[256]{0:T(256)} %param.19) | copy-start | bytes 3076
  35.0 17.1 %copy-start = (bf16[16,256]{1,0:T(8,128)(2,1)S(1)}, bf16[16,256]{1,0:T(8,128)(2,1)}, u32[]{:S(2)}) copy-start(bf16[16,256]{1,0:T(8,128)(2,1)} %refs_0_.1) | copy-start | bytes 24580
  35.0 17.1 %copy-start.4 = (bf16[16,256]{1,0:T(8,128)(2,1)S(1)}, bf16[16,256]{1,0:T(8,128)(2,1)}, u32[]{:S(2)}) copy-start(bf16[16,256]{1,0:T(8,128)(2,1)} %param.20) | copy-start | bytes 24580
  35.0 17.2 %copy-start.3 = (bf16[16,256]{1,0:T(8,128)(2,1)S(1)}, bf16[16,256]{1,0:T(8,128)(2,1)}, u32[]{:S(2)}) copy-start(bf16[16,256]{1,0:T(8,128)(2,1)} %param.21) | copy-start | bytes 24580
  35.0 17.2 %copy-start.5 = (bf16[32,256]{1,0:T(8,128)(2,1)S(1)}, bf16[32,256]{1,0:T(8,128)(2,1)}, u32[]{:S(2)}) copy-start(bf16[32,256]{1,0:T(8,128)(2,1)} %param.23) | copy-start | bytes 49156
  35.0 17.2 %copy-start.8 = (f32[32]{0:T(128)S(1)}, f32[32]{0:T(128)}, u32[]{:S(2)}) copy-start(f32[32]{0:T(128)} %param.22) | copy-start | bytes 388
  52.2 0.6 copy-start.1

commit v18 on v14

--- a/solution.py
+++ b/solution.py
@@ -135,6 +135,16 @@
             return carry
 
         lax.fori_loop(min(plan[1], 9), plan[1], finish, 0)
+        if plan[4]:
+            def gather_sum(k, total, plan=plan):
+                j = lax.rem(plan[12] + k, plan[1])
+                desc(plan, j, j).wait_recv()
+                return total + plan[8][j].astype(jnp.float32)
+
+            plan[7][...] = lax.fori_loop(
+                1, plan[1], gather_sum, plan[8][plan[12]].astype(jnp.float32)
+            )
+            continue
 
         def arrive(j, plan=plan):
             desc(plan, j, j).wait_recv()
@@ -151,6 +161,8 @@
         reduce, y_ref, buf = plan[4], plan[7], plan[8]
         if specs[e][6] > 1:
             buf = dict(seconds)[e][8]
+        elif reduce:
+            continue
         if reduce:
             y_ref[...] = jnp.sum(buf[...].astype(jnp.float32), axis=0)
         else:

time: 146 us -> 146 us (level)
  no operation moved by 1% of the time
where the time goes in v18:
time: 146 us; the launch traced here: 145 us
  Pallas kernels  82.1 us (56%)
  other arithmetic  32 us (22%)
  local copies, waits for them, and re-layouts  25.1 us (17%)
  matrix products  4.19 us (3%)
  between operations  1.63 us (1%)
    pallas_call x3, Pallas kernels, exchange_many(): pl.pallas_call(functools.partial(exchange_kernel, tuple(specs)), out_shap...  82.1 us
    scatter-add x1, other arithmetic, per_device(): contrib = jnp.zeros((col_width, FRESH * part_rows), jnp.float32).at[:, co...  23.8 us
    gather x1, local copies, waits for them, and re-layouts, per_device(): gathered = sources[:, neighbours].astype(jnp.float32)  13.8 us
    reshape x1, local copies, waits for them, and re-layouts, per_device(): sources = jnp.where(fresh_flag[None, :, None] == 1, blocks.transpose(1, 0...  3.11 us

profile of v18, /device:TPU:1, one launch (start us, length us, event | category | flops | bytes accessed | tf_op | source)
XLA Modules:
  0.0 145.1 jit_solution(12798208659706889770)
XLA Ops:
  0.6 29.2 %shard_map.137 = bf16[64,16,256]{2,1,0:T(8,128)(2,1)} custom-call(bf16[16,256]{1,0:T(8,128)(2,1)} %refs_0_.1), custom_call_target="tpu_custom_call" | custom-call | tf_op jit(solution)/shard_map/pallas_call | solution.py:199
  29.8 0.7 compare_convert_fusion
  30.5 1.3 bitcast_select_fusion
  31.9 3.1 %copy.40 = bf16[16,64,256]{0,2,1:T(8,128)(2,1)} copy(bf16[16,64,256]{2,0,1:T(8,128)(2,1)S(1)} %bitcast_select_fusion) | data formatting | bytes 1048576 | tf_op jit(solution)/shard_map/reshape | solution.py:242
  35.4 0.2 select_reduce_fusion
  35.7 13.8 %gather_fusion = bf16[4096,16]{1,0:T(8,128)(2,1)S(1)} fusion(bf16[16,16384]{0,1:T(8,128)(2,1)} %bitcast.68, s32[4096]{0:T(1024)S(1)} %broadcast_clamp_fusion), kind=kCustom, calls=%fused_computation | custom fusion | bytes 278528 | tf_op jit(solution)/shard_map/gather | solution.py:248
  49.5 0.6 dynamic_slice.15
  50.1 0.6 convert_divide_fusion
  50.7 0.7 fusion
  51.6 0.6 scatter.6.refs_1_
  52.2 17.8 %shard_map.138 = (bf16[8,96,256]{2,1,0:T(8,128)(2,1)}, f32[8,8,128]{2,1,0:T(8,128)}) custom-call(bf16[96,256]{1,0:T(8,128)(2,1)} %copy-done.1, f32[8,128]{1,0:T(8,128)} %scatter.6.refs_1_), custom_call_target="tpu_custom_call" | custom-call | tf_op jit(solution)/shard_map/pallas_call | solution.py:199
  70.1 0.9 slice.69
  71.0 0.7 compare_convert_fusion.1
  71.6 0.8 slice_reduce_fusion
  72.5 1.1 convolution_bitcast_fusion
  73.6 1.2 fusion.13
  74.8 0.6 multiply_convert_fusion
  75.4 0.1 fusion.8
  75.7 0.6 bitcast_multiply_fusion
  76.3 23.8 %scatter_custom_fusion = f32[16,4096]{0,1:T(8,128)} fusion(s32[4096]{0:T(1024)S(1)} %bitcast.77, f32[16,4096]{0,1:T(8,128)S(1)} %bitcast_multiply_fusion, f32[]{:T(128)} %constant.103.clone.1), kind=kCustom, calls=%fused_computation.5 | custom fusion | flops 65536 | bytes 2359300 | tf_op jit(solution)/shard_map/scatter-add | solution.py:298
  100.1 1.7 %convert_element_type.72 = bf16[16,4096]{0,1:T(8,128)(2,1)S(1)} convert(f32[16,4096]{0,1:T(8,128)} %scatter_custom_fusion) | non-fusion elementwise | flops 65536 | bytes 393216 | tf_op jit(solution)/shard_map/convert_element_type | solution.py:300
  101.8 0.3 copy.38
  102.2 0.6 gather_fusion.1
  102.8 0.8 copy.43
  103.7 0.2 convolution_convert_fusion.1
  103.9 0.2 fusion.9
  104.0 0.7 fusion.19.refs_1_
  104.7 35.1 %shard_map.139 = (f32[16,256]{1,0:T(8,128)}, f32[40,256]{1,0:T(8,128)}) custom-call(bf16[16,16384]{1,0:T(8,128)(2,1)} %bitcast.70, bf16[40,256]{1,0:T(8,128)(2,1)} %fusion.19.refs_1_), custom_call_target="tpu_custom_call" | custom-call | tf_op jit(solution)/shard_map/pallas_call | solution.py:199
  139.8 0.6 dynamic_slice.18
  141.0 1.5 %fusion.6 = bf16[16,256]{1,0:T(8,128)(2,1)} fusion(bf16[16,256]{1,0:T(8,128)(2,1)S(1)} %copy-done.4, bf16[256,256]{1,0:T(8,128)(2,1)S(1)} %get-tuple-element.39, f32[16,256]{1,0:T(8,128)} %get-tuple-element.35, f32[]{:T(128)} %bitcast.10), kind=kOutput, calls=%fused_computation.14 | convolution fusion | flops 2109440 | bytes 163844 | tf_op jit(solution)/shard_map/dot_general | solution.py:288
  142.5 1.3 fusion.29
  143.9 1.2 slice_bitcast_fusion
  (42 shorter events, 0.9 us)
Async XLA Ops:
  31.8 3.5 %copy-start.8 = (s32[64]{0:T(128)S(1)}, s32[64]{0:T(128)}, u32[]{:S(2)}) copy-start(s32[64]{0:T(128)} %param.16) | copy-start | bytes 772
  31.8 3.5 %copy-start.2 = (s32[16,256]{1,0:T(8,128)S(1)}, s32[16,256]{1,0:T(8,128)}, u32[]{:S(2)}) copy-start(s32[16,256]{1,0:T(8,128)} %param.18) | copy-start | bytes 49156
  31.9 17.6 %copy-start.9 = (s32[64]{0:T(128)S(1)}, s32[64]{0:T(128)}, u32[]{:S(2)}) copy-start(s32[64]{0:T(128)} %param.17) | copy-start | bytes 772
  31.9 18.2 %copy-start.6 = (s32[256]{0:T(256)S(1)}, s32[256]{0:T(256)}, u32[]{:S(2)}) copy-start(s32[256]{0:T(256)} %param.19) | copy-start | bytes 3076
  35.0 16.5 %copy-start = (bf16[16,256]{1,0:T(8,128)(2,1)S(1)}, bf16[16,256]{1,0:T(8,128)(2,1)}, u32[]{:S(2)}) copy-start(bf16[16,256]{1,0:T(8,128)(2,1)} %refs_0_.1) | copy-start | bytes 24580
  35.0 16.5 %copy-start.4 = (bf16[16,256]{1,0:T(8,128)(2,1)S(1)}, bf16[16,256]{1,0:T(8,128)(2,1)}, u32[]{:S(2)}) copy-start(bf16[16,256]{1,0:T(8,128)(2,1)} %param.20) | copy-start | bytes 24580
  35.0 16.6 %copy-start.3 = (bf16[16,256]{1,0:T(8,128)(2,1)S(1)}, bf16[16,256]{1,0:T(8,128)(2,1)}, u32[]{:S(2)}) copy-start(bf16[16,256]{1,0:T(8,128)(2,1)} %param.21) | copy-start | bytes 24580
  35.0 16.6 %copy-start.5 = (bf16[32,256]{1,0:T(8,128)(2,1)S(1)}, bf16[32,256]{1,0:T(8,128)(2,1)}, u32[]{:S(2)}) copy-start(bf16[32,256]{1,0:T(8,128)(2,1)} %param.23) | copy-start | bytes 49156
  35.0 16.6 %copy-start.7 = (f32[32]{0:T(128)S(1)}, f32[32]{0:T(128)}, u32[]{:S(2)}) copy-start(f32[32]{0:T(128)} %param.22) | copy-start | bytes 388
  51.6 0.6 copy-start.1

commit v19 on v18

--- a/solution.py
+++ b/solution.py
@@ -233,7 +233,7 @@
     fresh_flag = (staleness >= LIMIT).astype(jnp.int32)
     my_fresh = fresh_flag[my_index]
     col_inputs = jnp.concatenate([features, w_self, w_nbr, cotangent], axis=0)
-    bias_block = jnp.zeros((8, 128), jnp.float32).at[0, : sage_bias.shape[0]].set(sage_bias)
+    bias_block = sage_bias.reshape(1, -1)
     blocks = exchange(features, 0, "dom", n_dom, bcast=True)
     sources = jnp.where(
         fresh_flag[None, :, None] == 1,
@@ -260,7 +260,7 @@
     w_self_full = col_blocks[:, col_width : 2 * col_width].reshape(n_col * col_width, hidden)
     w_nbr_full = col_blocks[:, 2 * col_width : 3 * col_width].reshape(n_col * col_width, hidden)
     cot_full = col_blocks[:, 3 * col_width :].reshape(hidden, part_rows)
-    bias_full = bias_blocks[:, 0, : sage_bias.shape[0]].reshape(hidden)
+    bias_full = bias_blocks.reshape(hidden)
     pre_full = (
         left_product(w_self_full, feat_full)
         + left_product(w_nbr_full, agg_full)

time: 146 us -> 146 us (level)
  no operation moved by 1% of the time
where the time goes in v19:
time: 146 us
  Pallas kernels  81.7 us (56%)
  other arithmetic  33.4 us (23%)
  local copies, waits for them, and re-layouts  24.8 us (17%)
  matrix products  4.19 us (3%)
  between operations  1.62 us (1%)
    pallas_call x3, Pallas kernels, exchange_many(): pl.pallas_call(functools.partial(exchange_kernel, tuple(specs)), out_shap...  81.7 us
    scatter-add x1, other arithmetic, per_device(): contrib = jnp.zeros((col_width, FRESH * part_rows), jnp.float32).at[:, co...  23.8 us
    gather x1, local copies, waits for them, and re-layouts, per_device(): gathered = sources[:, neighbours].astype(jnp.float32)  13.8 us
    reshape x1, local copies, waits for them, and re-layouts, per_device(): sources = jnp.where(fresh_flag[None, :, None] == 1, blocks.transpose(1, 0...  3.11 us

profile of v19, /device:TPU:1, one launch (start us, length us, event | category | flops | bytes accessed | tf_op | source)
XLA Modules:
  0.0 145.7 jit_solution(3022201826226002013)
XLA Ops:
  0.6 29.2 %shard_map.137 = bf16[64,16,256]{2,1,0:T(8,128)(2,1)} custom-call(bf16[16,256]{1,0:T(8,128)(2,1)} %refs_0_.1), custom_call_target="tpu_custom_call" | custom-call | tf_op jit(solution)/shard_map/pallas_call | solution.py:199
  29.8 0.7 compare_convert_fusion
  30.5 1.3 bitcast_select_fusion
  31.9 3.1 %copy.40 = bf16[16,64,256]{0,2,1:T(8,128)(2,1)} copy(bf16[16,64,256]{2,0,1:T(8,128)(2,1)S(1)} %bitcast_select_fusion) | data formatting | bytes 1048576 | tf_op jit(solution)/shard_map/reshape | solution.py:242
  35.4 0.2 select_reduce_fusion
  35.7 13.8 %gather_fusion = bf16[4096,16]{1,0:T(8,128)(2,1)S(1)} fusion(bf16[16,16384]{0,1:T(8,128)(2,1)} %bitcast.68, s32[4096]{0:T(1024)S(1)} %broadcast_clamp_fusion), kind=kCustom, calls=%fused_computation | custom fusion | bytes 278528 | tf_op jit(solution)/shard_map/gather | solution.py:248
  49.4 0.6 dynamic_slice.15
  50.0 0.6 convert_divide_fusion
  50.7 0.7 fusion
  51.6 0.6 copy-done.1
  52.2 17.4 %shard_map.138 = (bf16[8,96,256]{2,1,0:T(8,128)(2,1)}, f32[8,1,32]{2,1,0:T(1,128)}) custom-call(bf16[96,256]{1,0:T(8,128)(2,1)} %copy-done.1, f32[1,32]{1,0:T(1,128)} %bitcast.79), custom_call_target="tpu_custom_call" | custom-call | tf_op jit(solution)/shard_map/pallas_call | solution.py:199
  69.6 0.9 slice.49
  70.5 0.7 compare_convert_fusion.1
  71.2 0.5 broadcast.172
  71.7 1.3 reduce.13
  73.1 1.1 convolution_bitcast_fusion
  74.2 1.2 fusion.13
  75.4 0.6 multiply_convert_fusion
  76.3 0.6 bitcast_multiply_fusion
  76.9 23.8 %scatter_custom_fusion = f32[16,4096]{0,1:T(8,128)} fusion(s32[4096]{0:T(1024)S(1)} %bitcast.77, f32[16,4096]{0,1:T(8,128)S(1)} %bitcast_multiply_fusion, f32[]{:T(128)} %constant.81.clone.1), kind=kCustom, calls=%fused_computation.5 | custom fusion | flops 65536 | bytes 2359300 | tf_op jit(solution)/shard_map/scatter-add | solution.py:298
  100.8 1.7 %convert_element_type.72 = bf16[16,4096]{0,1:T(8,128)(2,1)S(1)} convert(f32[16,4096]{0,1:T(8,128)} %scatter_custom_fusion) | non-fusion elementwise | flops 65536 | bytes 393216 | tf_op jit(solution)/shard_map/convert_element_type | solution.py:300
  102.5 0.3 copy.38
  102.8 0.6 gather_fusion.1
  103.4 0.8 copy.43
  104.3 0.2 convolution_convert_fusion.1
  104.5 0.2 fusion.9
  104.7 0.7 fusion.19.refs_1_
  105.3 35.1 %shard_map.139 = (f32[16,256]{1,0:T(8,128)}, f32[40,256]{1,0:T(8,128)}) custom-call(bf16[16,16384]{1,0:T(8,128)(2,1)} %bitcast.70, bf16[40,256]{1,0:T(8,128)(2,1)} %fusion.19.refs_1_), custom_call_target="tpu_custom_call" | custom-call | tf_op jit(solution)/shard_map/pallas_call | solution.py:199
  140.5 0.6 dynamic_slice.18
  141.7 1.5 %fusion.6 = bf16[16,256]{1,0:T(8,128)(2,1)} fusion(bf16[16,256]{1,0:T(8,128)(2,1)S(1)} %copy-done.4, bf16[256,256]{1,0:T(8,128)(2,1)S(1)} %get-tuple-element.27, f32[16,256]{1,0:T(8,128)} %get-tuple-element.23, f32[]{:T(128)} %bitcast.10), kind=kOutput, calls=%fused_computation.14 | convolution fusion | flops 2109440 | bytes 163844 | tf_op jit(solution)/shard_map/dot_general | solution.py:288
  143.2 1.3 fusion.29
  144.5 1.2 slice_bitcast_fusion
  (40 shorter events, 1.0 us)
Async XLA Ops:
  31.8 3.5 %copy-start.7 = (s32[64]{0:T(128)S(1)}, s32[64]{0:T(128)}, u32[]{:S(2)}) copy-start(s32[64]{0:T(128)} %param.14) | copy-start | bytes 772
  31.8 3.5 %copy-start.2 = (s32[16,256]{1,0:T(8,128)S(1)}, s32[16,256]{1,0:T(8,128)}, u32[]{:S(2)}) copy-start(s32[16,256]{1,0:T(8,128)} %param.16) | copy-start | bytes 49156
  31.9 17.6 %copy-start.8 = (s32[64]{0:T(128)S(1)}, s32[64]{0:T(128)}, u32[]{:S(2)}) copy-start(s32[64]{0:T(128)} %param.15) | copy-start | bytes 772
  31.9 18.2 %copy-start.6 = (s32[256]{0:T(256)S(1)}, s32[256]{0:T(256)}, u32[]{:S(2)}) copy-start(s32[256]{0:T(256)} %param.17) | copy-start | bytes 3076
  35.0 16.5 %copy-start = (bf16[16,256]{1,0:T(8,128)(2,1)S(1)}, bf16[16,256]{1,0:T(8,128)(2,1)}, u32[]{:S(2)}) copy-start(bf16[16,256]{1,0:T(8,128)(2,1)} %refs_0_.1) | copy-start | bytes 24580
  35.0 16.5 %copy-start.4 = (bf16[16,256]{1,0:T(8,128)(2,1)S(1)}, bf16[16,256]{1,0:T(8,128)(2,1)}, u32[]{:S(2)}) copy-start(bf16[16,256]{1,0:T(8,128)(2,1)} %param.18) | copy-start | bytes 24580
  35.0 16.5 %copy-start.3 = (bf16[16,256]{1,0:T(8,128)(2,1)S(1)}, bf16[16,256]{1,0:T(8,128)(2,1)}, u32[]{:S(2)}) copy-start(bf16[16,256]{1,0:T(8,128)(2,1)} %param.19) | copy-start | bytes 24580
  35.0 16.6 %copy-start.5 = (bf16[32,256]{1,0:T(8,128)(2,1)S(1)}, bf16[32,256]{1,0:T(8,128)(2,1)}, u32[]{:S(2)}) copy-start(bf16[32,256]{1,0:T(8,128)(2,1)} %param.21) | copy-start | bytes 49156
  51.6 0.6 copy-start.1

commit v20 on v18

--- a/solution.py
+++ b/solution.py
@@ -111,12 +111,14 @@
     for e, second in seconds:
         plan = plans[e]
 
-        def finish_first(j, plan=plan):
+        def first_sum(k, total, plan=plan):
+            j = lax.rem(plan[12] + k, plan[1])
             desc(plan, j, plan[12]).wait_send()
             desc(plan, j, j).wait_recv()
-
-        each_peer(plan, finish_first)
-        second[6][...] = jnp.sum(plan[8][...].astype(jnp.float32), axis=0).astype(second[6].dtype)
+            return total + plan[8][j].astype(jnp.float32)
+
+        total = lax.fori_loop(1, plan[1], first_sum, plan[8][plan[12]].astype(jnp.float32))
+        second[6][...] = total.astype(second[6].dtype)
     for e, plan in enumerate(plans):
         if specs[e][6] > 1:
             continue

time: 146 us -> 146 us (level)
  no operation moved by 1% of the time
where the time goes in v20:
time: 146 us; the launch traced here: 145 us
  Pallas kernels  82.2 us (56%)
  other arithmetic  32 us (22%)
  local copies, waits for them, and re-layouts  25.1 us (17%)
  matrix products  4.19 us (3%)
  between operations  1.63 us (1%)
    pallas_call x3, Pallas kernels, exchange_many(): pl.pallas_call(functools.partial(exchange_kernel, tuple(specs)), out_shap...  82.2 us
    scatter-add x1, other arithmetic, per_device(): contrib = jnp.zeros((col_width, FRESH * part_rows), jnp.float32).at[:, co...  23.8 us
    gather x1, local copies, waits for them, and re-layouts, per_device(): gathered = sources[:, neighbours].astype(jnp.float32)  13.8 us
    reshape x1, local copies, waits for them, and re-layouts, per_device(): sources = jnp.where(fresh_flag[None, :, None] == 1, blocks.transpose(1, 0...  3.11 us

profile of v20, /device:TPU:1, one launch (start us, length us, event | category | flops | bytes accessed | tf_op | source)
XLA Modules:
  0.0 145.1 jit_solution(15318691331811474558)
XLA Ops:
  0.6 29.2 %shard_map.137 = bf16[64,16,256]{2,1,0:T(8,128)(2,1)} custom-call(bf16[16,256]{1,0:T(8,128)(2,1)} %refs_0_.1), custom_call_target="tpu_custom_call" | custom-call | tf_op jit(solution)/shard_map/pallas_call | solution.py:201
  29.8 0.7 compare_convert_fusion
  30.5 1.3 bitcast_select_fusion
  31.9 3.1 %copy.40 = bf16[16,64,256]{0,2,1:T(8,128)(2,1)} copy(bf16[16,64,256]{2,0,1:T(8,128)(2,1)S(1)} %bitcast_select_fusion) | data formatting | bytes 1048576 | tf_op jit(solution)/shard_map/reshape | solution.py:244
  35.4 0.2 select_reduce_fusion
  35.7 13.8 %gather_fusion = bf16[4096,16]{1,0:T(8,128)(2,1)S(1)} fusion(bf16[16,16384]{0,1:T(8,128)(2,1)} %bitcast.68, s32[4096]{0:T(1024)S(1)} %broadcast_clamp_fusion), kind=kCustom, calls=%fused_computation | custom fusion | bytes 278528 | tf_op jit(solution)/shard_map/gather | solution.py:250
  49.5 0.6 dynamic_slice.15
  50.0 0.6 convert_divide_fusion
  50.7 0.7 fusion
  51.6 0.6 scatter.6.refs_1_
  52.2 17.8 %shard_map.138 = (bf16[8,96,256]{2,1,0:T(8,128)(2,1)}, f32[8,8,128]{2,1,0:T(8,128)}) custom-call(bf16[96,256]{1,0:T(8,128)(2,1)} %copy-done.1, f32[8,128]{1,0:T(8,128)} %scatter.6.refs_1_), custom_call_target="tpu_custom_call" | custom-call | tf_op jit(solution)/shard_map/pallas_call | solution.py:201
  70.1 0.9 slice.69
  71.0 0.7 compare_convert_fusion.1
  71.6 0.8 slice_reduce_fusion
  72.5 1.1 convolution_bitcast_fusion
  73.6 1.2 fusion.13
  74.8 0.6 multiply_convert_fusion
  75.4 0.1 fusion.8
  75.7 0.6 bitcast_multiply_fusion
  76.3 23.8 %scatter_custom_fusion = f32[16,4096]{0,1:T(8,128)} fusion(s32[4096]{0:T(1024)S(1)} %bitcast.77, f32[16,4096]{0,1:T(8,128)S(1)} %bitcast_multiply_fusion, f32[]{:T(128)} %constant.103.clone.1), kind=kCustom, calls=%fused_computation.5 | custom fusion | flops 65536 | bytes 2359300 | tf_op jit(solution)/shard_map/scatter-add | solution.py:300
  100.1 1.7 %convert_element_type.72 = bf16[16,4096]{0,1:T(8,128)(2,1)S(1)} convert(f32[16,4096]{0,1:T(8,128)} %scatter_custom_fusion) | non-fusion elementwise | flops 65536 | bytes 393216 | tf_op jit(solution)/shard_map/convert_element_type | solution.py:302
  101.8 0.3 copy.38
  102.2 0.6 gather_fusion.1
  102.8 0.8 copy.43
  103.7 0.2 convolution_convert_fusion.1
  103.8 0.2 fusion.9
  104.0 0.7 fusion.19.refs_1_
  104.7 35.1 %shard_map.139 = (f32[16,256]{1,0:T(8,128)}, f32[40,256]{1,0:T(8,128)}) custom-call(bf16[16,16384]{1,0:T(8,128)(2,1)} %bitcast.70, bf16[40,256]{1,0:T(8,128)(2,1)} %fusion.19.refs_1_), custom_call_target="tpu_custom_call" | custom-call | tf_op jit(solution)/shard_map/pallas_call | solution.py:201
  139.8 0.6 dynamic_slice.18
  141.1 1.5 %fusion.6 = bf16[16,256]{1,0:T(8,128)(2,1)} fusion(bf16[16,256]{1,0:T(8,128)(2,1)S(1)} %copy-done.4, bf16[256,256]{1,0:T(8,128)(2,1)S(1)} %get-tuple-element.39, f32[16,256]{1,0:T(8,128)} %get-tuple-element.35, f32[]{:T(128)} %bitcast.10), kind=kOutput, calls=%fused_computation.14 | convolution fusion | flops 2109440 | bytes 163844 | tf_op jit(solution)/shard_map/dot_general | solution.py:290
  142.6 1.3 fusion.29
  143.9 1.2 slice_bitcast_fusion
  (42 shorter events, 0.9 us)
Async XLA Ops:
  31.8 3.5 %copy-start.8 = (s32[64]{0:T(128)S(1)}, s32[64]{0:T(128)}, u32[]{:S(2)}) copy-start(s32[64]{0:T(128)} %param.16) | copy-start | bytes 772
  31.8 3.5 %copy-start.2 = (s32[16,256]{1,0:T(8,128)S(1)}, s32[16,256]{1,0:T(8,128)}, u32[]{:S(2)}) copy-start(s32[16,256]{1,0:T(8,128)} %param.18) | copy-start | bytes 49156
  31.9 17.6 %copy-start.9 = (s32[64]{0:T(128)S(1)}, s32[64]{0:T(128)}, u32[]{:S(2)}) copy-start(s32[64]{0:T(128)} %param.17) | copy-start | bytes 772
  31.9 18.2 %copy-start.6 = (s32[256]{0:T(256)S(1)}, s32[256]{0:T(256)}, u32[]{:S(2)}) copy-start(s32[256]{0:T(256)} %param.19) | copy-start | bytes 3076
  35.0 16.5 %copy-start = (bf16[16,256]{1,0:T(8,128)(2,1)S(1)}, bf16[16,256]{1,0:T(8,128)(2,1)}, u32[]{:S(2)}) copy-start(bf16[16,256]{1,0:T(8,128)(2,1)} %refs_0_.1) | copy-start | bytes 24580
  35.0 16.5 %copy-start.4 = (bf16[16,256]{1,0:T(8,128)(2,1)S(1)}, bf16[16,256]{1,0:T(8,128)(2,1)}, u32[]{:S(2)}) copy-start(bf16[16,256]{1,0:T(8,128)(2,1)} %param.20) | copy-start | bytes 24580
  35.0 16.6 %copy-start.3 = (bf16[16,256]{1,0:T(8,128)(2,1)S(1)}, bf16[16,256]{1,0:T(8,128)(2,1)}, u32[]{:S(2)}) copy-start(bf16[16,256]{1,0:T(8,128)(2,1)} %param.21) | copy-start | bytes 24580
  35.0 16.6 %copy-start.5 = (bf16[32,256]{1,0:T(8,128)(2,1)S(1)}, bf16[32,256]{1,0:T(8,128)(2,1)}, u32[]{:S(2)}) copy-start(bf16[32,256]{1,0:T(8,128)(2,1)} %param.23) | copy-start | bytes 49156
  35.0 16.6 %copy-start.7 = (f32[32]{0:T(128)S(1)}, f32[32]{0:T(128)}, u32[]{:S(2)}) copy-start(f32[32]{0:T(128)} %param.22) | copy-start | bytes 388
  51.6 0.6 copy-start.1
